TPU v7x, 256 devices: a whole 4x4x8 slice. The times are simulated.
256 devices in a mesh: dom: 64 (over y, z, core), rep: 4 (over x).
Axes of the slice: x: 4, y: 4, z: 8, core: 2. Of those that a mesh axis runs over, the one named last changes fastest.
Arguments:
- embedding: float32 [32768, 400], P('dom'), may hold values from -1.5 to 1.5
- adagrad_sum: float32 [32768], P('dom'), may hold values from 0.01 to 1
- row_lists: int32 [4, 64, 64, 16], P('rep', 'dom'), may hold values from 0 to 511, as said below
- source_slots: int32 [4, 64, 2, 512], P('rep', 'dom'), may hold values from 0 to 1023, as said below
- target_slots: int32 [4, 64, 2, 512], P('rep', 'dom'), may hold values from 0 to 1023, as said below
- negative_ids: int32 [4, 64, 2, 2, 512], P('rep', 'dom'), may hold values from 0 to 511
Outputs:
- new_embedding: float32 [32768, 400], P('dom')
- new_adagrad_sum: float32 [32768], P('dom')
Inputs may be any that keep to these rules, and one draw needn't show every extreme that they name: `row_lists`: for each worker and owner, a count of leading entries are distinct rows of that owner and the other entries are 0. For the worker with index w along dom, the owners (w + c) mod 64, c < 4, have all 16 entries live; every other owner has 1 to 8 live entries. `source_slots`: every slot named is among the leading live entries of the worker's row list for its owner; entries k >= 8 are named only for the owners (w + c) mod 64, c < 4, of the worker with index w along dom. `target_slots`: every slot named is among the leading live entries of the worker's row list for its owner; entries k >= 8 are named only for the owners (w + c) mod 64, c < 4, of the worker with index w along dom.
All inputs are finite; a program needn't handle non-finite values.
Results may differ from a plain program's by a relative error of at most 0.0003.
Values sent between devices are 32-bit elements; how exact they have to be, the bound alone decides.
No kernel may reach another device: no remote copies, remote signals or barrier semaphores. Data moves between devices by JAX's collectives and lax.ppermute only.
A program may use at most 64 MiB of HBM per device.

v0:
```python
import jax
import jax.numpy as jnp
from jax import lax
from jax.experimental import pallas as pl
from jax.experimental.pallas import tpu as pltpu
from jax.sharding import PartitionSpec as P

HEAVY = 4
LEARN_RATE = 0.1
LANES = 128
WIDTHS = (104, 104, 96, 96)
STARTS = (0, 104, 208, 304)
f32 = jnp.float32
bf16 = jnp.bfloat16


def passed_along(value, axis, steps):
    count = lax.axis_size(axis)
    pairs = [(source, (source + steps) % count) for source in range(count)]
    return lax.ppermute(value, axis, pairs)


def exchanged(value, axis):
    return lax.all_to_all(value, axis, 0, 0, tiled=True)


def halves(x):
    high = x.astype(bf16)
    low = (x - high.astype(f32)).astype(bf16)
    return high, low


def mm(a, b):
    return jnp.dot(a, b, preferred_element_type=f32)


def mm_nt(a, b):
    return lax.dot_general(a, b, (((1,), (1,)), ((), ())), preferred_element_type=f32)


def serve_body(head_ids, tail_ids, rows, heads, tails):
    def eight(w, carry):
        for k in range(8):
            heads[pl.ds(w * 8 + k, 1), :] = rows[pl.ds(head_ids[w * 8 + k], 1), :]
        return carry

    lax.fori_loop(0, heads.shape[0] // 8, eight, 0, unroll=2)
    for k in range(tails.shape[0]):
        tails[pl.ds(k, 1), :] = rows[pl.ds(tail_ids[k], 1), :]


def serve(head_ids, tail_ids, rows):
    width = rows.shape[1]
    return pl.pallas_call(
        serve_body,
        grid_spec=pltpu.PrefetchScalarGridSpec(
            num_scalar_prefetch=2,
            grid=(1,),
            in_specs=[pl.BlockSpec(rows.shape, lambda i, a, b: (0, 0))],
            out_specs=[
                pl.BlockSpec((head_ids.shape[0], width), lambda i, a, b: (0, 0)),
                pl.BlockSpec((tail_ids.shape[0], width), lambda i, a, b: (0, 0)),
            ],
        ),
        out_shape=[
            jax.ShapeDtypeStruct((head_ids.shape[0], width), f32),
            jax.ShapeDtypeStruct((tail_ids.shape[0], width), f32),
        ],
        name="serve",
    )(head_ids, tail_ids, rows)


def prep_body(slots, negs, by_edge, by_slot, count_row, count_col):
    edges = count_row.shape[2]
    parts = slots.shape[1] // edges
    live = by_slot.shape[0]
    padded = by_edge.shape[1]
    one, zero = jnp.ones((), f32), jnp.zeros((), f32)
    for p in range(parts):
        row = slots[:, p * edges : (p + 1) * edges]
        down = lax.broadcasted_iota(jnp.int32, (live, edges), 0)
        by_slot[:, p * edges : (p + 1) * edges] = jnp.where(down == row, one, zero).astype(bf16)
        column = jnp.broadcast_to(row, (LANES, edges)).T
        across = lax.broadcasted_iota(jnp.int32, (edges, LANES), 1)
        for c in range(padded // LANES):
            by_edge[p * edges : (p + 1) * edges, c * LANES : (c + 1) * LANES] = jnp.where(
                across + c * LANES == column, one, zero
            ).astype(bf16)
        neg = negs[:, p * edges : (p + 1) * edges]
        down = lax.broadcasted_iota(jnp.int32, (edges, edges), 0)
        drawn = jnp.where(down == neg, one, zero).astype(bf16)
        if p % 2 == 0:
            count_row[p // 2] = mm_nt(jnp.ones((8, edges), bf16), drawn)
        else:
            count_col[p // 2] = mm(drawn, jnp.ones((edges, LANES), bf16))


def prep(slots, negs, edges, live, padded):
    total = slots.shape[1]
    batches = total // edges // 2
    return pl.pallas_call(
        prep_body,
        out_shape=[
            jax.ShapeDtypeStruct((total, padded), bf16),
            jax.ShapeDtypeStruct((live, total), bf16),
            jax.ShapeDtypeStruct((batches, 8, edges), f32),
            jax.ShapeDtypeStruct((batches, edges, LANES), f32),
        ],
        name="prep",
    )(slots, negs)


def grads_body(heads, tails, by_edge, by_slot, count_row, count_col, out_heads, out_tails, high, low, d_high, d_low):
    head_count = heads.shape[0]
    live = head_count + tails.shape[0]
    padded = by_edge.shape[1]
    width = heads.shape[1]
    batches, _, edges = count_row.shape
    high[:head_count, :], low[:head_count, :] = halves(heads[...])
    high[head_count:live, :], low[head_count:live, :] = halves(tails[...])
    high[live:, :] = jnp.zeros((padded - live, width), bf16)
    low[live:, :] = jnp.zeros((padded - live, width), bf16)
    for b in range(batches):
        picks = []
        for side in range(2):
            at = (2 * b + side) * edges
            chosen = by_edge[at : at + edges, :]
            picks.append((mm(chosen, high[...]).astype(bf16), mm(chosen, low[...]).astype(bf16)))
        (s_high, s_low), (t_high, t_low) = picks
        scores = mm_nt(s_high, t_high) + mm_nt(s_high, t_low) + mm_nt(s_low, t_high)
        decay = jnp.exp(-jnp.abs(scores))
        upper = 1.0 / (1.0 + decay)
        lower = decay * upper
        sure = scores >= 0
        weight = jnp.where(sure, upper, lower)
        missing = jnp.where(sure, lower, upper)
        counts = count_row[b, 0:1, :] + jnp.concatenate([count_col[b]] * (edges // LANES), axis=1)
        down = lax.broadcasted_iota(jnp.int32, (edges, edges), 0)
        across = lax.broadcasted_iota(jnp.int32, (edges, edges), 1)
        gain = weight * counts * (1.0 / edges) - jnp.where(down == across, missing, 0.0)
        g_high, g_low = halves(gain)
        d_s = mm(g_high, t_high) + mm(g_high, t_low) + mm(g_low, t_high)
        at = 2 * b * edges
        d_high[at : at + edges, :], d_low[at : at + edges, :] = halves(d_s)
        g_high, g_low = halves(gain.T)
        d_t = mm(g_high, s_high) + mm(g_high, s_low) + mm(g_low, s_high)
        at += edges
        d_high[at : at + edges, :], d_low[at : at + edges, :] = halves(d_t)
    summed = mm(by_slot[...], d_high[...]) + mm(by_slot[...], d_low[...])
    for q in range(width // LANES):
        out_heads[q] = summed[:head_count, q * LANES : (q + 1) * LANES]
    out_tails[...] = summed[head_count:, :]


def grads(heads, tails, by_edge, by_slot, count_row, count_col):
    head_count, width = heads.shape
    padded = by_edge.shape[1]
    total = by_edge.shape[0]
    return pl.pallas_call(
        grads_body,
        out_shape=[
            jax.ShapeDtypeStruct((width // LANES, head_count, LANES), f32),
            jax.ShapeDtypeStruct(tails.shape, f32),
        ],
        scratch_shapes=[
            pltpu.VMEM((padded, width), bf16),
            pltpu.VMEM((padded, width), bf16),
            pltpu.VMEM((total, width), bf16),
            pltpu.VMEM((total, width), bf16),
        ],
        name="grads",
    )(heads, tails, by_edge, by_slot, count_row, count_col)


def owner_body(back, tails, head_ids, tail_ids, out):
    rows = out.shape[1]

    def part(values, ids):
        down = lax.broadcasted_iota(jnp.int32, (rows, ids.shape[1]), 0)
        hot = jnp.where(down == ids, 1.0, 0.0).astype(bf16)
        high, low = halves(values)
        return mm(hot, high) + mm(hot, low)

    summed = part(back[...], head_ids[...]) + part(tails[...], tail_ids[...])
    out[...] = summed.T[: out.shape[0], :]


def owner(back, tails, head_ids, tail_ids, rows):
    return pl.pallas_call(
        owner_body,
        out_shape=jax.ShapeDtypeStruct((max(WIDTHS), rows), f32),
        name="owner",
    )(back, tails, head_ids, tail_ids)


def update_body(quarters, rows, sums, new_rows, new_sums):
    squares = jnp.zeros(sums.shape, f32)
    for q in range(quarters.shape[0]):
        squares += jnp.sum(quarters[q] * quarters[q], axis=0, keepdims=True)
    fresh = sums[...] + squares * (1.0 / rows.shape[1])
    new_sums[...] = fresh
    scale = LEARN_RATE / jnp.sqrt(fresh)
    step = jnp.concatenate([quarters[q, :w, :] * scale for q, w in enumerate(WIDTHS)], axis=0)
    new_rows[...] = rows[...] - step.T


def update(quarters, rows, sums):
    return pl.pallas_call(
        update_body,
        out_shape=[
            jax.ShapeDtypeStruct(rows.shape, f32),
            jax.ShapeDtypeStruct(sums.shape, f32),
        ],
        name="update",
    )(quarters, rows, sums)


def compact(slots, here, owners, capacity):
    half = capacity // 2
    who, k = slots // capacity, slots % capacity
    return jnp.where(k < half, who * half + k, owners * half + (who - here) % owners * half + k - half)


def local(embedding, adagrad_sum, row_lists, source_slots, target_slots, negative_ids):
    requests = row_lists[0, 0]
    owners, capacity = requests.shape
    half = capacity // 2
    rows = embedding.shape[0]
    groups = lax.axis_size("rep")
    edges = source_slots.shape[3]
    here = lax.axis_index("dom")
    incoming = exchanged(requests, "dom")
    spread = jnp.concatenate(
        [jnp.pad(embedding[:, s : s + w], ((0, 0), (0, LANES - w))) for s, w in zip(STARTS, WIDTHS)],
        axis=1,
    )
    slots = jnp.stack([source_slots[0, 0], target_slots[0, 0]], axis=1).reshape(1, -1)
    slots = compact(slots, here, owners, capacity)
    live = owners * half + HEAVY * half
    padded = -(-live // LANES) * LANES
    plan = prep(slots, negative_ids[0, 0].reshape(1, -1), edges, live, padded)

    askers = (here - jnp.arange(HEAVY)) % owners
    tail_ids = incoming[askers, half:].reshape(-1)
    head_ids = incoming[:, :half].reshape(-1)
    heads, tails = serve(head_ids, tail_ids, spread)
    tails = tails.reshape(HEAVY, half, -1)
    tails = jnp.concatenate(
        [tails[0]] + [passed_along(tails[r], "dom", -r) for r in range(1, HEAVY)], axis=0
    )
    heads = exchanged(heads.reshape(owners, half, -1), "dom").reshape(owners * half, -1)
    all_ids = exchanged(
        jnp.broadcast_to(jnp.concatenate([head_ids, tail_ids])[None], (groups, live)), "rep"
    )

    head_grads, tail_grads = grads(heads, tails, *plan)
    tail_grads = tail_grads.reshape(HEAVY, half, -1)
    tail_grads = jnp.concatenate(
        [tail_grads[0]] + [passed_along(tail_grads[r], "dom", r) for r in range(1, HEAVY)], axis=0
    )
    tail_grads = jnp.moveaxis(tail_grads.reshape(HEAVY * half, groups, LANES), 1, 0)
    tail_back = exchanged(tail_grads, "rep").reshape(-1, LANES)
    back = exchanged(head_grads.reshape(groups * owners, half, LANES), ("rep", "dom"))
    quarter = owner(
        back.reshape(-1, LANES),
        tail_back,
        all_ids[:, : owners * half].reshape(1, -1),
        all_ids[:, owners * half :].reshape(1, -1),
        rows,
    )
    quarters = exchanged(jnp.broadcast_to(quarter[None], (groups, *quarter.shape)), "rep")
    new_rows, new_sums = update(quarters, embedding, adagrad_sum.reshape(1, -1))
    return new_rows, new_sums.reshape(-1)


def solution(mesh):
    in_specs = (
        P("dom", None),
        P("dom"),
        P("rep", "dom", None, None),
        P("rep", "dom", None, None),
        P("rep", "dom", None, None),
        P("rep", "dom", None, None, None),
    )
    out_specs = (P("dom", None), P("dom"))
    return jax.shard_map(local, mesh=mesh, in_specs=in_specs, out_specs=out_specs, check_vma=False)
```

profile of v0, /device:TPU:1, one launch (start us, length us, event | category | flops | bytes accessed | tf_op | source)
XLA Modules:
  0.0 177.0 jit_solution(2631445864880444095)
XLA Ops:
  0.6 1.4 copy.25
  2.0 13.1 %all-to-all-start = ((s32[64,1,16]{2,1,0:T(1,128)}), s32[64,1,16]{2,1,0:T(1,128)S(1)}, u32[]{:S(2)}, u32[]{:S(2)}) async-start(s32[64,1,16]{2,1,0:T(1,128)} %bitcast), calls=%async_computation | async-start | bytes 65536 | tf_op jit(solution)/shard_map/all_to_all | solution.py:24
  15.2 1.5 copy.28.rows
  17.1 1.1 select_maximum_fusion.rows
  18.2 6.2 %all-to-all-done = s32[64,1,16]{2,1,0:T(1,128)S(1)} async-done(((s32[64,1,16]{2,1,0:T(1,128)}), s32[64,1,16]{2,1,0:T(1,128)S(1)}, u32[]{:S(2)}, u32[]{:S(2)}) %all-to-all-start) | async-done | bytes 4128 | tf_op jit(solution)/shard_map/all_to_all | solution.py:24
  24.4 7.9 %while.1 = (s32[]{:T(128)}, s32[64,16]{1,0:T(8,128)S(1)}, s32[4,2]{0,1:T(2,128)S(1)}, s32[4,8]{1,0:T(4,128)S(1)}, s32[]{:T(128)}, /*index=5*/s32[]{:T(128)}) while((s32[]{:T(128)}, s32[64,16]{1,0:T(8,128)S(1)}, s32[4,2]{0,1:T(2,128)S(1)}, s32[4,8]{1,0:T(4,128)S(1)}, s32[]{:T(128)}, /*index=5*/s32[]{:T(128)}) %tuple.37), condition=%wide.while_cond, body=%wide.while_body.sunk | while | flops 2 | bytes 241 | solution.py:244
  24.5 0.5 fusion.11
  25.1 1.3 dynamic-slice.7
  26.5 0.5 fusion.11
  27.0 1.3 dynamic-slice.7
  28.5 0.5 fusion.11
  29.0 1.3 dynamic-slice.7
  30.4 0.5 fusion.11
  31.0 1.3 dynamic-slice.7
  32.3 0.6 reshape.332.tail_ids
  33.0 0.7 reshape.331.head_ids
  33.6 4.7 %serve.1 = (f32[512,512]{1,0:T(8,128)}, f32[32,512]{1,0:T(8,128)}) custom-call(s32[512]{0:T(512)} %reshape.331.head_ids, s32[32]{0:T(128)} %reshape.332.tail_ids, f32[512,512]{1,0:T(8,128)} %select_maximum_fusion.rows), custom_call_target="tpu_custom_call" | custom-call | tf_op jit(solution)/shard_map/serve/pallas_call | solution.py:54
  38.3 4.8 %all-to-all-start.1 = ((f32[64,8,512]{2,1,0:T(8,128)}), f32[64,8,512]{2,1,0:T(8,128)S(1)}, u32[]{:S(2)}, u32[]{:S(2)}) async-start(f32[64,8,512]{2,1,0:T(8,128)} %bitcast.35), calls=%async_computation.1 | async-start | bytes 2097152 | tf_op jit(solution)/shard_map/all_to_all | solution.py:24
  43.1 0.8 fusion.9
  43.9 0.6 collective-permute-start
  44.5 4.9 %collective-permute-start.1 = (f32[8,512]{1,0:T(8,128)S(1)}, f32[8,512]{1,0:T(8,128)S(1)}, u32[]{:S(2)}, u32[]{:S(2)}) collective-permute-start(f32[8,512]{1,0:T(8,128)S(1)} %get-tuple-element.58), channel_id=1, source_target_pairs={{0,248},{4,252},{8,0},{12,4},{16,8},{20,12},{24,16},{28,20},{32,24... | collective-permute-start | bytes 49160 | tf_op jit(solution)/shard_map/ppermute | solution.py:20
  49.5 2.5 %collective-permute-start.2 = (f32[8,512]{1,0:T(8,128)S(1)}, f32[8,512]{1,0:T(8,128)S(1)}, u32[]{:S(2)}, u32[]{:S(2)}) collective-permute-start(f32[8,512]{1,0:T(8,128)S(1)} %get-tuple-element.57), channel_id=1, source_target_pairs={{0,244},{4,248},{8,252},{12,0},{16,4},{20,8},{24,12},{28,16},{32,2... | collective-permute-start | bytes 49160 | tf_op jit(solution)/shard_map/ppermute | solution.py:20
  52.0 0.7 compare_select_fusion.2.slots
  52.7 0.6 reshape_squeeze.3.negs
  53.3 4.1 %prep.1 = (bf16[2048,640]{1,0:T(8,128)(2,1)}, bf16[544,2048]{1,0:T(8,128)(2,1)}, f32[2,8,512]{2,1,0:T(8,128)}, f32[2,512,128]{2,1,0:T(8,128)}) custom-call(s32[1,2048]{1,0:T(1,128)} %compare_select_fusion.2.slots, s32[1,2048]{1,0:T(1,128)} %reshape_squeeze.3.negs), custom_call_target="tpu_custom_call" | custom-call | tf_op jit(solution)/shard_map/prep/pallas_call | solution.py:101
  57.4 11.1 %collective-permute-done = f32[8,512]{1,0:T(8,128)S(1)} collective-permute-done((f32[8,512]{1,0:T(8,128)S(1)}, f32[8,512]{1,0:T(8,128)S(1)}, u32[]{:S(2)}, u32[]{:S(2)}) %collective-permute-start) | collective-permute-done | bytes 16416 | tf_op jit(solution)/shard_map/ppermute | solution.py:20
  68.5 0.4 collective-permute-done.2
  68.9 0.6 pad_maximum_fusion.tails
  69.6 2.1 %all-to-all-done.1 = f32[64,8,512]{2,1,0:T(8,128)S(1)} async-done(((f32[64,8,512]{2,1,0:T(8,128)}), f32[64,8,512]{2,1,0:T(8,128)S(1)}, u32[]{:S(2)}, u32[]{:S(2)}) %all-to-all-start.1) | async-done | bytes 1048608 | tf_op jit(solution)/shard_map/all_to_all | solution.py:24
  71.6 1.0 copy-done.1
  72.6 15.2 %grads.1 = (f32[4,512,128]{2,1,0:T(8,128)}, f32[32,512]{1,0:T(8,128)}) custom-call(f32[512,512]{1,0:T(8,128)} %bitcast.32, f32[32,512]{1,0:T(8,128)} %pad_maximum_fusion.tails, bf16[2048,640]{1,0:T(8,128)(2,1)} %get-tuple-element.14.by_edge, bf16[544,2048]{1,0:T(8,128)(2,1)} %get-tuple-element.15.by_slot, f32[2,8,512]{2,1,0:T(8,128)} %get-tuple-element.16.count_row, ...), custom_call_target="tpu_custom_call" | custom-call | tf_op jit(solution)/shard_map/grads/pallas_call | solution.py:159
  87.8 0.8 slice_bitcast_fusion
  88.6 0.8 collective-permute-start.4
  89.4 2.0 %collective-permute-start.5 = (f32[8,512]{1,0:T(8,128)S(1)}, f32[8,512]{1,0:T(8,128)S(1)}, u32[]{:S(2)}, u32[]{:S(2)}) collective-permute-start(f32[8,512]{1,0:T(8,128)S(1)} %get-tuple-element.53), channel_id=1, source_target_pairs={{0,12},{4,16},{8,20},{12,24},{16,28},{20,32},{24,36},{28,40},{32,4... | collective-permute-start | bytes 49160 | tf_op jit(solution)/shard_map/ppermute | solution.py:20
  91.8 0.6 broadcast_in_dim.4
  92.4 4.0 %all-to-all-start.4 = ((s32[4,1,544]{2,1,0:T(1,128)}), s32[4,1,544]{2,1,0:T(1,128)S(1)}, u32[]{:S(2)}, u32[]{:S(2)}) async-start(s32[4,1,544]{2,1,0:T(1,128)} %broadcast_in_dim.4), calls=%async_computation.4 | async-start | bytes 20480 | tf_op jit(solution)/shard_map/all_to_all | solution.py:24
  96.4 4.1 %all-to-all-done.4 = s32[4,1,544]{2,1,0:T(1,128)S(1)} async-done(((s32[4,1,544]{2,1,0:T(1,128)}), s32[4,1,544]{2,1,0:T(1,128)S(1)}, u32[]{:S(2)}, u32[]{:S(2)}) %all-to-all-start.4) | async-done | bytes 8736 | tf_op jit(solution)/shard_map/all_to_all | solution.py:24
  100.6 7.5 %all_to_all.41 = f32[4,32,128]{2,1,0:T(8,128)} all-to-all(f32[4,32,128]{2,1,0:T(8,128)S(1)} %maximum_bitcast_fusion), channel_id=1, replica_groups=mesh['dom'=64,'rep'=4] {'rep'}, dimensions={0} | all-to-all | bytes 131072 | tf_op jit(solution)/shard_map/all_to_all | solution.py:24
  108.1 10.1 %all-to-all-start.2 = ((f32[256,8,128]{2,1,0:T(8,128)}), f32[256,8,128]{2,1,0:T(8,128)S(1)}, u32[]{:S(2)}, u32[]{:S(2)}) async-start(f32[256,8,128]{2,1,0:T(8,128)} %bitcast.34), calls=%async_computation.2 | async-start | bytes 2097152 | tf_op jit(solution)/shard_map/all_to_all | solution.py:24
  118.2 0.6 copy.40
  118.8 0.6 reshape.340.tail_ids
  119.4 31.2 %all-to-all-done.2 = f32[256,8,128]{2,1,0:T(8,128)S(1)} async-done(((f32[256,8,128]{2,1,0:T(8,128)}), f32[256,8,128]{2,1,0:T(8,128)S(1)}, u32[]{:S(2)}, u32[]{:S(2)}) %all-to-all-start.2) | async-done | bytes 1048608 | tf_op jit(solution)/shard_map/all_to_all | solution.py:24
  150.7 1.0 copy-done.2
  151.6 3.4 %owner.1 = f32[104,512]{1,0:T(8,128)} custom-call(f32[2048,128]{1,0:T(8,128)} %bitcast.33, f32[128,128]{1,0:T(8,128)} %bitcast.36, s32[1,2048]{1,0:T(1,128)} %bitcast.41, s32[1,128]{1,0:T(1,128)} %reshape.340.tail_ids), custom_call_target="tpu_custom_call" | custom-call | tf_op jit(solution)/shard_map/owner/pallas_call | solution.py:189
  155.0 1.0 broadcast_in_dim.5
  156.0 15.6 %all_to_all.42.quarters = f32[4,104,512]{2,1,0:T(8,128)} all-to-all(f32[4,104,512]{2,1,0:T(8,128)S(1)} %broadcast_in_dim.5), channel_id=1, replica_groups=mesh['dom'=64,'rep'=4] {'rep'}, dimensions={0} | all-to-all | bytes 1703936 | tf_op jit(solution)/shard_map/all_to_all | solution.py:24
  171.7 2.9 %update.1 = (f32[512,400]{1,0:T(8,128)}, f32[1,512]{1,0:T(1,128)}) custom-call(f32[4,104,512]{2,1,0:T(8,128)} %all_to_all.42.quarters, f32[512,400]{1,0:T(8,128)} %copy-done, f32[1,512]{1,0:T(1,128)} %bitcast.47), custom_call_target="tpu_custom_call" | custom-call | tf_op jit(solution)/shard_map/update/pallas_call | solution.py:208
  174.6 2.4 %copy.34 = f32[512,400]{0,1:T(8,128)} copy(f32[512,400]{1,0:T(8,128)} %get-tuple-element.38) | data formatting | bytes 1638400
  (43 shorter events, 1.2 us)
Async XLA Ops:
  0.6 16.4 %copy-start.8 = (pred[128]{0:T(512)(128)(4,1)S(1)}, pred[128]{0:T(512)(128)(4,1)}, u32[]{:S(2)}) copy-start(pred[128]{0:T(512)(128)(4,1)} %constant.58.clone.1) | copy-start | bytes 388
  2.0 22.4 %all-to-all-start = ((s32[64,1,16]{2,1,0:T(1,128)}), s32[64,1,16]{2,1,0:T(1,128)S(1)}, u32[]{:S(2)}, u32[]{:S(2)}) async-start(s32[64,1,16]{2,1,0:T(1,128)} %bitcast), calls=%async_computation | async-start | bytes 65536 | tf_op jit(solution)/shard_map/all_to_all | solution.py:24
  16.7 21.6 %copy-start = (f32[512,400]{1,0:T(8,128)}, f32[512,400]{1,0:T(8,128)S(1)}, u32[]{:S(2)}) copy-start(f32[512,400]{1,0:T(8,128)S(1)} %copy.28.rows) | copy-start | bytes 2457604
  17.1 26.0 %copy-start.6 = (s32[1,1,2,512]{3,2,1,0:T(2,128)S(1)}, s32[1,1,2,512]{3,2,1,0:T(2,128)}, u32[]{:S(2)}) copy-start(s32[1,1,2,512]{3,2,1,0:T(2,128)} %param.10) | copy-start | bytes 12292
  17.1 26.0 %copy-start.7 = (s32[1,1,2,512]{3,2,1,0:T(2,128)S(1)}, s32[1,1,2,512]{3,2,1,0:T(2,128)}, u32[]{:S(2)}) copy-start(s32[1,1,2,512]{3,2,1,0:T(2,128)} %param.9) | copy-start | bytes 12292
  17.1 35.5 %copy-start.4 = (s32[1,1,2,2,512]{4,3,2,1,0:T(2,128)S(1)}, s32[1,1,2,2,512]{4,3,2,1,0:T(2,128)}, u32[]{:S(2)}) copy-start(s32[1,1,2,2,512]{4,3,2,1,0:T(2,128)} %param.11) | copy-start | bytes 24580
  38.3 33.3 %all-to-all-start.1 = ((f32[64,8,512]{2,1,0:T(8,128)}), f32[64,8,512]{2,1,0:T(8,128)S(1)}, u32[]{:S(2)}, u32[]{:S(2)}) async-start(f32[64,8,512]{2,1,0:T(8,128)} %bitcast.35), calls=%async_computation.1 | async-start | bytes 2097152 | tf_op jit(solution)/shard_map/all_to_all | solution.py:24
  43.9 24.6 %collective-permute-start = (f32[8,512]{1,0:T(8,128)S(1)}, f32[8,512]{1,0:T(8,128)S(1)}, u32[]{:S(2)}, u32[]{:S(2)}) collective-permute-start(f32[8,512]{1,0:T(8,128)S(1)} %get-tuple-element.59), channel_id=1, source_target_pairs={{0,252},{4,0},{8,4},{12,8},{16,12},{20,16},{24,20},{28,24},{32,28}... | collective-permute-start | bytes 49160 | tf_op jit(solution)/shard_map/ppermute | solution.py:20
  44.5 24.0 %collective-permute-start.1 = (f32[8,512]{1,0:T(8,128)S(1)}, f32[8,512]{1,0:T(8,128)S(1)}, u32[]{:S(2)}, u32[]{:S(2)}) collective-permute-start(f32[8,512]{1,0:T(8,128)S(1)} %get-tuple-element.58), channel_id=1, source_target_pairs={{0,248},{4,252},{8,0},{12,4},{16,8},{20,12},{24,16},{28,20},{32,24... | collective-permute-start | bytes 49160 | tf_op jit(solution)/shard_map/ppermute | solution.py:20
  49.5 19.5 %collective-permute-start.2 = (f32[8,512]{1,0:T(8,128)S(1)}, f32[8,512]{1,0:T(8,128)S(1)}, u32[]{:S(2)}, u32[]{:S(2)}) collective-permute-start(f32[8,512]{1,0:T(8,128)S(1)} %get-tuple-element.57), channel_id=1, source_target_pairs={{0,244},{4,248},{8,252},{12,0},{16,4},{20,8},{24,12},{28,16},{32,2... | collective-permute-start | bytes 49160 | tf_op jit(solution)/shard_map/ppermute | solution.py:20
  71.6 1.0 copy-start.1
  72.6 19.1 %copy-start.3 = (s32[512]{0:T(512)S(1)}, s32[512]{0:T(512)}, u32[]{:S(2)}) copy-start(s32[512]{0:T(512)} %reshape.331.head_ids) | copy-start | bytes 6148
  72.6 19.1 %copy-start.5 = (s32[32]{0:T(128)S(1)}, s32[32]{0:T(128)}, u32[]{:S(2)}) copy-start(s32[32]{0:T(128)} %reshape.332.tail_ids) | copy-start | bytes 388
  88.6 7.8 %collective-permute-start.4 = (f32[8,512]{1,0:T(8,128)S(1)}, f32[8,512]{1,0:T(8,128)S(1)}, u32[]{:S(2)}, u32[]{:S(2)}) collective-permute-start(f32[8,512]{1,0:T(8,128)S(1)} %get-tuple-element.54), channel_id=1, source_target_pairs={{0,8},{4,12},{8,16},{12,20},{16,24},{20,28},{24,32},{28,36},{32,40... | collective-permute-start | bytes 49160 | tf_op jit(solution)/shard_map/ppermute | solution.py:20
  89.4 7.0 %collective-permute-start.5 = (f32[8,512]{1,0:T(8,128)S(1)}, f32[8,512]{1,0:T(8,128)S(1)}, u32[]{:S(2)}, u32[]{:S(2)}) collective-permute-start(f32[8,512]{1,0:T(8,128)S(1)} %get-tuple-element.53), channel_id=1, source_target_pairs={{0,12},{4,16},{8,20},{12,24},{16,28},{20,32},{24,36},{28,40},{32,4... | collective-permute-start | bytes 49160 | tf_op jit(solution)/shard_map/ppermute | solution.py:20
  91.4 5.0 %collective-permute-start.3 = (f32[8,512]{1,0:T(8,128)S(1)}, f32[8,512]{1,0:T(8,128)S(1)}, u32[]{:S(2)}, u32[]{:S(2)}) collective-permute-start(f32[8,512]{1,0:T(8,128)S(1)} %get-tuple-element.55), channel_id=1, source_target_pairs={{0,4},{4,8},{8,12},{12,16},{16,20},{20,24},{24,28},{28,32},{32,36}... | collective-permute-start | bytes 49160 | tf_op jit(solution)/shard_map/ppermute | solution.py:20
  92.4 8.2 %all-to-all-start.4 = ((s32[4,1,544]{2,1,0:T(1,128)}), s32[4,1,544]{2,1,0:T(1,128)S(1)}, u32[]{:S(2)}, u32[]{:S(2)}) async-start(s32[4,1,544]{2,1,0:T(1,128)} %broadcast_in_dim.4), calls=%async_computation.4 | async-start | bytes 20480 | tf_op jit(solution)/shard_map/all_to_all | solution.py:24
  108.1 42.6 %all-to-all-start.2 = ((f32[256,8,128]{2,1,0:T(8,128)}), f32[256,8,128]{2,1,0:T(8,128)S(1)}, u32[]{:S(2)}, u32[]{:S(2)}) async-start(f32[256,8,128]{2,1,0:T(8,128)} %bitcast.34), calls=%async_computation.2 | async-start | bytes 2097152 | tf_op jit(solution)/shard_map/all_to_all | solution.py:24
  150.6 1.0 copy-start.2
where the time goes:
time: 178 us; the launch traced here: 177 us
  waiting for transfers between devices  55.2 us (31%)
  starting transfers between devices  43.2 us (24%)
  Pallas kernels  30.3 us (17%)
  blocking collectives  23.1 us (13%)
  local copies, waits for them, and re-layouts  21.9 us (12%)
  other arithmetic  2.45 us (1%)
    all_to_all x4, waiting for transfers between devices, exchanged(): return lax.all_to_all(value, axis, 0, 0, tiled=True)  43.7 us
    all_to_all x4, starting transfers between devices, exchanged(): return lax.all_to_all(value, axis, 0, 0, tiled=True)  32 us
    all_to_all x2, blocking collectives, exchanged(): return lax.all_to_all(value, axis, 0, 0, tiled=True)  23.1 us
    pallas_call x1, Pallas kernels, grads(): pl.pallas_call(grads_body, out_shape=[jax.ShapeDtypeStruct((width // LANE...  15.2 us
    ppermute x6, waiting for transfers between devices, passed_along(): return lax.ppermute(value, axis, pairs)  11.5 us
    ppermute x6, starting transfers between devices, passed_along(): return lax.ppermute(value, axis, pairs)  11.2 us
    unnamed x24, local copies, waits for them, and re-layouts  7.93 us
    gather x16, local copies, waits for them, and re-layouts  7.9 us
  transfers between devices with their start and end apart: 10, of which 6 were waited for; matrix products, arithmetic and copies ran while one was open for 4% of the time, Pallas kernels for 2%

commit v1 on v0

--- a/solution.py
+++ b/solution.py
@@ -4,6 +4,7 @@
 from jax.experimental import pallas as pl
 from jax.experimental.pallas import tpu as pltpu
 from jax.sharding import PartitionSpec as P
+
 
 HEAVY = 4
 LEARN_RATE = 0.1
@@ -38,19 +39,41 @@
     return lax.dot_general(a, b, (((1,), (1,)), ((), ())), preferred_element_type=f32)
 
 
-def serve_body(head_ids, tail_ids, rows, heads, tails):
+def spread_body(columns, out):
+    rows = columns.shape[1]
+    for q, (start, w) in enumerate(zip(STARTS, WIDTHS)):
+        piece = columns[start : start + w, :]
+        if w < LANES:
+            piece = jnp.concatenate([piece, jnp.zeros((LANES - w, rows), f32)], axis=0)
+        out[:, q * LANES : (q + 1) * LANES] = piece.T
+
+
+def spread_rows(columns):
+    return pl.pallas_call(
+        spread_body,
+        out_shape=jax.ShapeDtypeStruct((columns.shape[1], LANES * len(WIDTHS)), f32),
+        name="spread",
+    )(columns)
+
+
+def serve_body(ids, here, rows, heads, tails):
+    owners = ids.shape[0] // 16
+
     def eight(w, carry):
         for k in range(8):
-            heads[pl.ds(w * 8 + k, 1), :] = rows[pl.ds(head_ids[w * 8 + k], 1), :]
+            heads[pl.ds(w * 8 + k, 1), :] = rows[pl.ds(ids[w * 16 + k], 1), :]
         return carry
 
-    lax.fori_loop(0, heads.shape[0] // 8, eight, 0, unroll=2)
-    for k in range(tails.shape[0]):
-        tails[pl.ds(k, 1), :] = rows[pl.ds(tail_ids[k], 1), :]
-
-
-def serve(head_ids, tail_ids, rows):
+    lax.fori_loop(0, owners, eight, 0, unroll=4)
+    for reach in range(HEAVY):
+        asker = (here[0] + owners - reach) % owners
+        for k in range(8):
+            tails[reach * 8 + k : reach * 8 + k + 1, :] = rows[pl.ds(ids[asker * 16 + 8 + k], 1), :]
+
+
+def serve(ids, here, rows):
     width = rows.shape[1]
+    head_count = ids.shape[0] // 2
     return pl.pallas_call(
         serve_body,
         grid_spec=pltpu.PrefetchScalarGridSpec(
@@ -58,16 +81,16 @@
             grid=(1,),
             in_specs=[pl.BlockSpec(rows.shape, lambda i, a, b: (0, 0))],
             out_specs=[
-                pl.BlockSpec((head_ids.shape[0], width), lambda i, a, b: (0, 0)),
-                pl.BlockSpec((tail_ids.shape[0], width), lambda i, a, b: (0, 0)),
+                pl.BlockSpec((head_count, width), lambda i, a, b: (0, 0)),
+                pl.BlockSpec((HEAVY * 8, width), lambda i, a, b: (0, 0)),
             ],
         ),
         out_shape=[
-            jax.ShapeDtypeStruct((head_ids.shape[0], width), f32),
-            jax.ShapeDtypeStruct((tail_ids.shape[0], width), f32),
+            jax.ShapeDtypeStruct((head_count, width), f32),
+            jax.ShapeDtypeStruct((HEAVY * 8, width), f32),
         ],
         name="serve",
-    )(head_ids, tail_ids, rows)
+    )(ids, here, rows)
 
 
 def prep_body(slots, negs, by_edge, by_slot, count_row, count_col):
@@ -110,7 +133,7 @@
     )(slots, negs)
 
 
-def grads_body(heads, tails, by_edge, by_slot, count_row, count_col, out_heads, out_tails, high, low, d_high, d_low):
+def grads_body(heads, tails, by_edge, by_slot, count_row, count_col, ahead, out_heads, out_tails, high, low, d_high, d_low):
     head_count = heads.shape[0]
     live = head_count + tails.shape[0]
     padded = by_edge.shape[1]
@@ -152,12 +175,14 @@
     out_tails[...] = summed[head_count:, :]
 
 
-def grads(heads, tails, by_edge, by_slot, count_row, count_col):
+def grads(heads, tails, by_edge, by_slot, count_row, count_col, ahead):
     head_count, width = heads.shape
     padded = by_edge.shape[1]
     total = by_edge.shape[0]
+    vmem = pl.BlockSpec(memory_space=pltpu.VMEM)
     return pl.pallas_call(
         grads_body,
+        in_specs=[vmem] * 6 + [pl.BlockSpec(memory_space=pl.ANY)],
         out_shape=[
             jax.ShapeDtypeStruct((width // LANES, head_count, LANES), f32),
             jax.ShapeDtypeStruct(tails.shape, f32),
@@ -169,50 +194,87 @@
             pltpu.VMEM((total, width), bf16),
         ],
         name="grads",
-    )(heads, tails, by_edge, by_slot, count_row, count_col)
-
-
-def owner_body(back, tails, head_ids, tail_ids, out):
-    rows = out.shape[1]
-
-    def part(values, ids):
-        down = lax.broadcasted_iota(jnp.int32, (rows, ids.shape[1]), 0)
-        hot = jnp.where(down == ids, 1.0, 0.0).astype(bf16)
-        high, low = halves(values)
-        return mm(hot, high) + mm(hot, low)
-
-    summed = part(back[...], head_ids[...]) + part(tails[...], tail_ids[...])
+    )(heads, tails, by_edge, by_slot, count_row, count_col, ahead)
+
+
+def hot_body(me, *refs):
+    lists, hot = refs[:-1], refs[-1]
+    rows = hot.shape[0]
+    groups = len(lists)
+    tail_count = HEAVY * 8
+    head_count = lists[0].shape[1] - tail_count
+    for s, ids in enumerate(lists):
+        group = (me[0] + s) % groups
+        down = lax.broadcasted_iota(jnp.int32, (rows, head_count), 0)
+        spot = pl.multiple_of(group * head_count, LANES)
+        hot[:, pl.ds(spot, head_count)] = jnp.where(down == ids[:, :head_count], 1.0, 0.0).astype(bf16)
+    tails = jnp.concatenate([ids[:, head_count:] for ids in lists], axis=1)
+    down = lax.broadcasted_iota(jnp.int32, (rows, tails.shape[1]), 0)
+    hot[:, groups * head_count :] = jnp.where(down == tails, 1.0, 0.0).astype(bf16)
+
+
+def hot_rows(me, lists, rows):
+    vmem = pl.BlockSpec(memory_space=pltpu.VMEM)
+    return pl.pallas_call(
+        hot_body,
+        in_specs=[pl.BlockSpec(memory_space=pltpu.SMEM)] + [vmem] * len(lists),
+        out_shape=jax.ShapeDtypeStruct((rows, len(lists) * lists[0].shape[1]), bf16),
+        name="hot",
+    )(me, *lists)
+
+
+def owner_body(back, tails, hot, out):
+    count = back.shape[0]
+    high, low = halves(back[...])
+    summed = mm(hot[:, :count], high) + mm(hot[:, :count], low)
+    high, low = halves(tails[...])
+    summed += mm(hot[:, count:], high) + mm(hot[:, count:], low)
     out[...] = summed.T[: out.shape[0], :]
 
 
-def owner(back, tails, head_ids, tail_ids, rows):
+def owner(back, tails, hot):
     return pl.pallas_call(
         owner_body,
-        out_shape=jax.ShapeDtypeStruct((max(WIDTHS), rows), f32),
+        out_shape=jax.ShapeDtypeStruct((max(WIDTHS), hot.shape[0]), f32),
         name="owner",
-    )(back, tails, head_ids, tail_ids)
-
-
-def update_body(quarters, rows, sums, new_rows, new_sums):
+    )(back, tails, hot)
+
+
+def update_body(me, own, next1, next2, next3, rows, sums, new_rows, new_sums, quarters, sems):
+    copies = []
+    for s, piece in enumerate((own, next1, next2, next3)):
+        spot = (me[0] + 4 - s) % 4
+        copies.append(pltpu.make_async_copy(piece, quarters.at[spot], sems.at[s]))
+        copies[-1].start()
+    for copy in copies:
+        copy.wait()
     squares = jnp.zeros(sums.shape, f32)
-    for q in range(quarters.shape[0]):
+    for q in range(len(WIDTHS)):
         squares += jnp.sum(quarters[q] * quarters[q], axis=0, keepdims=True)
-    fresh = sums[...] + squares * (1.0 / rows.shape[1])
+    fresh = sums[...] + squares * (1.0 / rows.shape[0])
     new_sums[...] = fresh
     scale = LEARN_RATE / jnp.sqrt(fresh)
-    step = jnp.concatenate([quarters[q, :w, :] * scale for q, w in enumerate(WIDTHS)], axis=0)
-    new_rows[...] = rows[...] - step.T
-
-
-def update(quarters, rows, sums):
+    for q, (start, w) in enumerate(zip(STARTS, WIDTHS)):
+        new_rows[start : start + w, :] = rows[start : start + w, :] - quarters[q, :w, :] * scale
+
+
+def update(me, pieces, rows, sums):
+    vmem = pl.BlockSpec(memory_space=pltpu.VMEM)
     return pl.pallas_call(
         update_body,
+        in_specs=[pl.BlockSpec(memory_space=pltpu.SMEM)]
+        + [pl.BlockSpec(memory_space=pl.ANY)] * len(pieces)
+        + [vmem, vmem],
         out_shape=[
             jax.ShapeDtypeStruct(rows.shape, f32),
             jax.ShapeDtypeStruct(sums.shape, f32),
         ],
+        scratch_shapes=[
+            pltpu.VMEM((len(pieces), *pieces[0].shape), f32),
+            pltpu.SemaphoreType.DMA((len(pieces),)),
+        ],
         name="update",
-    )(quarters, rows, sums)
+    )(me, *pieces, rows, sums)
 
 
 def compact(slots, here, owners, capacity):
@@ -230,47 +292,46 @@
     edges = source_slots.shape[3]
     here = lax.axis_index("dom")
     incoming = exchanged(requests, "dom")
-    spread = jnp.concatenate(
-        [jnp.pad(embedding[:, s : s + w], ((0, 0), (0, LANES - w))) for s, w in zip(STARTS, WIDTHS)],
-        axis=1,
-    )
+    columns = embedding.T
+    spread = spread_rows(columns)
     slots = jnp.stack([source_slots[0, 0], target_slots[0, 0]], axis=1).reshape(1, -1)
     slots = compact(slots, here, owners, capacity)
     live = owners * half + HEAVY * half
     padded = -(-live // LANES) * LANES
     plan = prep(slots, negative_ids[0, 0].reshape(1, -1), edges, live, padded)
 
-    askers = (here - jnp.arange(HEAVY)) % owners
-    tail_ids = incoming[askers, half:].reshape(-1)
-    head_ids = incoming[:, :half].reshape(-1)
-    heads, tails = serve(head_ids, tail_ids, spread)
+    heads, tails = serve(incoming.reshape(-1), here.reshape(1).astype(jnp.int32), spread)
     tails = tails.reshape(HEAVY, half, -1)
     tails = jnp.concatenate(
         [tails[0]] + [passed_along(tails[r], "dom", -r) for r in range(1, HEAVY)], axis=0
     )
     heads = exchanged(heads.reshape(owners, half, -1), "dom").reshape(owners * half, -1)
-    all_ids = exchanged(
-        jnp.broadcast_to(jnp.concatenate([head_ids, tail_ids])[None], (groups, live)), "rep"
-    )
-
-    head_grads, tail_grads = grads(heads, tails, *plan)
+    me = lax.axis_index("rep")
+    mine = me.reshape(1).astype(jnp.int32)
+    askers = jnp.arange(owners)[None, :] == ((here - jnp.arange(HEAVY)) % owners)[:, None]
+    tail_ids = jnp.sum(jnp.where(askers[:, :, None], incoming[None, :, half:], 0), axis=1)
+    ids = jnp.concatenate([incoming[:, :half].reshape(1, -1), tail_ids.reshape(1, -1)], axis=1)
+    near = [ids] + [passed_along(ids, "rep", -s) for s in range(1, groups)]
+    hot = hot_rows(mine, near, rows)
+
+    head_grads, tail_grads = grads(heads, tails, *plan, hot)
     tail_grads = tail_grads.reshape(HEAVY, half, -1)
     tail_grads = jnp.concatenate(
         [tail_grads[0]] + [passed_along(tail_grads[r], "dom", r) for r in range(1, HEAVY)], axis=0
     )
     tail_grads = jnp.moveaxis(tail_grads.reshape(HEAVY * half, groups, LANES), 1, 0)
-    tail_back = exchanged(tail_grads, "rep").reshape(-1, LANES)
+    wanted = [
+        lax.dynamic_index_in_dim(tail_grads, (me + groups - s) % groups, 0, keepdims=False)
+        for s in range(groups)
+    ]
+    tail_back = jnp.concatenate(
+        [wanted[0]] + [passed_along(wanted[s], "rep", -s) for s in range(1, groups)], axis=0
+    )
     back = exchanged(head_grads.reshape(groups * owners, half, LANES), ("rep", "dom"))
-    quarter = owner(
-        back.reshape(-1, LANES),
-        tail_back,
-        all_ids[:, : owners * half].reshape(1, -1),
-        all_ids[:, owners * half :].reshape(1, -1),
-        rows,
-    )
-    quarters = exchanged(jnp.broadcast_to(quarter[None], (groups, *quarter.shape)), "rep")
-    new_rows, new_sums = update(quarters, embedding, adagrad_sum.reshape(1, -1))
-    return new_rows, new_sums.reshape(-1)
+    quarter = owner(back.reshape(-1, LANES), tail_back, hot)
+    pieces = [quarter] + [passed_along(quarter, "rep", s) for s in range(1, len(WIDTHS))]
+    new_rows, new_sums = update(mine, pieces, columns, adagrad_sum.reshape(1, -1))
+    return new_rows.T, new_sums.reshape(-1)
 
 
 def solution(mesh):
@@ -283,4 +344,5 @@
         P("rep", "dom", None, None, None),
     )
     out_specs = (P("dom", None), P("dom"))
+
     return jax.shard_map(local, mesh=mesh, in_specs=in_specs, out_specs=out_specs, check_vma=False)

time: 178 us -> 151 us (0.85)
  blocking collectives: 23.1 us -> 0 us
  local copies, waits for them, and re-layouts: 21.9 us -> 7.63 us
  starting transfers between devices: 43.2 us -> 53.6 us
  waiting for transfers between devices: 55.2 us -> 46.3 us
  Pallas kernels: 30.3 us -> 37.6 us
    all_to_all x4 -> x3, waiting for transfers between devices: 43.7 us -> 8.79 us  [exchanged(): return lax.all_to_all(value, axis, 0, 0, tiled=True)]
    ppermute x6 -> x15, waiting for transfers between devices: 11.5 us -> 37.5 us  [passed_along(): return lax.ppermute(value, axis, pairs)]
    all_to_all x2 -> x0, blocking collectives: 23.1 us -> none  [exchanged(): return lax.all_to_all(value, axis, 0, 0, tiled=True)]
    ppermute x6 -> x15, starting transfers between devices: 11.2 us -> 25.8 us  [passed_along(): return lax.ppermute(value, axis, pairs)]
    gather x16 -> x0, local copies, waits for them, and re-layouts: 7.9 us -> none
    pallas_call x3 -> x5, Pallas kernels: 21.5 us -> 28.3 us  [the longest x1 15.3 us: grads(): pl.pallas_call(grads_body, in_specs=[vmem] * 6 + [pl.BlockSpec(memory_spa...]
    all_to_all x4 -> x3, starting transfers between devices: 32 us -> 27.8 us  [exchanged(): return lax.all_to_all(value, axis, 0, 0, tiled=True)]
    unnamed x24 -> x28, local copies, waits for them, and re-layouts: 7.93 us -> 4.7 us
  transfers between devices with their start and end apart: 10 -> 18, of which waited for: 6 -> 11; matrix products, arithmetic and copies ran while one was open for 4% -> 3% of each run, Pallas kernels for 2% -> 6%
where the time goes in v1:
time: 151 us; the launch traced here: 149 us
  starting transfers between devices  53.6 us (35%)
  waiting for transfers between devices  46.3 us (31%)
  Pallas kernels  37.6 us (25%)
  local copies, waits for them, and re-layouts  7.63 us (5%)
  other arithmetic  2.94 us (2%)
    ppermute x15, waiting for transfers between devices, passed_along(): return lax.ppermute(value, axis, pairs)  37.5 us
    all_to_all x3, starting transfers between devices, exchanged(): return lax.all_to_all(value, axis, 0, 0, tiled=True)  27.8 us
    ppermute x15, starting transfers between devices, passed_along(): return lax.ppermute(value, axis, pairs)  25.8 us
    pallas_call x1, Pallas kernels, grads(): pl.pallas_call(grads_body, in_specs=[vmem] * 6 + [pl.BlockSpec(memory_spa...  15.3 us
    all_to_all x3, waiting for transfers between devices, exchanged(): return lax.all_to_all(value, axis, 0, 0, tiled=True)  8.79 us
    pallas_call x1, Pallas kernels, serve(): pl.pallas_call(serve_body, grid_spec=pltpu.PrefetchScalarGridSpec(num_sca...  5.12 us
    unnamed x28, local copies, waits for them, and re-layouts  4.7 us
    pallas_call x1, Pallas kernels, prep(): pl.pallas_call(prep_body, out_shape=[jax.ShapeDtypeStruct((total, padded)...  4.14 us
  transfers between devices with their start and end apart: 18, of which 11 were waited for; matrix products, arithmetic and copies ran while one was open for 3% of the time, Pallas kernels for 6%

profile of v1, /device:TPU:1, one launch (start us, length us, event | category | flops | bytes accessed | tf_op | source)
XLA Modules:
  0.0 149.0 jit_solution(8627951428309192667)
XLA Ops:
  0.6 1.4 copy.17
  2.0 13.1 %all-to-all-start = ((s32[64,1,16]{2,1,0:T(1,128)}), s32[64,1,16]{2,1,0:T(1,128)S(1)}, u32[]{:S(2)}, u32[]{:S(2)}) async-start(s32[64,1,16]{2,1,0:T(1,128)} %bitcast.1), calls=%async_computation | async-start | bytes 65536 | tf_op jit(solution)/shard_map/all_to_all | solution.py:25
  15.2 2.5 %spread.1.rows = f32[512,512]{1,0:T(8,128)} custom-call(f32[400,512]{1,0:T(8,128)} %bitcast.29), custom_call_target="tpu_custom_call" | custom-call | tf_op jit(solution)/shard_map/spread/pallas_call | solution.py:52
  17.7 6.7 %all-to-all-done = s32[64,1,16]{2,1,0:T(1,128)S(1)} async-done(((s32[64,1,16]{2,1,0:T(1,128)}), s32[64,1,16]{2,1,0:T(1,128)S(1)}, u32[]{:S(2)}, u32[]{:S(2)}) %all-to-all-start) | async-done | bytes 4128 | tf_op jit(solution)/shard_map/all_to_all | solution.py:25
  24.4 0.5 broadcast.244
  24.9 0.7 reduce.3
  25.7 0.7 reshape.321.ids
  26.3 5.1 %serve.1 = (f32[512,512]{1,0:T(8,128)}, f32[32,512]{1,0:T(8,128)}) custom-call(s32[1024]{0:T(1024)} %reshape.321.ids, s32[1]{0:T(128)} %bitcast.2.here, f32[512,512]{1,0:T(8,128)} %spread.1.rows), custom_call_target="tpu_custom_call" | custom-call | tf_op jit(solution)/shard_map/serve/pallas_call | solution.py:77
  31.5 4.9 %all-to-all-start.1 = ((f32[64,8,512]{2,1,0:T(8,128)}), f32[64,8,512]{2,1,0:T(8,128)S(1)}, u32[]{:S(2)}, u32[]{:S(2)}) async-start(f32[64,8,512]{2,1,0:T(8,128)} %bitcast.32), calls=%async_computation.1 | async-start | bytes 2097152 | tf_op jit(solution)/shard_map/all_to_all | solution.py:25
  37.0 2.6 %collective-permute-start.3 = (s32[1,544]{1,0:T(1,128)S(1)}, s32[1,544]{1,0:T(1,128)S(1)}, u32[]{:S(2)}, u32[]{:S(2)}) collective-permute-start(s32[1,544]{1,0:T(1,128)S(1)} %constant_dynamic-update-slice_fusion.refs_0_), channel_id=1, source_target_pairs={{0,3},{1,0},{2,1},{3,2},{4,7},{5,4},{6,5},{7,6},{8,11},{9,8},{10,9... | collective-permute-start | bytes 6536 | tf_op jit(solution)/shard_map/ppermute | solution.py:21
  39.6 0.5 collective-permute-start.4
  40.1 0.6 collective-permute-start.5
  40.7 1.5 collective-permute-start
  42.2 4.9 %collective-permute-start.1 = (f32[8,512]{1,0:T(8,128)S(1)}, f32[8,512]{1,0:T(8,128)S(1)}, u32[]{:S(2)}, u32[]{:S(2)}) collective-permute-start(f32[8,512]{1,0:T(8,128)S(1)} %get-tuple-element.32), channel_id=1, source_target_pairs={{0,248},{4,252},{8,0},{12,4},{16,8},{20,12},{24,16},{28,20},{32,24... | collective-permute-start | bytes 49160 | tf_op jit(solution)/shard_map/ppermute | solution.py:21
  47.1 1.7 %collective-permute-start.2 = (f32[8,512]{1,0:T(8,128)S(1)}, f32[8,512]{1,0:T(8,128)S(1)}, u32[]{:S(2)}, u32[]{:S(2)}) collective-permute-start(f32[8,512]{1,0:T(8,128)S(1)} %get-tuple-element.31), channel_id=1, source_target_pairs={{0,244},{4,248},{8,252},{12,0},{16,4},{20,8},{24,12},{28,16},{32,2... | collective-permute-start | bytes 49160 | tf_op jit(solution)/shard_map/ppermute | solution.py:21
  48.8 0.7 compare_select_fusion.2.slots
  49.5 0.6 reshape_squeeze.3.negs
  50.1 4.1 %prep.1 = (bf16[2048,640]{1,0:T(8,128)(2,1)}, bf16[544,2048]{1,0:T(8,128)(2,1)}, f32[2,8,512]{2,1,0:T(8,128)}, f32[2,512,128]{2,1,0:T(8,128)}) custom-call(s32[1,2048]{1,0:T(1,128)} %compare_select_fusion.2.slots, s32[1,2048]{1,0:T(1,128)} %reshape_squeeze.3.negs), custom_call_target="tpu_custom_call" | custom-call | tf_op jit(solution)/shard_map/prep/pallas_call | solution.py:124
  54.3 0.5 copy-done.11
  54.9 3.0 %hot.1.ahead = bf16[512,2176]{1,0:T(8,128)(2,1)} custom-call(s32[1]{0:T(128)} %bitcast.me, s32[1,544]{1,0:T(1,128)} %copy-done.6, s32[1,544]{1,0:T(1,128)} %copy-done.10, s32[1,544]{1,0:T(1,128)} %copy-done.11, s32[1,544]{1,0:T(1,128)} %copy-done.12), custom_call_target="tpu_custom_call" | custom-call | tf_op jit(solution)/shard_map/hot/pallas_call | solution.py:218
  57.9 3.9 %collective-permute-done = f32[8,512]{1,0:T(8,128)S(1)} collective-permute-done((f32[8,512]{1,0:T(8,128)S(1)}, f32[8,512]{1,0:T(8,128)S(1)}, u32[]{:S(2)}, u32[]{:S(2)}) %collective-permute-start) | collective-permute-done | bytes 16416 | tf_op jit(solution)/shard_map/ppermute | solution.py:21
  61.8 0.4 collective-permute-done.2
  62.2 0.6 pad_maximum_fusion.tails
  62.8 2.1 %all-to-all-done.1 = f32[64,8,512]{2,1,0:T(8,128)S(1)} async-done(((f32[64,8,512]{2,1,0:T(8,128)}), f32[64,8,512]{2,1,0:T(8,128)S(1)}, u32[]{:S(2)}, u32[]{:S(2)}) %all-to-all-start.1) | async-done | bytes 1048608 | tf_op jit(solution)/shard_map/all_to_all | solution.py:25
  64.9 1.0 copy-done.1
  65.9 15.3 %grads.1 = (f32[4,512,128]{2,1,0:T(8,128)}, f32[32,512]{1,0:T(8,128)}) custom-call(f32[512,512]{1,0:T(8,128)} %bitcast.28, f32[32,512]{1,0:T(8,128)} %pad_maximum_fusion.tails, bf16[2048,640]{1,0:T(8,128)(2,1)} %get-tuple-element.14.by_edge, bf16[544,2048]{1,0:T(8,128)(2,1)} %get-tuple-element.15.by_slot, f32[2,8,512]{2,1,0:T(8,128)} %get-tuple-element.16.count_row, ...), custom_call_target="tpu_custom_call" | custom-call | tf_op jit(solution)/shard_map/grads/pallas_call | solution.py:183
  81.2 9.8 %all-to-all-start.2 = ((f32[256,8,128]{2,1,0:T(8,128)}), f32[256,8,128]{2,1,0:T(8,128)S(1)}, u32[]{:S(2)}, u32[]{:S(2)}) async-start(f32[256,8,128]{2,1,0:T(8,128)} %bitcast.31), calls=%async_computation.2 | async-start | bytes 2097152 | tf_op jit(solution)/shard_map/all_to_all | solution.py:25
  91.0 0.8 slice_bitcast_fusion
  91.8 1.8 %collective-permute-start.6 = (f32[8,512]{1,0:T(8,128)S(1)}, f32[8,512]{1,0:T(8,128)S(1)}, u32[]{:S(2)}, u32[]{:S(2)}) collective-permute-start(f32[8,512]{1,0:T(8,128)S(1)} %get-tuple-element.29), channel_id=1, source_target_pairs={{0,4},{4,8},{8,12},{12,16},{16,20},{20,24},{24,28},{28,32},{32,36}... | collective-permute-start | bytes 49160 | tf_op jit(solution)/shard_map/ppermute | solution.py:21
  93.6 1.5 collective-permute-start.7
  95.0 1.6 %collective-permute-start.8 = (f32[8,512]{1,0:T(8,128)S(1)}, f32[8,512]{1,0:T(8,128)S(1)}, u32[]{:S(2)}, u32[]{:S(2)}) collective-permute-start(f32[8,512]{1,0:T(8,128)S(1)} %get-tuple-element.27), channel_id=1, source_target_pairs={{0,12},{4,16},{8,20},{12,24},{16,28},{20,32},{24,36},{28,40},{32,4... | collective-permute-start | bytes 49160 | tf_op jit(solution)/shard_map/ppermute | solution.py:21
  96.6 7.9 %collective-permute-done.6 = f32[8,512]{1,0:T(8,128)S(1)} collective-permute-done((f32[8,512]{1,0:T(8,128)S(1)}, f32[8,512]{1,0:T(8,128)S(1)}, u32[]{:S(2)}, u32[]{:S(2)}) %collective-permute-start.6) | collective-permute-done | bytes 16416 | tf_op jit(solution)/shard_map/ppermute | solution.py:21
  104.6 14.5 %collective-permute-done.7 = f32[8,512]{1,0:T(8,128)S(1)} collective-permute-done((f32[8,512]{1,0:T(8,128)S(1)}, f32[8,512]{1,0:T(8,128)S(1)}, u32[]{:S(2)}, u32[]{:S(2)}) %collective-permute-start.7) | collective-permute-done | bytes 16416 | tf_op jit(solution)/shard_map/ppermute | solution.py:21
  119.0 1.6 %collective-permute-done.8 = f32[8,512]{1,0:T(8,128)S(1)} collective-permute-done((f32[8,512]{1,0:T(8,128)S(1)}, f32[8,512]{1,0:T(8,128)S(1)}, u32[]{:S(2)}, u32[]{:S(2)}) %collective-permute-start.8) | collective-permute-done | bytes 16416 | tf_op jit(solution)/shard_map/ppermute | solution.py:21
  120.6 2.7 %collective-permute-start.10 = (f32[32,128]{1,0:T(8,128)S(1)}, f32[32,128]{1,0:T(8,128)S(1)}, u32[]{:S(2)}, u32[]{:S(2)}) collective-permute-start(f32[32,128]{1,0:T(8,128)S(1)} %get-tuple-element.24), channel_id=1, source_target_pairs={{0,2},{1,3},{2,0},{3,1},{4,6},{5,7},{6,4},{7,5},{8,10},{9,11},{10,... | collective-permute-start | bytes 49160 | tf_op jit(solution)/shard_map/ppermute | solution.py:21
  123.3 0.3 collective-permute-start.11
  123.6 2.4 %collective-permute-start.9 = (f32[32,128]{1,0:T(8,128)S(1)}, f32[32,128]{1,0:T(8,128)S(1)}, u32[]{:S(2)}, u32[]{:S(2)}) collective-permute-start(f32[32,128]{1,0:T(8,128)S(1)} %get-tuple-element.25), channel_id=1, source_target_pairs={{0,3},{1,0},{2,1},{3,2},{4,7},{5,4},{6,5},{7,6},{8,11},{9,8},{10,9... | collective-permute-start | bytes 49160 | tf_op jit(solution)/shard_map/ppermute | solution.py:21
  126.0 1.1 collective-permute-done.11
  127.1 0.6 pad_maximum_fusion.2.tails
  127.7 1.0 copy-done
  128.7 4.1 %owner.1.own = f32[104,512]{1,0:T(8,128)} custom-call(f32[2048,128]{1,0:T(8,128)} %bitcast.27, f32[128,128]{1,0:T(8,128)} %pad_maximum_fusion.2.tails, bf16[512,2176]{1,0:T(8,128)(2,1)} %hot.1.ahead), custom_call_target="tpu_custom_call" | custom-call | tf_op jit(solution)/shard_map/owner/pallas_call | solution.py:236
  132.8 3.9 %collective-permute-start.13 = (f32[104,512]{1,0:T(8,128)}, f32[104,512]{1,0:T(8,128)S(1)}, u32[]{:S(2)}, u32[]{:S(2)}) collective-permute-start(f32[104,512]{1,0:T(8,128)} %owner.1.own), channel_id=1, source_target_pairs={{0,2},{1,3},{2,0},{3,1},{4,6},{5,7},{6,4},{7,5},{8,10},{9,11},{10,... | collective-permute-start | bytes 638984 | tf_op jit(solution)/shard_map/ppermute | solution.py:21
  136.6 2.3 %collective-permute-done.12.next1 = f32[104,512]{1,0:T(8,128)S(1)} collective-permute-done((f32[104,512]{1,0:T(8,128)}, f32[104,512]{1,0:T(8,128)S(1)}, u32[]{:S(2)}, u32[]{:S(2)}) %collective-permute-start.12) | collective-permute-done | bytes 213024 | tf_op jit(solution)/shard_map/ppermute | solution.py:21
  138.9 5.5 %collective-permute-done.13.next2 = f32[104,512]{1,0:T(8,128)S(1)} collective-permute-done((f32[104,512]{1,0:T(8,128)}, f32[104,512]{1,0:T(8,128)S(1)}, u32[]{:S(2)}, u32[]{:S(2)}) %collective-permute-start.13) | collective-permute-done | bytes 213024 | tf_op jit(solution)/shard_map/ppermute | solution.py:21
  144.3 0.3 collective-permute-done.14.next3
  144.7 0.4 copy-done.3
  145.0 0.3 copy-done.4
  145.3 3.5 %update.1 = (f32[400,512]{1,0:T(8,128)}, f32[1,512]{1,0:T(1,128)}) custom-call(s32[1]{0:T(128)} %bitcast.me, f32[104,512]{1,0:T(8,128)} %owner.1.own, f32[104,512]{1,0:T(8,128)} %copy-done.2, f32[104,512]{1,0:T(8,128)} %copy-done.3, f32[104,512]{1,0:T(8,128)} %copy-done.4, f32[400,512]{1,0:T(8,128)} %bitcast.30, f32[1,512]{1,0:T(1,128)} %bitcast.39), custom_call_target="tpu_custom_call" | custom-call | tf_op jit(solution)/shard_map/update/pallas_call | solution.py:263
  (45 shorter events, 0.7 us)
Async XLA Ops:
  2.0 22.4 %all-to-all-start = ((s32[64,1,16]{2,1,0:T(1,128)}), s32[64,1,16]{2,1,0:T(1,128)S(1)}, u32[]{:S(2)}, u32[]{:S(2)}) async-start(s32[64,1,16]{2,1,0:T(1,128)} %bitcast.1), calls=%async_computation | async-start | bytes 65536 | tf_op jit(solution)/shard_map/all_to_all | solution.py:25
  15.2 21.2 %copy-start.8 = (s32[1,1,2,512]{3,2,1,0:T(2,128)S(1)}, s32[1,1,2,512]{3,2,1,0:T(2,128)}, u32[]{:S(2)}) copy-start(s32[1,1,2,512]{3,2,1,0:T(2,128)} %param.10) | copy-start | bytes 12292
  15.2 21.2 %copy-start.9 = (s32[1,1,2,512]{3,2,1,0:T(2,128)S(1)}, s32[1,1,2,512]{3,2,1,0:T(2,128)}, u32[]{:S(2)}) copy-start(s32[1,1,2,512]{3,2,1,0:T(2,128)} %param.9) | copy-start | bytes 12292
  17.7 31.8 %copy-start.7 = (s32[1,1,2,2,512]{4,3,2,1,0:T(2,128)S(1)}, s32[1,1,2,2,512]{4,3,2,1,0:T(2,128)}, u32[]{:S(2)}) copy-start(s32[1,1,2,2,512]{4,3,2,1,0:T(2,128)} %param.11) | copy-start | bytes 24580
  31.5 9.2 %copy-start.5 = (f32[32,512]{1,0:T(8,128)S(1)}, f32[32,512]{1,0:T(8,128)}, u32[]{:S(2)}) copy-start(f32[32,512]{1,0:T(8,128)} %get-tuple-element.13) | copy-start | bytes 196612
  31.5 33.4 %all-to-all-start.1 = ((f32[64,8,512]{2,1,0:T(8,128)}), f32[64,8,512]{2,1,0:T(8,128)S(1)}, u32[]{:S(2)}, u32[]{:S(2)}) async-start(f32[64,8,512]{2,1,0:T(8,128)} %bitcast.32), calls=%async_computation.1 | async-start | bytes 2097152 | tf_op jit(solution)/shard_map/all_to_all | solution.py:25
  37.0 17.3 %copy-start.6 = (s32[1,544]{1,0:T(1,128)}, s32[1,544]{1,0:T(1,128)S(1)}, u32[]{:S(2)}) copy-start(s32[1,544]{1,0:T(1,128)S(1)} %constant_dynamic-update-slice_fusion.refs_0_) | copy-start | bytes 6532
  37.0 10.1 %collective-permute-start.3 = (s32[1,544]{1,0:T(1,128)S(1)}, s32[1,544]{1,0:T(1,128)S(1)}, u32[]{:S(2)}, u32[]{:S(2)}) collective-permute-start(s32[1,544]{1,0:T(1,128)S(1)} %constant_dynamic-update-slice_fusion.refs_0_), channel_id=1, source_target_pairs={{0,3},{1,0},{2,1},{3,2},{4,7},{5,4},{6,5},{7,6},{8,11},{9,8},{10,9... | collective-permute-start | bytes 6536 | tf_op jit(solution)/shard_map/ppermute | solution.py:21
  39.6 14.7 %collective-permute-start.4 = (s32[1,544]{1,0:T(1,128)S(1)}, s32[1,544]{1,0:T(1,128)S(1)}, u32[]{:S(2)}, u32[]{:S(2)}) collective-permute-start(s32[1,544]{1,0:T(1,128)S(1)} %constant_dynamic-update-slice_fusion.refs_0_), channel_id=1, source_target_pairs={{0,2},{1,3},{2,0},{3,1},{4,6},{5,7},{6,4},{7,5},{8,10},{9,11},{10,... | collective-permute-start | bytes 6536 | tf_op jit(solution)/shard_map/ppermute | solution.py:21
  40.1 14.2 %collective-permute-start.5 = (s32[1,544]{1,0:T(1,128)S(1)}, s32[1,544]{1,0:T(1,128)S(1)}, u32[]{:S(2)}, u32[]{:S(2)}) collective-permute-start(s32[1,544]{1,0:T(1,128)S(1)} %constant_dynamic-update-slice_fusion.refs_0_), channel_id=1, source_target_pairs={{0,1},{1,2},{2,3},{3,0},{4,5},{5,6},{6,7},{7,4},{8,9},{9,10},{10,1... | collective-permute-start | bytes 6536 | tf_op jit(solution)/shard_map/ppermute | solution.py:21
  40.7 21.1 %collective-permute-start = (f32[8,512]{1,0:T(8,128)S(1)}, f32[8,512]{1,0:T(8,128)S(1)}, u32[]{:S(2)}, u32[]{:S(2)}) collective-permute-start(f32[8,512]{1,0:T(8,128)S(1)} %get-tuple-element.33), channel_id=1, source_target_pairs={{0,252},{4,0},{8,4},{12,8},{16,12},{20,16},{24,20},{28,24},{32,28}... | collective-permute-start | bytes 49160 | tf_op jit(solution)/shard_map/ppermute | solution.py:21
  42.2 19.6 %collective-permute-start.1 = (f32[8,512]{1,0:T(8,128)S(1)}, f32[8,512]{1,0:T(8,128)S(1)}, u32[]{:S(2)}, u32[]{:S(2)}) collective-permute-start(f32[8,512]{1,0:T(8,128)S(1)} %get-tuple-element.32), channel_id=1, source_target_pairs={{0,248},{4,252},{8,0},{12,4},{16,8},{20,12},{24,16},{28,20},{32,24... | collective-permute-start | bytes 49160 | tf_op jit(solution)/shard_map/ppermute | solution.py:21
  47.1 7.2 %copy-start.10 = (s32[1,544]{1,0:T(1,128)}, s32[1,544]{1,0:T(1,128)S(1)}, u32[]{:S(2)}) copy-start(s32[1,544]{1,0:T(1,128)S(1)} %collective-permute-done.3.refs_1_) | copy-start | bytes 6532
  47.1 15.1 %collective-permute-start.2 = (f32[8,512]{1,0:T(8,128)S(1)}, f32[8,512]{1,0:T(8,128)S(1)}, u32[]{:S(2)}, u32[]{:S(2)}) collective-permute-start(f32[8,512]{1,0:T(8,128)S(1)} %get-tuple-element.31), channel_id=1, source_target_pairs={{0,244},{4,248},{8,252},{12,0},{16,4},{20,8},{24,12},{28,16},{32,2... | collective-permute-start | bytes 49160 | tf_op jit(solution)/shard_map/ppermute | solution.py:21
  54.2 0.6 copy-start.11
  54.3 0.6 copy-start.12
  64.9 1.0 copy-start.1
  81.2 46.5 %all-to-all-start.2 = ((f32[256,8,128]{2,1,0:T(8,128)}), f32[256,8,128]{2,1,0:T(8,128)S(1)}, u32[]{:S(2)}, u32[]{:S(2)}) async-start(f32[256,8,128]{2,1,0:T(8,128)} %bitcast.31), calls=%async_computation.2 | async-start | bytes 2097152 | tf_op jit(solution)/shard_map/all_to_all | solution.py:25
  91.8 12.8 %collective-permute-start.6 = (f32[8,512]{1,0:T(8,128)S(1)}, f32[8,512]{1,0:T(8,128)S(1)}, u32[]{:S(2)}, u32[]{:S(2)}) collective-permute-start(f32[8,512]{1,0:T(8,128)S(1)} %get-tuple-element.29), channel_id=1, source_target_pairs={{0,4},{4,8},{8,12},{12,16},{16,20},{20,24},{24,28},{28,32},{32,36}... | collective-permute-start | bytes 49160 | tf_op jit(solution)/shard_map/ppermute | solution.py:21
  93.6 25.4 %collective-permute-start.7 = (f32[8,512]{1,0:T(8,128)S(1)}, f32[8,512]{1,0:T(8,128)S(1)}, u32[]{:S(2)}, u32[]{:S(2)}) collective-permute-start(f32[8,512]{1,0:T(8,128)S(1)} %get-tuple-element.28), channel_id=1, source_target_pairs={{0,8},{4,12},{8,16},{12,20},{16,24},{20,28},{24,32},{28,36},{32,40... | collective-permute-start | bytes 49160 | tf_op jit(solution)/shard_map/ppermute | solution.py:21
  95.0 25.6 %collective-permute-start.8 = (f32[8,512]{1,0:T(8,128)S(1)}, f32[8,512]{1,0:T(8,128)S(1)}, u32[]{:S(2)}, u32[]{:S(2)}) collective-permute-start(f32[8,512]{1,0:T(8,128)S(1)} %get-tuple-element.27), channel_id=1, source_target_pairs={{0,12},{4,16},{8,20},{12,24},{16,28},{20,32},{24,36},{28,40},{32,4... | collective-permute-start | bytes 49160 | tf_op jit(solution)/shard_map/ppermute | solution.py:21
  120.6 5.3 %collective-permute-start.10 = (f32[32,128]{1,0:T(8,128)S(1)}, f32[32,128]{1,0:T(8,128)S(1)}, u32[]{:S(2)}, u32[]{:S(2)}) collective-permute-start(f32[32,128]{1,0:T(8,128)S(1)} %get-tuple-element.24), channel_id=1, source_target_pairs={{0,2},{1,3},{2,0},{3,1},{4,6},{5,7},{6,4},{7,5},{8,10},{9,11},{10,... | collective-permute-start | bytes 49160 | tf_op jit(solution)/shard_map/ppermute | solution.py:21
  123.3 3.8 %collective-permute-start.11 = (f32[32,128]{1,0:T(8,128)S(1)}, f32[32,128]{1,0:T(8,128)S(1)}, u32[]{:S(2)}, u32[]{:S(2)}) collective-permute-start(f32[32,128]{1,0:T(8,128)S(1)} %get-tuple-element.23), channel_id=1, source_target_pairs={{0,1},{1,2},{2,3},{3,0},{4,5},{5,6},{6,7},{7,4},{8,9},{9,10},{10,1... | collective-permute-start | bytes 49160 | tf_op jit(solution)/shard_map/ppermute | solution.py:21
  123.6 3.5 %collective-permute-start.9 = (f32[32,128]{1,0:T(8,128)S(1)}, f32[32,128]{1,0:T(8,128)S(1)}, u32[]{:S(2)}, u32[]{:S(2)}) collective-permute-start(f32[32,128]{1,0:T(8,128)S(1)} %get-tuple-element.25), channel_id=1, source_target_pairs={{0,3},{1,0},{2,1},{3,2},{4,7},{5,4},{6,5},{7,6},{8,11},{9,8},{10,9... | collective-permute-start | bytes 49160 | tf_op jit(solution)/shard_map/ppermute | solution.py:21
  127.7 1.0 copy-start
  132.8 6.1 %collective-permute-start.12 = (f32[104,512]{1,0:T(8,128)}, f32[104,512]{1,0:T(8,128)S(1)}, u32[]{:S(2)}, u32[]{:S(2)}) collective-permute-start(f32[104,512]{1,0:T(8,128)} %owner.1.own), channel_id=1, source_target_pairs={{0,1},{1,2},{2,3},{3,0},{4,5},{5,6},{6,7},{7,4},{8,9},{9,10},{10,1... | collective-permute-start | bytes 638984 | tf_op jit(solution)/shard_map/ppermute | solution.py:21
  132.8 11.6 %collective-permute-start.13 = (f32[104,512]{1,0:T(8,128)}, f32[104,512]{1,0:T(8,128)S(1)}, u32[]{:S(2)}, u32[]{:S(2)}) collective-permute-start(f32[104,512]{1,0:T(8,128)} %owner.1.own), channel_id=1, source_target_pairs={{0,2},{1,3},{2,0},{3,1},{4,6},{5,7},{6,4},{7,5},{8,10},{9,11},{10,... | collective-permute-start | bytes 638984 | tf_op jit(solution)/shard_map/ppermute | solution.py:21
  136.6 8.0 %collective-permute-start.14 = (f32[104,512]{1,0:T(8,128)}, f32[104,512]{1,0:T(8,128)S(1)}, u32[]{:S(2)}, u32[]{:S(2)}) collective-permute-start(f32[104,512]{1,0:T(8,128)} %owner.1.own), channel_id=1, source_target_pairs={{0,3},{1,0},{2,1},{3,2},{4,7},{5,4},{6,5},{7,6},{8,11},{9,8},{10,9... | collective-permute-start | bytes 638984 | tf_op jit(solution)/shard_map/ppermute | solution.py:21
  138.9 5.8 %copy-start.2 = (f32[104,512]{1,0:T(8,128)}, f32[104,512]{1,0:T(8,128)S(1)}, u32[]{:S(2)}) copy-start(f32[104,512]{1,0:T(8,128)S(1)} %collective-permute-done.12.next1) | copy-start | bytes 638980
  144.3 0.7 copy-start.3
  144.7 0.7 copy-start.4

commit v2 on v1

--- a/solution.py
+++ b/solution.py
@@ -31,6 +31,23 @@
     return high, low
 
 
+VMEM = pl.BlockSpec(memory_space=pltpu.VMEM)
+SMEM = pl.BlockSpec(memory_space=pltpu.SMEM)
+HBM = pl.BlockSpec(memory_space=pltpu.HBM)
+
+
+def room(mib):
+    return pltpu.CompilerParams(vmem_limit_bytes=mib << 20)
+
+
+def far(x):
+    return pltpu.with_memory_space_constraint(x, pltpu.HBM)
+
+
+def near(x):
+    return pltpu.with_memory_space_constraint(x, pltpu.VMEM)
+
+
 def mm(a, b):
     return jnp.dot(a, b, preferred_element_type=f32)
 
@@ -51,46 +68,53 @@
 def spread_rows(columns):
     return pl.pallas_call(
         spread_body,
-        out_shape=jax.ShapeDtypeStruct((columns.shape[1], LANES * len(WIDTHS)), f32),
+        out_specs=VMEM,
+        out_shape=pltpu.VMEM((columns.shape[1], LANES * len(WIDTHS)), f32),
+        compiler_params=room(16),
         name="spread",
     )(columns)
 
 
-def serve_body(ids, here, rows, heads, tails):
-    owners = ids.shape[0] // 16
+def serve_body(ids, here, rows, heads, tails, picked, sems):
+    owners = ids.shape[0]
+    parts = sems.shape[0]
+    each = owners // parts
 
     def eight(w, carry):
+        taken = [rows[pl.ds(ids[w, 0, k], 1), :] for k in range(8)]
         for k in range(8):
-            heads[pl.ds(w * 8 + k, 1), :] = rows[pl.ds(ids[w * 16 + k], 1), :]
+            picked[pl.ds(w * 8 + k, 1), :] = taken[k]
         return carry
 
-    lax.fori_loop(0, owners, eight, 0, unroll=4)
     for reach in range(HEAVY):
         asker = (here[0] + owners - reach) % owners
         for k in range(8):
-            tails[reach * 8 + k : reach * 8 + k + 1, :] = rows[pl.ds(ids[asker * 16 + 8 + k], 1), :]
+            tails[reach * 8 + k : reach * 8 + k + 1, :] = rows[pl.ds(ids[asker, 0, 8 + k], 1), :]
+    copies = []
+    for part in range(parts):
+        lax.fori_loop(part * each, (part + 1) * each, eight, 0, unroll=4)
+        span = pl.ds(part * each * 8, each * 8)
+        copies.append(pltpu.make_async_copy(picked.at[span], heads.at[span], sems.at[part]))
+        copies[-1].start()
+    for copy in copies:
+        copy.wait()
 
 
 def serve(ids, here, rows):
     width = rows.shape[1]
-    head_count = ids.shape[0] // 2
+    head_count = ids.shape[0] * 8
     return pl.pallas_call(
         serve_body,
-        grid_spec=pltpu.PrefetchScalarGridSpec(
-            num_scalar_prefetch=2,
-            grid=(1,),
-            in_specs=[pl.BlockSpec(rows.shape, lambda i, a, b: (0, 0))],
-            out_specs=[
-                pl.BlockSpec((head_count, width), lambda i, a, b: (0, 0)),
-                pl.BlockSpec((HEAVY * 8, width), lambda i, a, b: (0, 0)),
-            ],
-        ),
+        in_specs=[SMEM, SMEM, VMEM],
+        out_specs=[HBM, VMEM],
         out_shape=[
-            jax.ShapeDtypeStruct((head_count, width), f32),
+            pltpu.HBM((head_count, width), f32),
             jax.ShapeDtypeStruct((HEAVY * 8, width), f32),
         ],
+        scratch_shapes=[pltpu.VMEM((head_count, width), f32), pltpu.SemaphoreType.DMA((4,))],
+        compiler_params=room(16),
         name="serve",
-    )(ids, here, rows)
+    )(ids, here, near(rows))
 
 
 def prep_body(slots, negs, by_edge, by_slot, count_row, count_col):
@@ -124,21 +148,30 @@
     return pl.pallas_call(
         prep_body,
         out_shape=[
-            jax.ShapeDtypeStruct((total, padded), bf16),
-            jax.ShapeDtypeStruct((live, total), bf16),
-            jax.ShapeDtypeStruct((batches, 8, edges), f32),
-            jax.ShapeDtypeStruct((batches, edges, LANES), f32),
+            pltpu.HBM((total, padded), bf16),
+            pltpu.HBM((live, total), bf16),
+            pltpu.HBM((batches, 8, edges), f32),
+            pltpu.HBM((batches, edges, LANES), f32),
         ],
+        compiler_params=room(24),
         name="prep",
     )(slots, negs)
 
 
-def grads_body(heads, tails, by_edge, by_slot, count_row, count_col, ahead, out_heads, out_tails, high, low, d_high, d_low):
+def grads_body(heads, tails, by_edge, by_slot, count_row, count_col, ahead, out_heads, out_tails,
+               high, low, d_high, d_low, edge_part, slot_part, summed, in_sems, out_sems):
     head_count = heads.shape[0]
     live = head_count + tails.shape[0]
     padded = by_edge.shape[1]
     width = heads.shape[1]
     batches, _, edges = count_row.shape
+    loads = []
+    for p in range(2 * batches):
+        span = pl.ds(p * edges, edges)
+        loads.append(pltpu.make_async_copy(by_edge.at[span], edge_part.at[span], in_sems.at[p]))
+        loads[-1].start()
+    last = pltpu.make_async_copy(by_slot, slot_part, in_sems.at[2 * batches])
+    last.start()
     high[:head_count, :], low[:head_count, :] = halves(heads[...])
     high[head_count:live, :], low[head_count:live, :] = halves(tails[...])
     high[live:, :] = jnp.zeros((padded - live, width), bf16)
@@ -147,7 +180,8 @@
         picks = []
         for side in range(2):
             at = (2 * b + side) * edges
-            chosen = by_edge[at : at + edges, :]
+            loads[2 * b + side].wait()
+            chosen = edge_part[at : at + edges, :]
             picks.append((mm(chosen, high[...]).astype(bf16), mm(chosen, low[...]).astype(bf16)))
         (s_high, s_low), (t_high, t_low) = picks
         scores = mm_nt(s_high, t_high) + mm_nt(s_high, t_low) + mm_nt(s_low, t_high)
@@ -169,32 +203,47 @@
         d_t = mm(g_high, s_high) + mm(g_high, s_low) + mm(g_low, s_high)
         at += edges
         d_high[at : at + edges, :], d_low[at : at + edges, :] = halves(d_t)
-    summed = mm(by_slot[...], d_high[...]) + mm(by_slot[...], d_low[...])
-    for q in range(width // LANES):
-        out_heads[q] = summed[:head_count, q * LANES : (q + 1) * LANES]
-    out_tails[...] = summed[head_count:, :]
+    last.wait()
+    stores = []
+    block = 2 * LANES
+    for h in range(width // block):
+        span = slice(h * block, (h + 1) * block)
+        part = mm(slot_part[...], d_high[:, span]) + mm(slot_part[...], d_low[:, span])
+        for q in range(2):
+            summed[2 * h + q] = part[:head_count, q * LANES : (q + 1) * LANES]
+        out_tails[:, span] = part[head_count:, :]
+        stores.append(
+            pltpu.make_async_copy(summed.at[pl.ds(2 * h, 2)], out_heads.at[pl.ds(2 * h, 2)], out_sems.at[h])
+        )
+        stores[-1].start()
+    for store in stores:
+        store.wait()
 
 
 def grads(heads, tails, by_edge, by_slot, count_row, count_col, ahead):
     head_count, width = heads.shape
     padded = by_edge.shape[1]
     total = by_edge.shape[0]
-    vmem = pl.BlockSpec(memory_space=pltpu.VMEM)
+    shape = (width // LANES, head_count, LANES)
     return pl.pallas_call(
         grads_body,
-        in_specs=[vmem] * 6 + [pl.BlockSpec(memory_space=pl.ANY)],
-        out_shape=[
-            jax.ShapeDtypeStruct((width // LANES, head_count, LANES), f32),
-            jax.ShapeDtypeStruct(tails.shape, f32),
-        ],
+        in_specs=[VMEM, VMEM, HBM, HBM, VMEM, VMEM, HBM],
+        out_specs=[HBM, VMEM],
+        out_shape=[pltpu.HBM(shape, f32), jax.ShapeDtypeStruct(tails.shape, f32)],
         scratch_shapes=[
             pltpu.VMEM((padded, width), bf16),
             pltpu.VMEM((padded, width), bf16),
             pltpu.VMEM((total, width), bf16),
             pltpu.VMEM((total, width), bf16),
+            pltpu.VMEM(by_edge.shape, bf16),
+            pltpu.VMEM(by_slot.shape, bf16),
+            pltpu.VMEM(shape, f32),
+            pltpu.SemaphoreType.DMA((2 * count_row.shape[0] + 1,)),
+            pltpu.SemaphoreType.DMA((width // LANES // 2,)),
         ],
+        compiler_params=room(48),
         name="grads",
-    )(heads, tails, by_edge, by_slot, count_row, count_col, ahead)
+    )(near(heads), tails, far(by_edge), far(by_slot), count_row, count_col, far(ahead))
 
 
 def hot_body(me, *refs):
@@ -218,63 +267,79 @@
     return pl.pallas_call(
         hot_body,
         in_specs=[pl.BlockSpec(memory_space=pltpu.SMEM)] + [vmem] * len(lists),
-        out_shape=jax.ShapeDtypeStruct((rows, len(lists) * lists[0].shape[1]), bf16),
+        out_shape=pltpu.HBM((rows, len(lists) * lists[0].shape[1]), bf16),
+        compiler_params=room(16),
         name="hot",
     )(me, *lists)
 
 
-def owner_body(back, tails, hot, out):
+def owner_body(back, tails, hot, out, spots, sems):
     count = back.shape[0]
-    high, low = halves(back[...])
-    summed = mm(hot[:, :count], high) + mm(hot[:, :count], low)
-    high, low = halves(tails[...])
-    summed += mm(hot[:, count:], high) + mm(hot[:, count:], low)
+    parts = sems.shape[0] - 1
+    each = count // parts
+    spans = [(p * each, each) for p in range(parts)] + [(count, tails.shape[0])]
+    loads = []
+    for p, (at, size) in enumerate(spans):
+        loads.append(pltpu.make_async_copy(hot.at[:, pl.ds(at, size)], spots.at[:, pl.ds(at, size)], sems.at[p]))
+        loads[-1].start()
+    summed = jnp.zeros((hot.shape[0], LANES), f32)
+    for p, (at, size) in enumerate(spans):
+        values = back[at : at + size, :] if p < parts else tails[...]
+        both = jnp.concatenate(halves(values), axis=1)
+        loads[p].wait()
+        part = mm(spots[:, at : at + size], both)
+        summed += part[:, :LANES] + part[:, LANES:]
     out[...] = summed.T[: out.shape[0], :]
 
 
 def owner(back, tails, hot):
     return pl.pallas_call(
         owner_body,
+        in_specs=[VMEM, VMEM, HBM],
+        out_specs=VMEM,
         out_shape=jax.ShapeDtypeStruct((max(WIDTHS), hot.shape[0]), f32),
+        scratch_shapes=[pltpu.VMEM(hot.shape, bf16), pltpu.SemaphoreType.DMA((5,))],
+        compiler_params=room(16),
         name="owner",
-    )(back, tails, hot)
-
-
-def update_body(me, own, next1, next2, next3, rows, sums, new_rows, new_sums, quarters, sems):
-    copies = []
+    )(near(back), tails, far(hot))
+
+
+def update_body(me, own, next1, next2, next3, rows, sums, new_rows, new_sums, quarters, fresh_rows, sems):
     for s, piece in enumerate((own, next1, next2, next3)):
-        spot = (me[0] + 4 - s) % 4
-        copies.append(pltpu.make_async_copy(piece, quarters.at[spot], sems.at[s]))
-        copies[-1].start()
-    for copy in copies:
-        copy.wait()
+        quarters[(me[0] + 4 - s) % 4] = piece[...]
     squares = jnp.zeros(sums.shape, f32)
     for q in range(len(WIDTHS)):
         squares += jnp.sum(quarters[q] * quarters[q], axis=0, keepdims=True)
     fresh = sums[...] + squares * (1.0 / rows.shape[0])
     new_sums[...] = fresh
     scale = LEARN_RATE / jnp.sqrt(fresh)
+    stores = []
     for q, (start, w) in enumerate(zip(STARTS, WIDTHS)):
-        new_rows[start : start + w, :] = rows[start : start + w, :] - quarters[q, :w, :] * scale
+        fresh_rows[start : start + w, :] = rows[start : start + w, :] - quarters[q, :w, :] * scale
+        span = pl.ds(start, w)
+        stores.append(pltpu.make_async_copy(fresh_rows.at[span], new_rows.at[span], sems.at[q]))
+        stores[-1].start()
+    for store in stores:
+        store.wait()
 
 
 def update(me, pieces, rows, sums):
-    vmem = pl.BlockSpec(memory_space=pltpu.VMEM)
     return pl.pallas_call(
         update_body,
-        in_specs=[pl.BlockSpec(memory_space=pltpu.SMEM)]
-        + [pl.BlockSpec(memory_space=pl.ANY)] * len(pieces)
-        + [vmem, vmem],
+        in_specs=[SMEM] + [VMEM] * len(pieces) + [VMEM, VMEM],
+        out_specs=[HBM, VMEM],
         out_shape=[
             jax.ShapeDtypeStruct(rows.shape, f32),
             jax.ShapeDtypeStruct(sums.shape, f32),
         ],
         scratch_shapes=[
             pltpu.VMEM((len(pieces), *pieces[0].shape), f32),
+            pltpu.VMEM(rows.shape, f32),
             pltpu.SemaphoreType.DMA((len(pieces),)),
         ],
+        compiler_params=room(16),
         name="update",
-    )(me, *pieces, rows, sums)
+    )(me, *[near(piece) for piece in pieces], near(rows), sums)
 
 
 def compact(slots, here, owners, capacity):
@@ -291,7 +356,8 @@
     groups = lax.axis_size("rep")
     edges = source_slots.shape[3]
     here = lax.axis_index("dom")
-    incoming = exchanged(requests, "dom")
+    given = exchanged(requests.reshape(owners, 1, capacity), "dom")
+    incoming = given.reshape(owners, capacity)
     columns = embedding.T
     spread = spread_rows(columns)
     slots = jnp.stack([source_slots[0, 0], target_slots[0, 0]], axis=1).reshape(1, -1)
@@ -300,7 +366,7 @@
     padded = -(-live // LANES) * LANES
     plan = prep(slots, negative_ids[0, 0].reshape(1, -1), edges, live, padded)
 
-    heads, tails = serve(incoming.reshape(-1), here.reshape(1).astype(jnp.int32), spread)
+    heads, tails = serve(given, here.reshape(1).astype(jnp.int32), spread)
     tails = tails.reshape(HEAVY, half, -1)
     tails = jnp.concatenate(
         [tails[0]] + [passed_along(tails[r], "dom", -r) for r in range(1, HEAVY)], axis=0
@@ -311,8 +377,8 @@
     askers = jnp.arange(owners)[None, :] == ((here - jnp.arange(HEAVY)) % owners)[:, None]
     tail_ids = jnp.sum(jnp.where(askers[:, :, None], incoming[None, :, half:], 0), axis=1)
     ids = jnp.concatenate([incoming[:, :half].reshape(1, -1), tail_ids.reshape(1, -1)], axis=1)
-    near = [ids] + [passed_along(ids, "rep", -s) for s in range(1, groups)]
-    hot = hot_rows(mine, near, rows)
+    listed = [ids] + [passed_along(ids, "rep", -s) for s in range(1, groups)]
+    hot = hot_rows(mine, listed, rows)
 
     head_grads, tail_grads = grads(heads, tails, *plan, hot)
     tail_grads = tail_grads.reshape(HEAVY, half, -1)

time: 151 us -> 139 us (0.921)
  Pallas kernels: 37.6 us -> 29 us
  waiting for transfers between devices: 46.3 us -> 51.9 us
  local copies, waits for them, and re-layouts: 7.63 us -> 2.96 us
  other arithmetic: 2.94 us -> 0.38 us
    pallas_call x6, Pallas kernels: 34.6 us -> 26.7 us  [the longest x1 14.2 us: grads(): pl.pallas_call(grads_body, in_specs=[VMEM, VMEM, HBM, HBM, VMEM, VMEM, HB...]
    ppermute x15, waiting for transfers between devices: 37.5 us -> 41.5 us  [passed_along(): return lax.ppermute(value, axis, pairs)]
    unnamed x28 -> x18, local copies, waits for them, and re-layouts: 4.7 us -> 2.57 us
    all_to_all x3, waiting for transfers between devices: 8.79 us -> 10.4 us  [exchanged(): return lax.all_to_all(value, axis, 0, 0, tiled=True)]
  transfers between devices with their start and end apart: 18 -> 18, of which waited for: 11 -> 11; matrix products, arithmetic and copies ran while one was open for 3% -> 1% of each run, Pallas kernels for 6% -> 4%
where the time goes in v2:
time: 139 us; the launch traced here: 138 us
  starting transfers between devices  52.9 us (38%)
  waiting for transfers between devices  51.9 us (37%)
  Pallas kernels  29 us (21%)
  local copies, waits for them, and re-layouts  2.96 us (2%)
    ppermute x15, waiting for transfers between devices, passed_along(): return lax.ppermute(value, axis, pairs)  41.5 us
    all_to_all x3, starting transfers between devices, exchanged(): return lax.all_to_all(value, axis, 0, 0, tiled=True)  27.1 us
    ppermute x15, starting transfers between devices, passed_along(): return lax.ppermute(value, axis, pairs)  25.8 us
    pallas_call x1, Pallas kernels, grads(): pl.pallas_call(grads_body, in_specs=[VMEM, VMEM, HBM, HBM, VMEM, VMEM, HB...  14.2 us
    all_to_all x3, waiting for transfers between devices, exchanged(): return lax.all_to_all(value, axis, 0, 0, tiled=True)  10.4 us
    pallas_call x1, Pallas kernels, serve(): pl.pallas_call(serve_body, in_specs=[SMEM, SMEM, VMEM], out_specs=[HBM, V...  4.02 us
    pallas_call x1, Pallas kernels, prep(): pl.pallas_call(prep_body, out_shape=[pltpu.HBM((total, padded), bf16), pl...  3.44 us
    pallas_call x1, Pallas kernels, owner(): pl.pallas_call(owner_body, in_specs=[VMEM, VMEM, HBM], out_specs=VMEM, ou...  3.09 us
  transfers between devices with their start and end apart: 18, of which 11 were waited for; matrix products, arithmetic and copies ran while one was open for 1% of the time, Pallas kernels for 4%

profile of v2, /device:TPU:1, one launch (start us, length us, event | category | flops | bytes accessed | tf_op | source)
XLA Modules:
  0.0 138.1 jit_solution(4586129782647606847)
XLA Ops:
  0.6 1.4 %copy.12 = s32[1,1,64,16]{3,2,1,0:T(8,128)} copy(s32[1,1,64,16]{2,3,1,0:T(8,128)} %param.8) | data formatting | bytes 8192 | tf_op args[2]
  2.0 13.1 %all-to-all-start = ((s32[64,1,16]{2,1,0:T(1,128)}), s32[64,1,16]{2,1,0:T(1,128)S(1)}, u32[]{:S(2)}, u32[]{:S(2)}) async-start(s32[64,1,16]{2,1,0:T(1,128)} %bitcast.1), calls=%async_computation | async-start | bytes 65536 | tf_op jit(solution)/shard_map/all_to_all | solution.py:25
  15.2 0.0 copy-start
  15.2 1.1 copy-done
  16.3 0.3 spread.1.rows
  16.7 0.0 copy-start.5
  16.7 7.7 %all-to-all-done.ids = s32[64,1,16]{2,1,0:T(1,128)S(1)} async-done(((s32[64,1,16]{2,1,0:T(1,128)}), s32[64,1,16]{2,1,0:T(1,128)S(1)}, u32[]{:S(2)}, u32[]{:S(2)}) %all-to-all-start) | async-done | bytes 4128 | tf_op jit(solution)/shard_map/all_to_all | solution.py:25
  24.4 4.0 %serve.1 = (f32[512,512]{1,0:T(8,128)}, f32[32,512]{1,0:T(8,128)S(1)}) custom-call(s32[64,1,16]{2,1,0:T(1,128)S(1)} %all-to-all-done.ids, s32[1]{0:T(128)} %bitcast.2.here, f32[512,512]{1,0:T(8,128)S(1)} %spread.1.rows), custom_call_target="tpu_custom_call" | custom-call | tf_op jit(solution)/shard_map/serve/pallas_call | solution.py:106
  28.4 4.8 %all-to-all-start.1 = ((f32[64,8,512]{2,1,0:T(8,128)}), f32[64,8,512]{2,1,0:T(8,128)S(1)}, u32[]{:S(2)}, u32[]{:S(2)}) async-start(f32[64,8,512]{2,1,0:T(8,128)} %bitcast.34), calls=%async_computation.1 | async-start | bytes 2097152 | tf_op jit(solution)/shard_map/all_to_all | solution.py:25
  33.3 0.1 iota_compare_fusion
  33.4 0.1 fusion.6
  33.4 0.1 copy.14
  33.5 0.2 select_reduce_fusion
  33.7 0.1 reshape.323
  33.8 0.1 reshape.322
  33.9 2.6 %collective-permute-start.3 = (s32[1,544]{1,0:T(1,128)S(1)}, s32[1,544]{1,0:T(1,128)S(1)}, u32[]{:S(2)}, u32[]{:S(2)}) collective-permute-start(s32[1,544]{1,0:T(1,128)S(1)} %constant_dynamic-update-slice_fusion.refs_0_), channel_id=1, source_target_pairs={{0,3},{1,0},{2,1},{3,2},{4,7},{5,4},{6,5},{7,6},{8,11},{9,8},{10,9... | collective-permute-start | bytes 6536 | tf_op jit(solution)/shard_map/ppermute | solution.py:21
  36.4 0.5 collective-permute-start.4
  37.0 0.6 collective-permute-start.5
  37.6 1.4 %collective-permute-start = (f32[8,512]{1,0:T(8,128)S(1)}, f32[8,512]{1,0:T(8,128)S(1)}, u32[]{:S(2)}, u32[]{:S(2)}) collective-permute-start(f32[8,512]{1,0:T(8,128)S(1)} %get-tuple-element.33), channel_id=1, source_target_pairs={{0,252},{4,0},{8,4},{12,8},{16,12},{20,16},{24,20},{28,24},{32,28}... | collective-permute-start | bytes 49160 | tf_op jit(solution)/shard_map/ppermute | solution.py:21
  39.0 4.9 %collective-permute-start.1 = (f32[8,512]{1,0:T(8,128)S(1)}, f32[8,512]{1,0:T(8,128)S(1)}, u32[]{:S(2)}, u32[]{:S(2)}) collective-permute-start(f32[8,512]{1,0:T(8,128)S(1)} %get-tuple-element.32), channel_id=1, source_target_pairs={{0,248},{4,252},{8,0},{12,4},{16,8},{20,12},{24,16},{28,20},{32,24... | collective-permute-start | bytes 49160 | tf_op jit(solution)/shard_map/ppermute | solution.py:21
  43.9 1.7 %collective-permute-start.2 = (f32[8,512]{1,0:T(8,128)S(1)}, f32[8,512]{1,0:T(8,128)S(1)}, u32[]{:S(2)}, u32[]{:S(2)}) collective-permute-start(f32[8,512]{1,0:T(8,128)S(1)} %get-tuple-element.31), channel_id=1, source_target_pairs={{0,244},{4,248},{8,252},{12,0},{16,4},{20,8},{24,12},{28,16},{32,2... | collective-permute-start | bytes 49160 | tf_op jit(solution)/shard_map/ppermute | solution.py:21
  45.6 0.1 compare_select_fusion.2.slots
  45.7 3.4 %prep.1 = (bf16[2048,640]{1,0:T(8,128)(2,1)}, bf16[544,2048]{1,0:T(8,128)(2,1)}, f32[2,8,512]{2,1,0:T(8,128)}, f32[2,512,128]{2,1,0:T(8,128)}) custom-call(s32[1,2048]{1,0:T(1,128)S(1)} %compare_select_fusion.2.slots, s32[1,2048]{1,0:T(1,128)S(1)} %reshape_squeeze.7.negs), custom_call_target="tpu_custom_call" | custom-call | tf_op jit(solution)/shard_map/prep/pallas_call | solution.py:148
  49.2 2.3 %hot.1.ahead = bf16[512,2176]{1,0:T(8,128)(2,1)} custom-call(s32[1]{0:T(128)} %bitcast.me, s32[1,544]{1,0:T(1,128)S(1)} %constant_dynamic-update-slice_fusion.refs_0_, s32[1,544]{1,0:T(1,128)S(1)} %collective-permute-done.3.refs_1_, s32[1,544]{1,0:T(1,128)S(1)} %collective-permute-done.4.refs_2_, s32[1,544]{1,0:T(1,128)S(1)} %collective-permute-done.5.refs_3_), custom_call_target="tpu_custom_call" | custom-call | tf_op jit(solution)/shard_map/hot/pallas_call | solution.py:267
  51.5 7.2 %collective-permute-done = f32[8,512]{1,0:T(8,128)S(1)} collective-permute-done((f32[8,512]{1,0:T(8,128)S(1)}, f32[8,512]{1,0:T(8,128)S(1)}, u32[]{:S(2)}, u32[]{:S(2)}) %collective-permute-start) | collective-permute-done | bytes 16416 | tf_op jit(solution)/shard_map/ppermute | solution.py:21
  58.7 0.4 collective-permute-done.2
  59.1 2.7 %all-to-all-done.1 = f32[64,8,512]{2,1,0:T(8,128)S(1)} async-done(((f32[64,8,512]{2,1,0:T(8,128)}), f32[64,8,512]{2,1,0:T(8,128)S(1)}, u32[]{:S(2)}, u32[]{:S(2)}) %all-to-all-start.1) | async-done | bytes 1048608 | tf_op jit(solution)/shard_map/all_to_all | solution.py:25
  61.8 14.2 %grads.1 = (f32[4,512,128]{2,1,0:T(8,128)}, f32[32,512]{1,0:T(8,128)S(1)}) custom-call(f32[512,512]{1,0:T(8,128)S(1)} %bitcast.28, f32[32,512]{1,0:T(8,128)S(1)} %pad_maximum_fusion.tails, bf16[2048,640]{1,0:T(8,128)(2,1)} %get-tuple-element.14.by_edge, bf16[544,2048]{1,0:T(8,128)(2,1)} %get-tuple-element.15.by_slot, f32[2,8,512]{2,1,0:T(8,128)S(1)} %copy-done.3, ...), custom_call_target="tpu_custom_call" | custom-call | tf_op jit(solution)/shard_map/grads/pallas_call | solution.py:228
  76.0 9.2 %all-to-all-start.2 = ((f32[256,8,128]{2,1,0:T(8,128)}), f32[256,8,128]{2,1,0:T(8,128)S(1)}, u32[]{:S(2)}, u32[]{:S(2)}) async-start(f32[256,8,128]{2,1,0:T(8,128)} %bitcast.33), calls=%async_computation.2 | async-start | bytes 2097152 | tf_op jit(solution)/shard_map/all_to_all | solution.py:25
  85.1 0.0 copy-start.1
  85.1 0.0 copy-start.4
  85.2 1.8 %collective-permute-start.6 = (f32[8,512]{1,0:T(8,128)S(1)}, f32[8,512]{1,0:T(8,128)S(1)}, u32[]{:S(2)}, u32[]{:S(2)}) collective-permute-start(f32[8,512]{1,0:T(8,128)S(1)} %get-tuple-element.29), channel_id=1, source_target_pairs={{0,4},{4,8},{8,12},{12,16},{16,20},{20,24},{24,28},{28,32},{32,36}... | collective-permute-start | bytes 49160 | tf_op jit(solution)/shard_map/ppermute | solution.py:21
  87.0 1.5 %collective-permute-start.7 = (f32[8,512]{1,0:T(8,128)S(1)}, f32[8,512]{1,0:T(8,128)S(1)}, u32[]{:S(2)}, u32[]{:S(2)}) collective-permute-start(f32[8,512]{1,0:T(8,128)S(1)} %get-tuple-element.28), channel_id=1, source_target_pairs={{0,8},{4,12},{8,16},{12,20},{16,24},{20,28},{24,32},{28,36},{32,40... | collective-permute-start | bytes 49160 | tf_op jit(solution)/shard_map/ppermute | solution.py:21
  88.5 1.6 %collective-permute-start.8 = (f32[8,512]{1,0:T(8,128)S(1)}, f32[8,512]{1,0:T(8,128)S(1)}, u32[]{:S(2)}, u32[]{:S(2)}) collective-permute-start(f32[8,512]{1,0:T(8,128)S(1)} %get-tuple-element.27), channel_id=1, source_target_pairs={{0,12},{4,16},{8,20},{12,24},{16,28},{20,32},{24,36},{28,40},{32,4... | collective-permute-start | bytes 49160 | tf_op jit(solution)/shard_map/ppermute | solution.py:21
  90.0 8.7 %collective-permute-done.6 = f32[8,512]{1,0:T(8,128)S(1)} collective-permute-done((f32[8,512]{1,0:T(8,128)S(1)}, f32[8,512]{1,0:T(8,128)S(1)}, u32[]{:S(2)}, u32[]{:S(2)}) %collective-permute-start.6) | collective-permute-done | bytes 16416 | tf_op jit(solution)/shard_map/ppermute | solution.py:21
  98.7 14.5 %collective-permute-done.7 = f32[8,512]{1,0:T(8,128)S(1)} collective-permute-done((f32[8,512]{1,0:T(8,128)S(1)}, f32[8,512]{1,0:T(8,128)S(1)}, u32[]{:S(2)}, u32[]{:S(2)}) %collective-permute-start.7) | collective-permute-done | bytes 16416 | tf_op jit(solution)/shard_map/ppermute | solution.py:21
  113.2 1.6 %collective-permute-done.8 = f32[8,512]{1,0:T(8,128)S(1)} collective-permute-done((f32[8,512]{1,0:T(8,128)S(1)}, f32[8,512]{1,0:T(8,128)S(1)}, u32[]{:S(2)}, u32[]{:S(2)}) %collective-permute-start.8) | collective-permute-done | bytes 16416 | tf_op jit(solution)/shard_map/ppermute | solution.py:21
  114.7 2.7 %collective-permute-start.10 = (f32[32,128]{1,0:T(8,128)S(1)}, f32[32,128]{1,0:T(8,128)S(1)}, u32[]{:S(2)}, u32[]{:S(2)}) collective-permute-start(f32[32,128]{1,0:T(8,128)S(1)} %get-tuple-element.24), channel_id=1, source_target_pairs={{0,2},{1,3},{2,0},{3,1},{4,6},{5,7},{6,4},{7,5},{8,10},{9,11},{10,... | collective-permute-start | bytes 49160 | tf_op jit(solution)/shard_map/ppermute | solution.py:21
  117.4 0.3 collective-permute-start.11
  117.7 2.4 %collective-permute-start.9 = (f32[32,128]{1,0:T(8,128)S(1)}, f32[32,128]{1,0:T(8,128)S(1)}, u32[]{:S(2)}, u32[]{:S(2)}) collective-permute-start(f32[32,128]{1,0:T(8,128)S(1)} %get-tuple-element.25), channel_id=1, source_target_pairs={{0,3},{1,0},{2,1},{3,2},{4,7},{5,4},{6,5},{7,6},{8,11},{9,8},{10,9... | collective-permute-start | bytes 49160 | tf_op jit(solution)/shard_map/ppermute | solution.py:21
  120.1 1.1 collective-permute-done.11
  121.2 3.1 %owner.1.own = f32[104,512]{1,0:T(8,128)S(1)} custom-call(f32[2048,128]{1,0:T(8,128)S(1)} %bitcast.27, f32[128,128]{1,0:T(8,128)S(1)} %pad_maximum_fusion.2.tails, bf16[512,2176]{1,0:T(8,128)(2,1)} %hot.1.ahead), custom_call_target="tpu_custom_call" | custom-call | tf_op jit(solution)/shard_map/owner/pallas_call | solution.py:296
  124.3 0.1 collective-permute-start.12
  124.4 3.8 %collective-permute-start.13 = (f32[104,512]{1,0:T(8,128)S(1)}, f32[104,512]{1,0:T(8,128)S(1)}, u32[]{:S(2)}, u32[]{:S(2)}) collective-permute-start(f32[104,512]{1,0:T(8,128)S(1)} %owner.1.own), channel_id=1, source_target_pairs={{0,2},{1,3},{2,0},{3,1},{4,6},{5,7},{6,4},{7,5},{8,10},{9,11},{10,... | collective-permute-start | bytes 638984 | tf_op jit(solution)/shard_map/ppermute | solution.py:21
  128.2 2.1 %collective-permute-done.12.next1 = f32[104,512]{1,0:T(8,128)S(1)} collective-permute-done((f32[104,512]{1,0:T(8,128)S(1)}, f32[104,512]{1,0:T(8,128)S(1)}, u32[]{:S(2)}, u32[]{:S(2)}) %collective-permute-start.12) | collective-permute-done | bytes 213024 | tf_op jit(solution)/shard_map/ppermute | solution.py:21
  130.3 5.5 %collective-permute-done.13.next2 = f32[104,512]{1,0:T(8,128)S(1)} collective-permute-done((f32[104,512]{1,0:T(8,128)S(1)}, f32[104,512]{1,0:T(8,128)S(1)}, u32[]{:S(2)}, u32[]{:S(2)}) %collective-permute-start.13) | collective-permute-done | bytes 213024 | tf_op jit(solution)/shard_map/ppermute | solution.py:21
  135.8 0.5 collective-permute-done.14.next3
  136.3 1.7 %update.1 = (f32[400,512]{1,0:T(8,128)}, f32[1,512]{1,0:T(1,128)}) custom-call(s32[1]{0:T(128)} %bitcast.me, f32[104,512]{1,0:T(8,128)S(1)} %owner.1.own, f32[104,512]{1,0:T(8,128)S(1)} %collective-permute-done.12.next1, f32[104,512]{1,0:T(8,128)S(1)} %collective-permute-done.13.next2, f32[104,512]{1,0:T(8,128)S(1)} %collective-permute-done.14.next3, ...), custom_call_target="tpu_custom_call" | custom-call | tf_op jit(solution)/shard_map/update/pallas_call | solution.py:327
  (32 shorter events, 0.2 us)
Async XLA Ops:
  2.0 22.4 %all-to-all-start = ((s32[64,1,16]{2,1,0:T(1,128)}), s32[64,1,16]{2,1,0:T(1,128)S(1)}, u32[]{:S(2)}, u32[]{:S(2)}) async-start(s32[64,1,16]{2,1,0:T(1,128)} %bitcast.1), calls=%async_computation | async-start | bytes 65536 | tf_op jit(solution)/shard_map/all_to_all | solution.py:25
  15.2 1.1 copy-start
  16.3 16.9 %copy-start.6 = (s32[1,1,2,512]{3,2,1,0:T(2,128)S(1)}, s32[1,1,2,512]{3,2,1,0:T(2,128)}, u32[]{:S(2)}) copy-start(s32[1,1,2,512]{3,2,1,0:T(2,128)} %param.10) | copy-start | bytes 12292
  16.3 16.9 %copy-start.7 = (s32[1,1,2,512]{3,2,1,0:T(2,128)S(1)}, s32[1,1,2,512]{3,2,1,0:T(2,128)}, u32[]{:S(2)}) copy-start(s32[1,1,2,512]{3,2,1,0:T(2,128)} %param.9) | copy-start | bytes 12292
  16.7 29.0 %copy-start.5 = (s32[1,1,2,2,512]{4,3,2,1,0:T(2,128)S(1)}, s32[1,1,2,2,512]{4,3,2,1,0:T(2,128)}, u32[]{:S(2)}) copy-start(s32[1,1,2,2,512]{4,3,2,1,0:T(2,128)} %param.11) | copy-start | bytes 24580
  28.4 33.3 %all-to-all-start.1 = ((f32[64,8,512]{2,1,0:T(8,128)}), f32[64,8,512]{2,1,0:T(8,128)S(1)}, u32[]{:S(2)}, u32[]{:S(2)}) async-start(f32[64,8,512]{2,1,0:T(8,128)} %bitcast.34), calls=%async_computation.1 | async-start | bytes 2097152 | tf_op jit(solution)/shard_map/all_to_all | solution.py:25
  33.9 10.0 %collective-permute-start.3 = (s32[1,544]{1,0:T(1,128)S(1)}, s32[1,544]{1,0:T(1,128)S(1)}, u32[]{:S(2)}, u32[]{:S(2)}) collective-permute-start(s32[1,544]{1,0:T(1,128)S(1)} %constant_dynamic-update-slice_fusion.refs_0_), channel_id=1, source_target_pairs={{0,3},{1,0},{2,1},{3,2},{4,7},{5,4},{6,5},{7,6},{8,11},{9,8},{10,9... | collective-permute-start | bytes 6536 | tf_op jit(solution)/shard_map/ppermute | solution.py:21
  36.4 12.7 %collective-permute-start.4 = (s32[1,544]{1,0:T(1,128)S(1)}, s32[1,544]{1,0:T(1,128)S(1)}, u32[]{:S(2)}, u32[]{:S(2)}) collective-permute-start(s32[1,544]{1,0:T(1,128)S(1)} %constant_dynamic-update-slice_fusion.refs_0_), channel_id=1, source_target_pairs={{0,2},{1,3},{2,0},{3,1},{4,6},{5,7},{6,4},{7,5},{8,10},{9,11},{10,... | collective-permute-start | bytes 6536 | tf_op jit(solution)/shard_map/ppermute | solution.py:21
  37.0 12.2 %collective-permute-start.5 = (s32[1,544]{1,0:T(1,128)S(1)}, s32[1,544]{1,0:T(1,128)S(1)}, u32[]{:S(2)}, u32[]{:S(2)}) collective-permute-start(s32[1,544]{1,0:T(1,128)S(1)} %constant_dynamic-update-slice_fusion.refs_0_), channel_id=1, source_target_pairs={{0,1},{1,2},{2,3},{3,0},{4,5},{5,6},{6,7},{7,4},{8,9},{9,10},{10,1... | collective-permute-start | bytes 6536 | tf_op jit(solution)/shard_map/ppermute | solution.py:21
  37.6 21.1 %collective-permute-start = (f32[8,512]{1,0:T(8,128)S(1)}, f32[8,512]{1,0:T(8,128)S(1)}, u32[]{:S(2)}, u32[]{:S(2)}) collective-permute-start(f32[8,512]{1,0:T(8,128)S(1)} %get-tuple-element.33), channel_id=1, source_target_pairs={{0,252},{4,0},{8,4},{12,8},{16,12},{20,16},{24,20},{28,24},{32,28}... | collective-permute-start | bytes 49160 | tf_op jit(solution)/shard_map/ppermute | solution.py:21
  39.0 19.7 %collective-permute-start.1 = (f32[8,512]{1,0:T(8,128)S(1)}, f32[8,512]{1,0:T(8,128)S(1)}, u32[]{:S(2)}, u32[]{:S(2)}) collective-permute-start(f32[8,512]{1,0:T(8,128)S(1)} %get-tuple-element.32), channel_id=1, source_target_pairs={{0,248},{4,252},{8,0},{12,4},{16,8},{20,12},{24,16},{28,20},{32,24... | collective-permute-start | bytes 49160 | tf_op jit(solution)/shard_map/ppermute | solution.py:21
  43.9 15.2 %collective-permute-start.2 = (f32[8,512]{1,0:T(8,128)S(1)}, f32[8,512]{1,0:T(8,128)S(1)}, u32[]{:S(2)}, u32[]{:S(2)}) collective-permute-start(f32[8,512]{1,0:T(8,128)S(1)} %get-tuple-element.31), channel_id=1, source_target_pairs={{0,244},{4,248},{8,252},{12,0},{16,4},{20,8},{24,12},{28,16},{32,2... | collective-permute-start | bytes 49160 | tf_op jit(solution)/shard_map/ppermute | solution.py:21
  49.1 12.6 %copy-start.2 = (f32[2,512,128]{2,1,0:T(8,128)S(1)}, f32[2,512,128]{2,1,0:T(8,128)}, u32[]{:S(2)}) copy-start(f32[2,512,128]{2,1,0:T(8,128)} %get-tuple-element.17.count_col) | copy-start | bytes 1572868
  49.2 12.6 %copy-start.3 = (f32[2,8,512]{2,1,0:T(8,128)S(1)}, f32[2,8,512]{2,1,0:T(8,128)}, u32[]{:S(2)}) copy-start(f32[2,8,512]{2,1,0:T(8,128)} %get-tuple-element.16.count_row) | copy-start | bytes 98308
  76.0 45.3 %all-to-all-start.2 = ((f32[256,8,128]{2,1,0:T(8,128)}), f32[256,8,128]{2,1,0:T(8,128)S(1)}, u32[]{:S(2)}, u32[]{:S(2)}) async-start(f32[256,8,128]{2,1,0:T(8,128)} %bitcast.33), calls=%async_computation.2 | async-start | bytes 2097152 | tf_op jit(solution)/shard_map/all_to_all | solution.py:25
  85.1 51.1 %copy-start.1 = (f32[512,400]{0,1:T(8,128)S(1)}, f32[512,400]{0,1:T(8,128)}, u32[]{:S(2)}) copy-start(f32[512,400]{0,1:T(8,128)} %param.6) | copy-start | bytes 2457604
  85.1 51.1 %copy-start.4 = (f32[512]{0:T(512)S(1)}, f32[512]{0:T(512)}, u32[]{:S(2)}) copy-start(f32[512]{0:T(512)} %param.7) | copy-start | bytes 6148
  85.2 13.5 %collective-permute-start.6 = (f32[8,512]{1,0:T(8,128)S(1)}, f32[8,512]{1,0:T(8,128)S(1)}, u32[]{:S(2)}, u32[]{:S(2)}) collective-permute-start(f32[8,512]{1,0:T(8,128)S(1)} %get-tuple-element.29), channel_id=1, source_target_pairs={{0,4},{4,8},{8,12},{12,16},{16,20},{20,24},{24,28},{28,32},{32,36}... | collective-permute-start | bytes 49160 | tf_op jit(solution)/shard_map/ppermute | solution.py:21
  87.0 26.2 %collective-permute-start.7 = (f32[8,512]{1,0:T(8,128)S(1)}, f32[8,512]{1,0:T(8,128)S(1)}, u32[]{:S(2)}, u32[]{:S(2)}) collective-permute-start(f32[8,512]{1,0:T(8,128)S(1)} %get-tuple-element.28), channel_id=1, source_target_pairs={{0,8},{4,12},{8,16},{12,20},{16,24},{20,28},{24,32},{28,36},{32,40... | collective-permute-start | bytes 49160 | tf_op jit(solution)/shard_map/ppermute | solution.py:21
  88.5 26.3 %collective-permute-start.8 = (f32[8,512]{1,0:T(8,128)S(1)}, f32[8,512]{1,0:T(8,128)S(1)}, u32[]{:S(2)}, u32[]{:S(2)}) collective-permute-start(f32[8,512]{1,0:T(8,128)S(1)} %get-tuple-element.27), channel_id=1, source_target_pairs={{0,12},{4,16},{8,20},{12,24},{16,28},{20,32},{24,36},{28,40},{32,4... | collective-permute-start | bytes 49160 | tf_op jit(solution)/shard_map/ppermute | solution.py:21
  114.7 5.3 %collective-permute-start.10 = (f32[32,128]{1,0:T(8,128)S(1)}, f32[32,128]{1,0:T(8,128)S(1)}, u32[]{:S(2)}, u32[]{:S(2)}) collective-permute-start(f32[32,128]{1,0:T(8,128)S(1)} %get-tuple-element.24), channel_id=1, source_target_pairs={{0,2},{1,3},{2,0},{3,1},{4,6},{5,7},{6,4},{7,5},{8,10},{9,11},{10,... | collective-permute-start | bytes 49160 | tf_op jit(solution)/shard_map/ppermute | solution.py:21
  117.4 3.8 %collective-permute-start.11 = (f32[32,128]{1,0:T(8,128)S(1)}, f32[32,128]{1,0:T(8,128)S(1)}, u32[]{:S(2)}, u32[]{:S(2)}) collective-permute-start(f32[32,128]{1,0:T(8,128)S(1)} %get-tuple-element.23), channel_id=1, source_target_pairs={{0,1},{1,2},{2,3},{3,0},{4,5},{5,6},{6,7},{7,4},{8,9},{9,10},{10,1... | collective-permute-start | bytes 49160 | tf_op jit(solution)/shard_map/ppermute | solution.py:21
  117.7 3.5 %collective-permute-start.9 = (f32[32,128]{1,0:T(8,128)S(1)}, f32[32,128]{1,0:T(8,128)S(1)}, u32[]{:S(2)}, u32[]{:S(2)}) collective-permute-start(f32[32,128]{1,0:T(8,128)S(1)} %get-tuple-element.25), channel_id=1, source_target_pairs={{0,3},{1,0},{2,1},{3,2},{4,7},{5,4},{6,5},{7,6},{8,11},{9,8},{10,9... | collective-permute-start | bytes 49160 | tf_op jit(solution)/shard_map/ppermute | solution.py:21
  124.3 6.0 %collective-permute-start.12 = (f32[104,512]{1,0:T(8,128)S(1)}, f32[104,512]{1,0:T(8,128)S(1)}, u32[]{:S(2)}, u32[]{:S(2)}) collective-permute-start(f32[104,512]{1,0:T(8,128)S(1)} %owner.1.own), channel_id=1, source_target_pairs={{0,1},{1,2},{2,3},{3,0},{4,5},{5,6},{6,7},{7,4},{8,9},{9,10},{10,1... | collective-permute-start | bytes 638984 | tf_op jit(solution)/shard_map/ppermute | solution.py:21
  124.4 11.3 %collective-permute-start.13 = (f32[104,512]{1,0:T(8,128)S(1)}, f32[104,512]{1,0:T(8,128)S(1)}, u32[]{:S(2)}, u32[]{:S(2)}) collective-permute-start(f32[104,512]{1,0:T(8,128)S(1)} %owner.1.own), channel_id=1, source_target_pairs={{0,2},{1,3},{2,0},{3,1},{4,6},{5,7},{6,4},{7,5},{8,10},{9,11},{10,... | collective-permute-start | bytes 638984 | tf_op jit(solution)/shard_map/ppermute | solution.py:21
  128.2 8.0 %collective-permute-start.14 = (f32[104,512]{1,0:T(8,128)S(1)}, f32[104,512]{1,0:T(8,128)S(1)}, u32[]{:S(2)}, u32[]{:S(2)}) collective-permute-start(f32[104,512]{1,0:T(8,128)S(1)} %owner.1.own), channel_id=1, source_target_pairs={{0,3},{1,0},{2,1},{3,2},{4,7},{5,4},{6,5},{7,6},{8,11},{9,8},{10,9... | collective-permute-start | bytes 638984 | tf_op jit(solution)/shard_map/ppermute | solution.py:21

commit v3 on v2

--- a/solution.py
+++ b/solution.py
@@ -9,8 +9,9 @@
 HEAVY = 4
 LEARN_RATE = 0.1
 LANES = 128
-WIDTHS = (104, 104, 96, 96)
-STARTS = (0, 104, 208, 304)
+MAIN = 104
+SPARE = LANES - MAIN
+QUARTERS = 4
 f32 = jnp.float32
 bf16 = jnp.bfloat16
 
@@ -57,33 +58,37 @@
 
 
 def spread_body(columns, out):
-    rows = columns.shape[1]
-    for q, (start, w) in enumerate(zip(STARTS, WIDTHS)):
-        piece = columns[start : start + w, :]
-        if w < LANES:
-            piece = jnp.concatenate([piece, jnp.zeros((LANES - w, rows), f32)], axis=0)
-        out[:, q * LANES : (q + 1) * LANES] = piece.T
+    depth, rows = columns.shape
+    for c in range(out.shape[1] // LANES):
+        piece = columns[c * LANES : min((c + 1) * LANES, depth), :]
+        if piece.shape[0] < LANES:
+            piece = jnp.concatenate([piece, jnp.zeros((LANES - piece.shape[0], rows), f32)], axis=0)
+        out[:, c * LANES : (c + 1) * LANES] = piece.T
 
 
 def spread_rows(columns):
     return pl.pallas_call(
         spread_body,
         out_specs=VMEM,
-        out_shape=pltpu.VMEM((columns.shape[1], LANES * len(WIDTHS)), f32),
+        out_shape=pltpu.VMEM((columns.shape[1], LANES * QUARTERS), f32),
         compiler_params=room(16),
         name="spread",
     )(columns)
 
 
-def serve_body(ids, here, rows, heads, tails, picked, sems):
+def serve_body(ids, here, rows, heads, tails, picked, ends, sems):
     owners = ids.shape[0]
     parts = sems.shape[0]
     each = owners // parts
+    blocks = QUARTERS - 1
+    tall = 8 * blocks + 1
 
     def eight(w, carry):
         taken = [rows[pl.ds(ids[w, 0, k], 1), :] for k in range(8)]
         for k in range(8):
-            picked[pl.ds(w * 8 + k, 1), :] = taken[k]
+            for c in range(blocks):
+                picked[pl.ds(w * tall + 8 * c + k, 1), :] = taken[k][:, c * LANES : (c + 1) * LANES]
+            ends[pl.ds(w * 8 + k, 1), :] = taken[k][:, blocks * LANES :]
         return carry
 
     for reach in range(HEAVY):
@@ -93,7 +98,11 @@
     copies = []
     for part in range(parts):
         lax.fori_loop(part * each, (part + 1) * each, eight, 0, unroll=4)
-        span = pl.ds(part * each * 8, each * 8)
+        joined = ends[pl.ds(part * each * 8, each, stride=8), :]
+        for k in range(1, 8):
+            joined += pltpu.roll(ends[pl.ds(part * each * 8 + k, each, stride=8), :], 16 * k, 1)
+        picked[pl.ds(part * each * tall + tall - 1, each, stride=tall), :] = joined
+        span = pl.ds(part * each * tall, each * tall)
         copies.append(pltpu.make_async_copy(picked.at[span], heads.at[span], sems.at[part]))
         copies[-1].start()
     for copy in copies:
@@ -102,16 +111,18 @@
 
 def serve(ids, here, rows):
     width = rows.shape[1]
-    head_count = ids.shape[0] * 8
+    owners = ids.shape[0]
+    shape = (owners * (8 * (QUARTERS - 1) + 1), LANES)
     return pl.pallas_call(
         serve_body,
         in_specs=[SMEM, SMEM, VMEM],
         out_specs=[HBM, VMEM],
-        out_shape=[
-            pltpu.HBM((head_count, width), f32),
-            jax.ShapeDtypeStruct((HEAVY * 8, width), f32),
+        out_shape=[pltpu.HBM(shape, f32), jax.ShapeDtypeStruct((HEAVY * 8, width), f32)],
+        scratch_shapes=[
+            pltpu.VMEM(shape, f32),
+            pltpu.VMEM((owners * 8, LANES), f32),
+            pltpu.SemaphoreType.DMA((4,)),
         ],
-        scratch_shapes=[pltpu.VMEM((head_count, width), f32), pltpu.SemaphoreType.DMA((4,))],
         compiler_params=room(16),
         name="serve",
     )(ids, here, near(rows))
@@ -158,12 +169,29 @@
     )(slots, negs)
 
 
+def lanes_of(shape):
+    return lax.broadcasted_iota(jnp.int32, shape, 1)
+
+
+def leftover(blocks):
+    lane = lanes_of(blocks[0].shape)
+    out = jnp.zeros(blocks[0].shape, f32)
+    for c, block in enumerate(blocks):
+        at = SPARE * c
+        wide = SPARE if c < QUARTERS - 1 else 16
+        moved = pltpu.roll(block, (at - (MAIN if c < QUARTERS - 1 else 0)) % LANES, 1)
+        out = jnp.where((lane >= at) & (lane < at + wide), moved, out)
+    return out
+
+
 def grads_body(heads, tails, by_edge, by_slot, count_row, count_col, ahead, out_heads, out_tails,
-               high, low, d_high, d_low, edge_part, slot_part, summed, in_sems, out_sems):
-    head_count = heads.shape[0]
-    live = head_count + tails.shape[0]
+               high, low, d_high, d_low, edge_part, slot_part, summed, packed, in_sems, out_sems):
+    live = by_slot.shape[0]
+    head_count = live - tails.shape[0]
+    owners = head_count // 8
+    tall = heads.shape[0] // owners
     padded = by_edge.shape[1]
-    width = heads.shape[1]
+    width = tails.shape[1]
     batches, _, edges = count_row.shape
     loads = []
     for p in range(2 * batches):
@@ -172,7 +200,17 @@
         loads[-1].start()
     last = pltpu.make_async_copy(by_slot, slot_part, in_sems.at[2 * batches])
     last.start()
-    high[:head_count, :], low[:head_count, :] = halves(heads[...])
+    ends = heads[pl.ds(tall - 1, owners, stride=tall), :]
+    for k in range(8):
+        span = slice(k * owners, (k + 1) * owners)
+        for c in range(QUARTERS):
+            lanes = slice(c * LANES, (c + 1) * LANES)
+            if c < QUARTERS - 1:
+                block = heads[pl.ds(8 * c + k, owners, stride=tall), :]
+            else:
+                block = pltpu.roll(ends, (LANES - 16 * k) % LANES, 1) if k else ends
+                block = jnp.where(lanes_of(block.shape) < 16, block, 0.0)
+            high[span, lanes], low[span, lanes] = halves(block)
     high[head_count:live, :], low[head_count:live, :] = halves(tails[...])
     high[live:, :] = jnp.zeros((padded - live, width), bf16)
     low[live:, :] = jnp.zeros((padded - live, width), bf16)
@@ -206,25 +244,37 @@
     last.wait()
     stores = []
     block = 2 * LANES
+    short = 7 * owners
     for h in range(width // block):
         span = slice(h * block, (h + 1) * block)
-        part = mm(slot_part[...], d_high[:, span]) + mm(slot_part[...], d_low[:, span])
-        for q in range(2):
-            summed[2 * h + q] = part[:head_count, q * LANES : (q + 1) * LANES]
-        out_tails[:, span] = part[head_count:, :]
-        stores.append(
-            pltpu.make_async_copy(summed.at[pl.ds(2 * h, 2)], out_heads.at[pl.ds(2 * h, 2)], out_sems.at[h])
-        )
+        summed[:, span] = mm(slot_part[...], d_high[:, span]) + mm(slot_part[...], d_low[:, span])
+        for q in (2 * h, 2 * h + 1):
+
+            def quarter(at, size):
+                if q < QUARTERS - 1:
+                    return summed[at : at + size, q * LANES : (q + 1) * LANES]
+                return leftover([summed[at : at + size, c * LANES : (c + 1) * LANES] for c in range(QUARTERS)])
+
+            eighth = quarter(7 * owners, owners)
+            for k in range(7):
+                value = quarter(k * owners, owners)
+                if SPARE * k < MAIN:
+                    moved = pltpu.roll(eighth, (MAIN - SPARE * k) % LANES, 1)
+                    value = jnp.where(lanes_of(value.shape) < MAIN, value, moved)
+                packed[pl.ds(q * short + k, owners, stride=7), :] = value
+            out_tails[:, q * LANES : (q + 1) * LANES] = quarter(head_count, live - head_count)
+        part = pl.ds(2 * h * short, 2 * short)
+        stores.append(pltpu.make_async_copy(packed.at[part], out_heads.at[part], out_sems.at[h]))
         stores[-1].start()
     for store in stores:
         store.wait()
 
 
 def grads(heads, tails, by_edge, by_slot, count_row, count_col, ahead):
-    head_count, width = heads.shape
-    padded = by_edge.shape[1]
-    total = by_edge.shape[0]
-    shape = (width // LANES, head_count, LANES)
+    width = tails.shape[1]
+    total, padded = by_edge.shape
+    live = by_slot.shape[0]
+    shape = (QUARTERS * 7 * (live - tails.shape[0]) // 8, LANES)
     return pl.pallas_call(
         grads_body,
         in_specs=[VMEM, VMEM, HBM, HBM, VMEM, VMEM, HBM],
@@ -237,6 +287,7 @@
             pltpu.VMEM((total, width), bf16),
             pltpu.VMEM(by_edge.shape, bf16),
             pltpu.VMEM(by_slot.shape, bf16),
+            pltpu.VMEM((live, width), f32),
             pltpu.VMEM(shape, f32),
             pltpu.SemaphoreType.DMA((2 * count_row.shape[0] + 1,)),
             pltpu.SemaphoreType.DMA((width // LANES // 2,)),
@@ -274,17 +325,26 @@
 
 
 def owner_body(back, tails, hot, out, spots, sems):
-    count = back.shape[0]
     parts = sems.shape[0] - 1
-    each = count // parts
-    spans = [(p * each, each) for p in range(parts)] + [(count, tails.shape[0])]
+    short = back.shape[0] // parts
+    each = short // 7 * 8
+    owners = short // 7
+    spans = [(p * each, each) for p in range(parts)] + [(parts * each, tails.shape[0])]
     loads = []
     for p, (at, size) in enumerate(spans):
         loads.append(pltpu.make_async_copy(hot.at[:, pl.ds(at, size)], spots.at[:, pl.ds(at, size)], sems.at[p]))
         loads[-1].start()
     summed = jnp.zeros((hot.shape[0], LANES), f32)
     for p, (at, size) in enumerate(spans):
-        values = back[at : at + size, :] if p < parts else tails[...]
+        if p < parts:
+            eighth = jnp.zeros((owners, LANES), f32)
+            lane = lanes_of(eighth.shape)
+            for k in range(-(-MAIN // SPARE)):
+                moved = pltpu.roll(back[pl.ds(p * short + k, owners, stride=7), :], (SPARE * k - MAIN) % LANES, 1)
+                eighth = jnp.where((lane >= SPARE * k) & (lane < SPARE * (k + 1)), moved, eighth)
+            values = jnp.concatenate([back[p * short : (p + 1) * short, :], eighth], axis=0)
+        else:
+            values = tails[...]
         both = jnp.concatenate(halves(values), axis=1)
         loads[p].wait()
         part = mm(spots[:, at : at + size], both)
@@ -297,7 +357,7 @@
         owner_body,
         in_specs=[VMEM, VMEM, HBM],
         out_specs=VMEM,
-        out_shape=jax.ShapeDtypeStruct((max(WIDTHS), hot.shape[0]), f32),
+        out_shape=jax.ShapeDtypeStruct((MAIN, hot.shape[0]), f32),
         scratch_shapes=[pltpu.VMEM(hot.shape, bf16), pltpu.SemaphoreType.DMA((5,))],
         compiler_params=room(16),
         name="owner",
@@ -308,16 +368,26 @@
     for s, piece in enumerate((own, next1, next2, next3)):
         quarters[(me[0] + 4 - s) % 4] = piece[...]
     squares = jnp.zeros(sums.shape, f32)
-    for q in range(len(WIDTHS)):
+    for q in range(QUARTERS):
         squares += jnp.sum(quarters[q] * quarters[q], axis=0, keepdims=True)
     fresh = sums[...] + squares * (1.0 / rows.shape[0])
     new_sums[...] = fresh
     scale = LEARN_RATE / jnp.sqrt(fresh)
+    depth = rows.shape[0]
     stores = []
-    for q, (start, w) in enumerate(zip(STARTS, WIDTHS)):
-        fresh_rows[start : start + w, :] = rows[start : start + w, :] - quarters[q, :w, :] * scale
-        span = pl.ds(start, w)
-        stores.append(pltpu.make_async_copy(fresh_rows.at[span], new_rows.at[span], sems.at[q]))
+    for c in range(QUARTERS - 1):
+        at = c * LANES
+        end = at + LANES
+        wide = SPARE
+        if c == QUARTERS - 2:
+            end = depth
+            wide = depth - at - MAIN
+        main = slice(at, at + MAIN)
+        rest = slice(at + MAIN, end)
+        fresh_rows[main, :] = rows[main, :] - quarters[c] * scale
+        fresh_rows[rest, :] = rows[rest, :] - quarters[QUARTERS - 1, SPARE * c : SPARE * c + wide, :] * scale
+        span = pl.ds(at, end - at)
+        stores.append(pltpu.make_async_copy(fresh_rows.at[span], new_rows.at[span], sems.at[c]))
         stores[-1].start()
     for store in stores:
         store.wait()
@@ -345,7 +415,7 @@
 def compact(slots, here, owners, capacity):
     half = capacity // 2
     who, k = slots // capacity, slots % capacity
-    return jnp.where(k < half, who * half + k, owners * half + (who - here) % owners * half + k - half)
+    return jnp.where(k < half, k * owners + who, owners * half + (who - here) % owners * half + k - half)
 
 
 def local(embedding, adagrad_sum, row_lists, source_slots, target_slots, negative_ids):
@@ -371,12 +441,13 @@
     tails = jnp.concatenate(
         [tails[0]] + [passed_along(tails[r], "dom", -r) for r in range(1, HEAVY)], axis=0
     )
-    heads = exchanged(heads.reshape(owners, half, -1), "dom").reshape(owners * half, -1)
+    heads = exchanged(heads.reshape(owners, -1, 1, LANES), "dom").reshape(-1, LANES)
     me = lax.axis_index("rep")
     mine = me.reshape(1).astype(jnp.int32)
     askers = jnp.arange(owners)[None, :] == ((here - jnp.arange(HEAVY)) % owners)[:, None]
     tail_ids = jnp.sum(jnp.where(askers[:, :, None], incoming[None, :, half:], 0), axis=1)
-    ids = jnp.concatenate([incoming[:, :half].reshape(1, -1), tail_ids.reshape(1, -1)], axis=1)
+    ids = [incoming[:, : half - 1], incoming[:, half - 1], tail_ids]
+    ids = jnp.concatenate([part.reshape(1, -1) for part in ids], axis=1)
     listed = [ids] + [passed_along(ids, "rep", -s) for s in range(1, groups)]
     hot = hot_rows(mine, listed, rows)
 
@@ -393,9 +464,9 @@
     tail_back = jnp.concatenate(
         [wanted[0]] + [passed_along(wanted[s], "rep", -s) for s in range(1, groups)], axis=0
     )
-    back = exchanged(head_grads.reshape(groups * owners, half, LANES), ("rep", "dom"))
+    back = exchanged(head_grads.reshape(groups * owners, half - 1, 1, LANES), ("rep", "dom"))
     quarter = owner(back.reshape(-1, LANES), tail_back, hot)
-    pieces = [quarter] + [passed_along(quarter, "rep", s) for s in range(1, len(WIDTHS))]
+    pieces = [quarter] + [passed_along(quarter, "rep", s) for s in range(1, groups)]
     new_rows, new_sums = update(mine, pieces, columns, adagrad_sum.reshape(1, -1))
     return new_rows.T, new_sums.reshape(-1)
 

time: 139 us -> 131 us (0.942)
  waiting for transfers between devices: 51.9 us -> 44.1 us
    ppermute x15, waiting for transfers between devices: 41.5 us -> 33.7 us  [passed_along(): return lax.ppermute(value, axis, pairs)]
  transfers between devices with their start and end apart: 18 -> 18, of which waited for: 11 -> 11; matrix products, arithmetic and copies ran while one was open for 1% -> 1% of each run, Pallas kernels for 4% -> 5%
where the time goes in v3:
time: 131 us; the launch traced here: 130 us
  starting transfers between devices  52.7 us (40%)
  waiting for transfers between devices  44.1 us (34%)
  Pallas kernels  28.7 us (22%)
  local copies, waits for them, and re-layouts  3.17 us (2%)
    ppermute x15, waiting for transfers between devices, passed_along(): return lax.ppermute(value, axis, pairs)  33.7 us
    all_to_all x3, starting transfers between devices, exchanged(): return lax.all_to_all(value, axis, 0, 0, tiled=True)  27 us
    ppermute x15, starting transfers between devices, passed_along(): return lax.ppermute(value, axis, pairs)  25.7 us
    pallas_call x1, Pallas kernels, grads(): pl.pallas_call(grads_body, in_specs=[VMEM, VMEM, HBM, HBM, VMEM, VMEM, HB...  14.4 us
    all_to_all x3, waiting for transfers between devices, exchanged(): return lax.all_to_all(value, axis, 0, 0, tiled=True)  10.4 us
    pallas_call x1, Pallas kernels, serve(): pl.pallas_call(serve_body, in_specs=[SMEM, SMEM, VMEM], out_specs=[HBM, V...  3.48 us
    pallas_call x1, Pallas kernels, prep(): pl.pallas_call(prep_body, out_shape=[pltpu.HBM((total, padded), bf16), pl...  3.35 us
    pallas_call x1, Pallas kernels, owner(): pl.pallas_call(owner_body, in_specs=[VMEM, VMEM, HBM], out_specs=VMEM, ou...  3.08 us
  transfers between devices with their start and end apart: 18, of which 11 were waited for; matrix products, arithmetic and copies ran while one was open for 1% of the time, Pallas kernels for 5%

profile of v3, /device:TPU:1, one launch (start us, length us, event | category | flops | bytes accessed | tf_op | source)
XLA Modules:
  0.0 130.1 jit_solution(12933205362176261491)
XLA Ops:
  0.6 1.4 %copy.16 = s32[1,1,64,16]{3,2,1,0:T(8,128)} copy(s32[1,1,64,16]{2,3,1,0:T(8,128)} %param.8) | data formatting | bytes 8192 | tf_op args[2]
  2.0 13.1 %all-to-all-start = ((s32[64,1,16]{2,1,0:T(1,128)}), s32[64,1,16]{2,1,0:T(1,128)S(1)}, u32[]{:S(2)}, u32[]{:S(2)}) async-start(s32[64,1,16]{2,1,0:T(1,128)} %bitcast.1), calls=%async_computation | async-start | bytes 65536 | tf_op jit(solution)/shard_map/all_to_all | solution.py:26
  15.2 0.0 copy-start
  15.2 1.1 copy-done
  16.3 0.3 spread.1.rows
  16.7 7.7 %all-to-all-done.ids = s32[64,1,16]{2,1,0:T(1,128)S(1)} async-done(((s32[64,1,16]{2,1,0:T(1,128)}), s32[64,1,16]{2,1,0:T(1,128)S(1)}, u32[]{:S(2)}, u32[]{:S(2)}) %all-to-all-start) | async-done | bytes 4128 | tf_op jit(solution)/shard_map/all_to_all | solution.py:26
  24.4 3.5 %serve.1 = (f32[1600,128]{1,0:T(8,128)}, f32[32,512]{1,0:T(8,128)S(1)}) custom-call(s32[64,1,16]{2,1,0:T(1,128)S(1)} %all-to-all-done.ids, s32[1]{0:T(128)} %bitcast.2.here, f32[512,512]{1,0:T(8,128)S(1)} %spread.1.rows), custom_call_target="tpu_custom_call" | custom-call | tf_op jit(solution)/shard_map/serve/pallas_call | solution.py:116
  27.9 4.8 %all-to-all-start.1 = ((f32[64,25,1,128]{3,2,1,0:T(1,128)}), f32[64,25,1,128]{3,2,1,0:T(1,128)S(1)}, u32[]{:S(2)}, u32[]{:S(2)}) async-start(f32[64,25,1,128]{3,2,1,0:T(1,128)} %bitcast.38), calls=%async_computation.1 | async-start | bytes 1638400 | tf_op jit(solution)/shard_map/all_to_all | solution.py:26
  32.8 0.1 iota_compare_fusion
  32.8 0.1 slice.54
  32.9 0.1 copy.19
  33.0 0.2 select_reduce_fusion
  33.1 0.1 reshape.323
  33.2 0.1 reshape.322
  33.4 0.2 slice_reduce_fusion
  33.5 0.1 pad_add_fusion.1.refs_0_
  33.6 2.5 %collective-permute-start.3 = (s32[1,544]{1,0:T(1,128)S(1)}, s32[1,544]{1,0:T(1,128)S(1)}, u32[]{:S(2)}, u32[]{:S(2)}) collective-permute-start(s32[1,544]{1,0:T(1,128)S(1)} %pad_add_fusion.1.refs_0_), channel_id=1, source_target_pairs={{0,3},{1,0},{2,1},{3,2},{4,7},{5,4},{6,5},{7,6},{8,11},{9,8},{10,9... | collective-permute-start | bytes 6536 | tf_op jit(solution)/shard_map/ppermute | solution.py:22
  36.1 0.5 collective-permute-start.4
  36.6 0.6 collective-permute-start.5
  37.2 1.4 %collective-permute-start = (f32[8,512]{1,0:T(8,128)S(1)}, f32[8,512]{1,0:T(8,128)S(1)}, u32[]{:S(2)}, u32[]{:S(2)}) collective-permute-start(f32[8,512]{1,0:T(8,128)S(1)} %get-tuple-element.33), channel_id=1, source_target_pairs={{0,252},{4,0},{8,4},{12,8},{16,12},{20,16},{24,20},{28,24},{32,28}... | collective-permute-start | bytes 49160 | tf_op jit(solution)/shard_map/ppermute | solution.py:22
  38.7 4.9 %collective-permute-start.1 = (f32[8,512]{1,0:T(8,128)S(1)}, f32[8,512]{1,0:T(8,128)S(1)}, u32[]{:S(2)}, u32[]{:S(2)}) collective-permute-start(f32[8,512]{1,0:T(8,128)S(1)} %get-tuple-element.32), channel_id=1, source_target_pairs={{0,248},{4,252},{8,0},{12,4},{16,8},{20,12},{24,16},{28,20},{32,24... | collective-permute-start | bytes 49160 | tf_op jit(solution)/shard_map/ppermute | solution.py:22
  43.6 1.7 %collective-permute-start.2 = (f32[8,512]{1,0:T(8,128)S(1)}, f32[8,512]{1,0:T(8,128)S(1)}, u32[]{:S(2)}, u32[]{:S(2)}) collective-permute-start(f32[8,512]{1,0:T(8,128)S(1)} %get-tuple-element.31), channel_id=1, source_target_pairs={{0,244},{4,248},{8,252},{12,0},{16,4},{20,8},{24,12},{28,16},{32,2... | collective-permute-start | bytes 49160 | tf_op jit(solution)/shard_map/ppermute | solution.py:22
  45.2 0.1 compare_select_fusion.2.slots
  45.4 3.4 %prep.1 = (bf16[2048,640]{1,0:T(8,128)(2,1)}, bf16[544,2048]{1,0:T(8,128)(2,1)}, f32[2,8,512]{2,1,0:T(8,128)}, f32[2,512,128]{2,1,0:T(8,128)}) custom-call(s32[1,2048]{1,0:T(1,128)S(1)} %compare_select_fusion.2.slots, s32[1,2048]{1,0:T(1,128)S(1)} %reshape_squeeze.10.negs), custom_call_target="tpu_custom_call" | custom-call | tf_op jit(solution)/shard_map/prep/pallas_call | solution.py:159
  48.8 2.3 %hot.1.ahead = bf16[512,2176]{1,0:T(8,128)(2,1)} custom-call(s32[1]{0:T(128)} %bitcast.me, s32[1,544]{1,0:T(1,128)S(1)} %pad_add_fusion.1.refs_0_, s32[1,544]{1,0:T(1,128)S(1)} %collective-permute-done.3.refs_1_, s32[1,544]{1,0:T(1,128)S(1)} %collective-permute-done.4.refs_2_, s32[1,544]{1,0:T(1,128)S(1)} %collective-permute-done.5.refs_3_), custom_call_target="tpu_custom_call" | custom-call | tf_op jit(solution)/shard_map/hot/pallas_call | solution.py:318
  51.1 2.1 %collective-permute-done = f32[8,512]{1,0:T(8,128)S(1)} collective-permute-done((f32[8,512]{1,0:T(8,128)S(1)}, f32[8,512]{1,0:T(8,128)S(1)}, u32[]{:S(2)}, u32[]{:S(2)}) %collective-permute-start) | collective-permute-done | bytes 16416 | tf_op jit(solution)/shard_map/ppermute | solution.py:22
  53.2 0.6 collective-permute-done.2
  53.8 2.6 %all-to-all-done.1 = f32[64,25,1,128]{3,2,1,0:T(1,128)S(1)} async-done(((f32[64,25,1,128]{3,2,1,0:T(1,128)}), f32[64,25,1,128]{3,2,1,0:T(1,128)S(1)}, u32[]{:S(2)}, u32[]{:S(2)}) %all-to-all-start.1) | async-done | bytes 819232 | tf_op jit(solution)/shard_map/all_to_all | solution.py:26
  56.4 14.4 %grads.1 = (f32[1792,128]{1,0:T(8,128)}, f32[32,512]{1,0:T(8,128)S(1)}) custom-call(f32[1600,128]{1,0:T(8,128)S(1)} %bitcast.30, f32[32,512]{1,0:T(8,128)S(1)} %pad_maximum_fusion.tails, bf16[2048,640]{1,0:T(8,128)(2,1)} %get-tuple-element.14.by_edge, bf16[544,2048]{1,0:T(8,128)(2,1)} %get-tuple-element.15.by_slot, f32[2,8,512]{2,1,0:T(8,128)S(1)} %copy-done.3, ...), custom_call_target="tpu_custom_call" | custom-call | tf_op jit(solution)/shard_map/grads/pallas_call | solution.py:278
  70.8 9.1 %all-to-all-start.2 = ((f32[256,7,1,128]{3,2,1,0:T(1,128)}), f32[256,7,1,128]{3,2,1,0:T(1,128)S(1)}, u32[]{:S(2)}, u32[]{:S(2)}) async-start(f32[256,7,1,128]{3,2,1,0:T(1,128)} %bitcast.37), calls=%async_computation.2 | async-start | bytes 1835008 | tf_op jit(solution)/shard_map/all_to_all | solution.py:26
  79.9 0.0 copy-start.1
  80.0 1.8 %collective-permute-start.6 = (f32[8,512]{1,0:T(8,128)S(1)}, f32[8,512]{1,0:T(8,128)S(1)}, u32[]{:S(2)}, u32[]{:S(2)}) collective-permute-start(f32[8,512]{1,0:T(8,128)S(1)} %get-tuple-element.29), channel_id=1, source_target_pairs={{0,4},{4,8},{8,12},{12,16},{16,20},{20,24},{24,28},{28,32},{32,36}... | collective-permute-start | bytes 49160 | tf_op jit(solution)/shard_map/ppermute | solution.py:22
  81.8 1.5 %collective-permute-start.7 = (f32[8,512]{1,0:T(8,128)S(1)}, f32[8,512]{1,0:T(8,128)S(1)}, u32[]{:S(2)}, u32[]{:S(2)}) collective-permute-start(f32[8,512]{1,0:T(8,128)S(1)} %get-tuple-element.28), channel_id=1, source_target_pairs={{0,8},{4,12},{8,16},{12,20},{16,24},{20,28},{24,32},{28,36},{32,40... | collective-permute-start | bytes 49160 | tf_op jit(solution)/shard_map/ppermute | solution.py:22
  83.3 1.6 %collective-permute-start.8 = (f32[8,512]{1,0:T(8,128)S(1)}, f32[8,512]{1,0:T(8,128)S(1)}, u32[]{:S(2)}, u32[]{:S(2)}) collective-permute-start(f32[8,512]{1,0:T(8,128)S(1)} %get-tuple-element.27), channel_id=1, source_target_pairs={{0,12},{4,16},{8,20},{12,24},{16,28},{20,32},{24,36},{28,40},{32,4... | collective-permute-start | bytes 49160 | tf_op jit(solution)/shard_map/ppermute | solution.py:22
  84.8 5.9 %collective-permute-done.6 = f32[8,512]{1,0:T(8,128)S(1)} collective-permute-done((f32[8,512]{1,0:T(8,128)S(1)}, f32[8,512]{1,0:T(8,128)S(1)}, u32[]{:S(2)}, u32[]{:S(2)}) %collective-permute-start.6) | collective-permute-done | bytes 16416 | tf_op jit(solution)/shard_map/ppermute | solution.py:22
  90.7 14.4 %collective-permute-done.7 = f32[8,512]{1,0:T(8,128)S(1)} collective-permute-done((f32[8,512]{1,0:T(8,128)S(1)}, f32[8,512]{1,0:T(8,128)S(1)}, u32[]{:S(2)}, u32[]{:S(2)}) %collective-permute-start.7) | collective-permute-done | bytes 16416 | tf_op jit(solution)/shard_map/ppermute | solution.py:22
  105.1 1.6 %collective-permute-done.8 = f32[8,512]{1,0:T(8,128)S(1)} collective-permute-done((f32[8,512]{1,0:T(8,128)S(1)}, f32[8,512]{1,0:T(8,128)S(1)}, u32[]{:S(2)}, u32[]{:S(2)}) %collective-permute-start.8) | collective-permute-done | bytes 16416 | tf_op jit(solution)/shard_map/ppermute | solution.py:22
  106.7 2.6 %collective-permute-start.10 = (f32[32,128]{1,0:T(8,128)S(1)}, f32[32,128]{1,0:T(8,128)S(1)}, u32[]{:S(2)}, u32[]{:S(2)}) collective-permute-start(f32[32,128]{1,0:T(8,128)S(1)} %get-tuple-element.24), channel_id=1, source_target_pairs={{0,2},{1,3},{2,0},{3,1},{4,6},{5,7},{6,4},{7,5},{8,10},{9,11},{10,... | collective-permute-start | bytes 49160 | tf_op jit(solution)/shard_map/ppermute | solution.py:22
  109.3 0.5 collective-permute-start.11
  109.8 2.2 %collective-permute-start.9 = (f32[32,128]{1,0:T(8,128)S(1)}, f32[32,128]{1,0:T(8,128)S(1)}, u32[]{:S(2)}, u32[]{:S(2)}) collective-permute-start(f32[32,128]{1,0:T(8,128)S(1)} %get-tuple-element.25), channel_id=1, source_target_pairs={{0,3},{1,0},{2,1},{3,2},{4,7},{5,4},{6,5},{7,6},{8,11},{9,8},{10,9... | collective-permute-start | bytes 49160 | tf_op jit(solution)/shard_map/ppermute | solution.py:22
  112.0 1.1 collective-permute-done.11
  113.2 3.1 %owner.1.own = f32[104,512]{1,0:T(8,128)S(1)} custom-call(f32[1792,128]{1,0:T(8,128)S(1)} %bitcast.29, f32[128,128]{1,0:T(8,128)S(1)} %pad_maximum_fusion.2.tails, bf16[512,2176]{1,0:T(8,128)(2,1)} %hot.1.ahead), custom_call_target="tpu_custom_call" | custom-call | tf_op jit(solution)/shard_map/owner/pallas_call | solution.py:356
  116.3 0.1 collective-permute-start.12
  116.3 3.8 %collective-permute-start.13 = (f32[104,512]{1,0:T(8,128)S(1)}, f32[104,512]{1,0:T(8,128)S(1)}, u32[]{:S(2)}, u32[]{:S(2)}) collective-permute-start(f32[104,512]{1,0:T(8,128)S(1)} %owner.1.own), channel_id=1, source_target_pairs={{0,2},{1,3},{2,0},{3,1},{4,6},{5,7},{6,4},{7,5},{8,10},{9,11},{10,... | collective-permute-start | bytes 638984 | tf_op jit(solution)/shard_map/ppermute | solution.py:22
  120.2 2.1 %collective-permute-done.12.next1 = f32[104,512]{1,0:T(8,128)S(1)} collective-permute-done((f32[104,512]{1,0:T(8,128)S(1)}, f32[104,512]{1,0:T(8,128)S(1)}, u32[]{:S(2)}, u32[]{:S(2)}) %collective-permute-start.12) | collective-permute-done | bytes 213024 | tf_op jit(solution)/shard_map/ppermute | solution.py:22
  122.2 5.5 %collective-permute-done.13.next2 = f32[104,512]{1,0:T(8,128)S(1)} collective-permute-done((f32[104,512]{1,0:T(8,128)S(1)}, f32[104,512]{1,0:T(8,128)S(1)}, u32[]{:S(2)}, u32[]{:S(2)}) %collective-permute-start.13) | collective-permute-done | bytes 213024 | tf_op jit(solution)/shard_map/ppermute | solution.py:22
  127.7 0.5 collective-permute-done.14.next3
  128.2 1.7 %update.1 = (f32[400,512]{1,0:T(8,128)}, f32[1,512]{1,0:T(1,128)}) custom-call(s32[1]{0:T(128)} %bitcast.me, f32[104,512]{1,0:T(8,128)S(1)} %owner.1.own, f32[104,512]{1,0:T(8,128)S(1)} %collective-permute-done.12.next1, f32[104,512]{1,0:T(8,128)S(1)} %collective-permute-done.13.next2, f32[104,512]{1,0:T(8,128)S(1)} %collective-permute-done.14.next3, ...), custom_call_target="tpu_custom_call" | custom-call | tf_op jit(solution)/shard_map/update/pallas_call | solution.py:397
  (32 shorter events, 0.1 us)
Async XLA Ops:
  2.0 22.4 %all-to-all-start = ((s32[64,1,16]{2,1,0:T(1,128)}), s32[64,1,16]{2,1,0:T(1,128)S(1)}, u32[]{:S(2)}, u32[]{:S(2)}) async-start(s32[64,1,16]{2,1,0:T(1,128)} %bitcast.1), calls=%async_computation | async-start | bytes 65536 | tf_op jit(solution)/shard_map/all_to_all | solution.py:26
  15.2 1.1 copy-start
  16.3 16.3 %copy-start.6 = (s32[1,1,2,512]{3,2,1,0:T(2,128)S(1)}, s32[1,1,2,512]{3,2,1,0:T(2,128)}, u32[]{:S(2)}) copy-start(s32[1,1,2,512]{3,2,1,0:T(2,128)} %param.10) | copy-start | bytes 12292
  16.3 16.3 %copy-start.7 = (s32[1,1,2,512]{3,2,1,0:T(2,128)S(1)}, s32[1,1,2,512]{3,2,1,0:T(2,128)}, u32[]{:S(2)}) copy-start(s32[1,1,2,512]{3,2,1,0:T(2,128)} %param.9) | copy-start | bytes 12292
  16.3 29.0 %copy-start.5 = (s32[1,1,2,2,512]{4,3,2,1,0:T(2,128)S(1)}, s32[1,1,2,2,512]{4,3,2,1,0:T(2,128)}, u32[]{:S(2)}) copy-start(s32[1,1,2,2,512]{4,3,2,1,0:T(2,128)} %param.11) | copy-start | bytes 24580
  27.9 28.5 %all-to-all-start.1 = ((f32[64,25,1,128]{3,2,1,0:T(1,128)}), f32[64,25,1,128]{3,2,1,0:T(1,128)S(1)}, u32[]{:S(2)}, u32[]{:S(2)}) async-start(f32[64,25,1,128]{3,2,1,0:T(1,128)} %bitcast.38), calls=%async_computation.1 | async-start | bytes 1638400 | tf_op jit(solution)/shard_map/all_to_all | solution.py:26
  33.6 10.0 %collective-permute-start.3 = (s32[1,544]{1,0:T(1,128)S(1)}, s32[1,544]{1,0:T(1,128)S(1)}, u32[]{:S(2)}, u32[]{:S(2)}) collective-permute-start(s32[1,544]{1,0:T(1,128)S(1)} %pad_add_fusion.1.refs_0_), channel_id=1, source_target_pairs={{0,3},{1,0},{2,1},{3,2},{4,7},{5,4},{6,5},{7,6},{8,11},{9,8},{10,9... | collective-permute-start | bytes 6536 | tf_op jit(solution)/shard_map/ppermute | solution.py:22
  36.1 12.6 %collective-permute-start.4 = (s32[1,544]{1,0:T(1,128)S(1)}, s32[1,544]{1,0:T(1,128)S(1)}, u32[]{:S(2)}, u32[]{:S(2)}) collective-permute-start(s32[1,544]{1,0:T(1,128)S(1)} %pad_add_fusion.1.refs_0_), channel_id=1, source_target_pairs={{0,2},{1,3},{2,0},{3,1},{4,6},{5,7},{6,4},{7,5},{8,10},{9,11},{10,... | collective-permute-start | bytes 6536 | tf_op jit(solution)/shard_map/ppermute | solution.py:22
  36.6 12.1 %collective-permute-start.5 = (s32[1,544]{1,0:T(1,128)S(1)}, s32[1,544]{1,0:T(1,128)S(1)}, u32[]{:S(2)}, u32[]{:S(2)}) collective-permute-start(s32[1,544]{1,0:T(1,128)S(1)} %pad_add_fusion.1.refs_0_), channel_id=1, source_target_pairs={{0,1},{1,2},{2,3},{3,0},{4,5},{5,6},{6,7},{7,4},{8,9},{9,10},{10,1... | collective-permute-start | bytes 6536 | tf_op jit(solution)/shard_map/ppermute | solution.py:22
  37.2 16.0 %collective-permute-start = (f32[8,512]{1,0:T(8,128)S(1)}, f32[8,512]{1,0:T(8,128)S(1)}, u32[]{:S(2)}, u32[]{:S(2)}) collective-permute-start(f32[8,512]{1,0:T(8,128)S(1)} %get-tuple-element.33), channel_id=1, source_target_pairs={{0,252},{4,0},{8,4},{12,8},{16,12},{20,16},{24,20},{28,24},{32,28}... | collective-permute-start | bytes 49160 | tf_op jit(solution)/shard_map/ppermute | solution.py:22
  38.7 14.5 %collective-permute-start.1 = (f32[8,512]{1,0:T(8,128)S(1)}, f32[8,512]{1,0:T(8,128)S(1)}, u32[]{:S(2)}, u32[]{:S(2)}) collective-permute-start(f32[8,512]{1,0:T(8,128)S(1)} %get-tuple-element.32), channel_id=1, source_target_pairs={{0,248},{4,252},{8,0},{12,4},{16,8},{20,12},{24,16},{28,20},{32,24... | collective-permute-start | bytes 49160 | tf_op jit(solution)/shard_map/ppermute | solution.py:22
  43.6 10.2 %collective-permute-start.2 = (f32[8,512]{1,0:T(8,128)S(1)}, f32[8,512]{1,0:T(8,128)S(1)}, u32[]{:S(2)}, u32[]{:S(2)}) collective-permute-start(f32[8,512]{1,0:T(8,128)S(1)} %get-tuple-element.31), channel_id=1, source_target_pairs={{0,244},{4,248},{8,252},{12,0},{16,4},{20,8},{24,12},{28,16},{32,2... | collective-permute-start | bytes 49160 | tf_op jit(solution)/shard_map/ppermute | solution.py:22
  48.7 7.6 %copy-start.2 = (f32[2,512,128]{2,1,0:T(8,128)S(1)}, f32[2,512,128]{2,1,0:T(8,128)}, u32[]{:S(2)}) copy-start(f32[2,512,128]{2,1,0:T(8,128)} %get-tuple-element.17.count_col) | copy-start | bytes 1572868
  48.7 7.6 %copy-start.3 = (f32[2,8,512]{2,1,0:T(8,128)S(1)}, f32[2,8,512]{2,1,0:T(8,128)}, u32[]{:S(2)}) copy-start(f32[2,8,512]{2,1,0:T(8,128)} %get-tuple-element.16.count_row) | copy-start | bytes 98308
  70.8 42.3 %all-to-all-start.2 = ((f32[256,7,1,128]{3,2,1,0:T(1,128)}), f32[256,7,1,128]{3,2,1,0:T(1,128)S(1)}, u32[]{:S(2)}, u32[]{:S(2)}) async-start(f32[256,7,1,128]{3,2,1,0:T(1,128)} %bitcast.37), calls=%async_computation.2 | async-start | bytes 1835008 | tf_op jit(solution)/shard_map/all_to_all | solution.py:26
  79.9 48.3 %copy-start.1 = (f32[512,400]{0,1:T(8,128)S(1)}, f32[512,400]{0,1:T(8,128)}, u32[]{:S(2)}) copy-start(f32[512,400]{0,1:T(8,128)} %param.6) | copy-start | bytes 2457604
  80.0 48.3 %copy-start.4 = (f32[512]{0:T(512)S(1)}, f32[512]{0:T(512)}, u32[]{:S(2)}) copy-start(f32[512]{0:T(512)} %param.7) | copy-start | bytes 6148
  80.0 10.7 %collective-permute-start.6 = (f32[8,512]{1,0:T(8,128)S(1)}, f32[8,512]{1,0:T(8,128)S(1)}, u32[]{:S(2)}, u32[]{:S(2)}) collective-permute-start(f32[8,512]{1,0:T(8,128)S(1)} %get-tuple-element.29), channel_id=1, source_target_pairs={{0,4},{4,8},{8,12},{12,16},{16,20},{20,24},{24,28},{28,32},{32,36}... | collective-permute-start | bytes 49160 | tf_op jit(solution)/shard_map/ppermute | solution.py:22
  81.8 23.3 %collective-permute-start.7 = (f32[8,512]{1,0:T(8,128)S(1)}, f32[8,512]{1,0:T(8,128)S(1)}, u32[]{:S(2)}, u32[]{:S(2)}) collective-permute-start(f32[8,512]{1,0:T(8,128)S(1)} %get-tuple-element.28), channel_id=1, source_target_pairs={{0,8},{4,12},{8,16},{12,20},{16,24},{20,28},{24,32},{28,36},{32,40... | collective-permute-start | bytes 49160 | tf_op jit(solution)/shard_map/ppermute | solution.py:22
  83.3 23.4 %collective-permute-start.8 = (f32[8,512]{1,0:T(8,128)S(1)}, f32[8,512]{1,0:T(8,128)S(1)}, u32[]{:S(2)}, u32[]{:S(2)}) collective-permute-start(f32[8,512]{1,0:T(8,128)S(1)} %get-tuple-element.27), channel_id=1, source_target_pairs={{0,12},{4,16},{8,20},{12,24},{16,28},{20,32},{24,36},{28,40},{32,4... | collective-permute-start | bytes 49160 | tf_op jit(solution)/shard_map/ppermute | solution.py:22
  106.7 5.3 %collective-permute-start.10 = (f32[32,128]{1,0:T(8,128)S(1)}, f32[32,128]{1,0:T(8,128)S(1)}, u32[]{:S(2)}, u32[]{:S(2)}) collective-permute-start(f32[32,128]{1,0:T(8,128)S(1)} %get-tuple-element.24), channel_id=1, source_target_pairs={{0,2},{1,3},{2,0},{3,1},{4,6},{5,7},{6,4},{7,5},{8,10},{9,11},{10,... | collective-permute-start | bytes 49160 | tf_op jit(solution)/shard_map/ppermute | solution.py:22
  109.3 3.8 %collective-permute-start.11 = (f32[32,128]{1,0:T(8,128)S(1)}, f32[32,128]{1,0:T(8,128)S(1)}, u32[]{:S(2)}, u32[]{:S(2)}) collective-permute-start(f32[32,128]{1,0:T(8,128)S(1)} %get-tuple-element.23), channel_id=1, source_target_pairs={{0,1},{1,2},{2,3},{3,0},{4,5},{5,6},{6,7},{7,4},{8,9},{9,10},{10,1... | collective-permute-start | bytes 49160 | tf_op jit(solution)/shard_map/ppermute | solution.py:22
  109.8 3.3 %collective-permute-start.9 = (f32[32,128]{1,0:T(8,128)S(1)}, f32[32,128]{1,0:T(8,128)S(1)}, u32[]{:S(2)}, u32[]{:S(2)}) collective-permute-start(f32[32,128]{1,0:T(8,128)S(1)} %get-tuple-element.25), channel_id=1, source_target_pairs={{0,3},{1,0},{2,1},{3,2},{4,7},{5,4},{6,5},{7,6},{8,11},{9,8},{10,9... | collective-permute-start | bytes 49160 | tf_op jit(solution)/shard_map/ppermute | solution.py:22
  116.3 6.0 %collective-permute-start.12 = (f32[104,512]{1,0:T(8,128)S(1)}, f32[104,512]{1,0:T(8,128)S(1)}, u32[]{:S(2)}, u32[]{:S(2)}) collective-permute-start(f32[104,512]{1,0:T(8,128)S(1)} %owner.1.own), channel_id=1, source_target_pairs={{0,1},{1,2},{2,3},{3,0},{4,5},{5,6},{6,7},{7,4},{8,9},{9,10},{10,1... | collective-permute-start | bytes 638984 | tf_op jit(solution)/shard_map/ppermute | solution.py:22
  116.3 11.3 %collective-permute-start.13 = (f32[104,512]{1,0:T(8,128)S(1)}, f32[104,512]{1,0:T(8,128)S(1)}, u32[]{:S(2)}, u32[]{:S(2)}) collective-permute-start(f32[104,512]{1,0:T(8,128)S(1)} %owner.1.own), channel_id=1, source_target_pairs={{0,2},{1,3},{2,0},{3,1},{4,6},{5,7},{6,4},{7,5},{8,10},{9,11},{10,... | collective-permute-start | bytes 638984 | tf_op jit(solution)/shard_map/ppermute | solution.py:22
  120.2 8.0 %collective-permute-start.14 = (f32[104,512]{1,0:T(8,128)S(1)}, f32[104,512]{1,0:T(8,128)S(1)}, u32[]{:S(2)}, u32[]{:S(2)}) collective-permute-start(f32[104,512]{1,0:T(8,128)S(1)} %owner.1.own), channel_id=1, source_target_pairs={{0,3},{1,0},{2,1},{3,2},{4,7},{5,4},{6,5},{7,6},{8,11},{9,8},{10,9... | collective-permute-start | bytes 638984 | tf_op jit(solution)/shard_map/ppermute | solution.py:22

commit v4 on v3

--- a/solution.py
+++ b/solution.py
@@ -214,15 +214,21 @@
     high[head_count:live, :], low[head_count:live, :] = halves(tails[...])
     high[live:, :] = jnp.zeros((padded - live, width), bf16)
     low[live:, :] = jnp.zeros((padded - live, width), bf16)
-    for b in range(batches):
+
+    def gathered(b):
         picks = []
         for side in range(2):
             at = (2 * b + side) * edges
             loads[2 * b + side].wait()
             chosen = edge_part[at : at + edges, :]
             picks.append((mm(chosen, high[...]).astype(bf16), mm(chosen, low[...]).astype(bf16)))
+        return picks
+
+    def scored(picks):
         (s_high, s_low), (t_high, t_low) = picks
-        scores = mm_nt(s_high, t_high) + mm_nt(s_high, t_low) + mm_nt(s_low, t_high)
+        return mm_nt(s_high, t_high) + mm_nt(s_high, t_low) + mm_nt(s_low, t_high)
+
+    def gained(b, scores):
         decay = jnp.exp(-jnp.abs(scores))
         upper = 1.0 / (1.0 + decay)
         lower = decay * upper
@@ -232,15 +238,25 @@
         counts = count_row[b, 0:1, :] + jnp.concatenate([count_col[b]] * (edges // LANES), axis=1)
         down = lax.broadcasted_iota(jnp.int32, (edges, edges), 0)
         across = lax.broadcasted_iota(jnp.int32, (edges, edges), 1)
-        gain = weight * counts * (1.0 / edges) - jnp.where(down == across, missing, 0.0)
+        return weight * counts * (1.0 / edges) - jnp.where(down == across, missing, 0.0)
+
+    def pulled(at, gain, high_rows, low_rows):
         g_high, g_low = halves(gain)
-        d_s = mm(g_high, t_high) + mm(g_high, t_low) + mm(g_low, t_high)
-        at = 2 * b * edges
-        d_high[at : at + edges, :], d_low[at : at + edges, :] = halves(d_s)
-        g_high, g_low = halves(gain.T)
-        d_t = mm(g_high, s_high) + mm(g_high, s_low) + mm(g_low, s_high)
-        at += edges
-        d_high[at : at + edges, :], d_low[at : at + edges, :] = halves(d_t)
+        moved = mm(g_high, high_rows) + mm(g_high, low_rows) + mm(g_low, high_rows)
+        d_high[at : at + edges, :], d_low[at : at + edges, :] = halves(moved)
+
+    picks = gathered(0)
+    scores = scored(picks)
+    for b in range(batches):
+        if b + 1 < batches:
+            next_picks = gathered(b + 1)
+        gain = gained(b, scores)
+        if b + 1 < batches:
+            next_scores = scored(next_picks)
+        pulled(2 * b * edges, gain, *picks[1])
+        pulled((2 * b + 1) * edges, gain.T, *picks[0])
+        if b + 1 < batches:
+            picks, scores = next_picks, next_scores
     last.wait()
     stores = []
     block = 2 * LANES
@@ -452,19 +468,17 @@
     hot = hot_rows(mine, listed, rows)
 
     head_grads, tail_grads = grads(heads, tails, *plan, hot)
-    tail_grads = tail_grads.reshape(HEAVY, half, -1)
-    tail_grads = jnp.concatenate(
-        [tail_grads[0]] + [passed_along(tail_grads[r], "dom", r) for r in range(1, HEAVY)], axis=0
-    )
+    back = exchanged(head_grads.reshape(groups * owners, half - 1, 1, LANES), ("rep", "dom"))
     tail_grads = jnp.moveaxis(tail_grads.reshape(HEAVY * half, groups, LANES), 1, 0)
     wanted = [
         lax.dynamic_index_in_dim(tail_grads, (me + groups - s) % groups, 0, keepdims=False)
         for s in range(groups)
     ]
-    tail_back = jnp.concatenate(
+    tail_grads = jnp.stack(
         [wanted[0]] + [passed_along(wanted[s], "rep", -s) for s in range(1, groups)], axis=0
-    )
-    back = exchanged(head_grads.reshape(groups * owners, half - 1, 1, LANES), ("rep", "dom"))
+    ).reshape(groups, HEAVY, half, LANES)
+    tail_back = [tail_grads[:, 0]] + [passed_along(tail_grads[:, r], "dom", r) for r in range(1, HEAVY)]
+    tail_back = jnp.stack(tail_back, axis=1).reshape(-1, LANES)
     quarter = owner(back.reshape(-1, LANES), tail_back, hot)
     pieces = [quarter] + [passed_along(quarter, "rep", s) for s in range(1, groups)]
     new_rows, new_sums = update(mine, pieces, columns, adagrad_sum.reshape(1, -1))

time: 131 us -> 128 us (0.977)
  waiting for transfers between devices: 44.1 us -> 42.6 us
    ppermute x15, waiting for transfers between devices: 33.7 us -> 28.5 us  [passed_along(): return lax.ppermute(value, axis, pairs)]
    all_to_all x3, waiting for transfers between devices: 10.4 us -> 14.1 us  [exchanged(): return lax.all_to_all(value, axis, 0, 0, tiled=True)]
  transfers between devices with their start and end apart: 18 -> 18, of which waited for: 11 -> 10; matrix products, arithmetic and copies ran while one was open for 1% -> 1% of each run, Pallas kernels for 5% -> 5%
where the time goes in v4:
time: 128 us
  starting transfers between devices  52 us (41%)
  waiting for transfers between devices  42.6 us (33%)
  Pallas kernels  28.4 us (22%)
  local copies, waits for them, and re-layouts  3.25 us (3%)
    ppermute x15, waiting for transfers between devices, passed_along(): return lax.ppermute(value, axis, pairs)  28.5 us
    all_to_all x3, starting transfers between devices, exchanged(): return lax.all_to_all(value, axis, 0, 0, tiled=True)  27 us
    ppermute x15, starting transfers between devices, passed_along(): return lax.ppermute(value, axis, pairs)  25 us
    pallas_call x1, Pallas kernels, grads(): pl.pallas_call(grads_body, in_specs=[VMEM, VMEM, HBM, HBM, VMEM, VMEM, HB...  14.2 us
    all_to_all x3, waiting for transfers between devices, exchanged(): return lax.all_to_all(value, axis, 0, 0, tiled=True)  14.1 us
    pallas_call x1, Pallas kernels, serve(): pl.pallas_call(serve_body, in_specs=[SMEM, SMEM, VMEM], out_specs=[HBM, V...  3.48 us
    pallas_call x1, Pallas kernels, prep(): pl.pallas_call(prep_body, out_shape=[pltpu.HBM((total, padded), bf16), pl...  3.35 us
    pallas_call x1, Pallas kernels, owner(): pl.pallas_call(owner_body, in_specs=[VMEM, VMEM, HBM], out_specs=VMEM, ou...  3.08 us
  transfers between devices with their start and end apart: 18, of which 10 were waited for; matrix products, arithmetic and copies ran while one was open for 1% of the time, Pallas kernels for 5%

profile of v4, /device:TPU:1, one launch (start us, length us, event | category | flops | bytes accessed | tf_op | source)
XLA Modules:
  0.0 127.8 jit_solution(8455968869347318741)
XLA Ops:
  0.6 1.4 %copy.25 = s32[1,1,64,16]{3,2,1,0:T(8,128)} copy(s32[1,1,64,16]{2,3,1,0:T(8,128)} %param.8) | data formatting | bytes 8192 | tf_op args[2]
  2.0 13.1 %all-to-all-start = ((s32[64,1,16]{2,1,0:T(1,128)}), s32[64,1,16]{2,1,0:T(1,128)S(1)}, u32[]{:S(2)}, u32[]{:S(2)}) async-start(s32[64,1,16]{2,1,0:T(1,128)} %bitcast.1), calls=%async_computation | async-start | bytes 65536 | tf_op jit(solution)/shard_map/all_to_all | solution.py:26
  15.2 0.0 copy-start
  15.2 1.1 copy-done
  16.3 0.3 spread.1.rows
  16.7 7.7 %all-to-all-done.ids = s32[64,1,16]{2,1,0:T(1,128)S(1)} async-done(((s32[64,1,16]{2,1,0:T(1,128)}), s32[64,1,16]{2,1,0:T(1,128)S(1)}, u32[]{:S(2)}, u32[]{:S(2)}) %all-to-all-start) | async-done | bytes 4128 | tf_op jit(solution)/shard_map/all_to_all | solution.py:26
  24.4 3.5 %serve.1 = (f32[1600,128]{1,0:T(8,128)}, f32[32,512]{1,0:T(8,128)S(1)}) custom-call(s32[64,1,16]{2,1,0:T(1,128)S(1)} %all-to-all-done.ids, s32[1]{0:T(128)} %bitcast.2.here, f32[512,512]{1,0:T(8,128)S(1)} %spread.1.rows), custom_call_target="tpu_custom_call" | custom-call | tf_op jit(solution)/shard_map/serve/pallas_call | solution.py:116
  27.9 4.8 %all-to-all-start.1 = ((f32[64,25,1,128]{3,2,1,0:T(1,128)}), f32[64,25,1,128]{3,2,1,0:T(1,128)S(1)}, u32[]{:S(2)}, u32[]{:S(2)}) async-start(f32[64,25,1,128]{3,2,1,0:T(1,128)} %bitcast.49), calls=%async_computation.1 | async-start | bytes 1638400 | tf_op jit(solution)/shard_map/all_to_all | solution.py:26
  32.8 0.1 iota_compare_fusion
  32.8 0.1 slice.50
  32.9 0.1 copy.28
  33.0 0.2 select_reduce_fusion
  33.1 0.1 reshape.323
  33.2 0.1 reshape.322
  33.4 0.2 slice_reduce_fusion
  33.5 0.1 pad_add_fusion.1.refs_0_
  33.6 2.5 %collective-permute-start.3 = (s32[1,544]{1,0:T(1,128)S(1)}, s32[1,544]{1,0:T(1,128)S(1)}, u32[]{:S(2)}, u32[]{:S(2)}) collective-permute-start(s32[1,544]{1,0:T(1,128)S(1)} %pad_add_fusion.1.refs_0_), channel_id=1, source_target_pairs={{0,3},{1,0},{2,1},{3,2},{4,7},{5,4},{6,5},{7,6},{8,11},{9,8},{10,9... | collective-permute-start | bytes 6536 | tf_op jit(solution)/shard_map/ppermute | solution.py:22
  36.1 0.5 collective-permute-start.4
  36.6 0.6 collective-permute-start.5
  37.2 6.2 %collective-permute-start.2 = (f32[8,512]{1,0:T(8,128)S(1)}, f32[8,512]{1,0:T(8,128)S(1)}, u32[]{:S(2)}, u32[]{:S(2)}) collective-permute-start(f32[8,512]{1,0:T(8,128)S(1)} %get-tuple-element.31), channel_id=1, source_target_pairs={{0,244},{4,248},{8,252},{12,0},{16,4},{20,8},{24,12},{28,16},{32,2... | collective-permute-start | bytes 49160 | tf_op jit(solution)/shard_map/ppermute | solution.py:22
  43.5 1.2 collective-permute-start.1
  44.6 0.4 collective-permute-start
  45.1 0.1 compare_select_fusion.2.slots
  45.2 3.4 %prep.1 = (bf16[2048,640]{1,0:T(8,128)(2,1)}, bf16[544,2048]{1,0:T(8,128)(2,1)}, f32[2,8,512]{2,1,0:T(8,128)}, f32[2,512,128]{2,1,0:T(8,128)}) custom-call(s32[1,2048]{1,0:T(1,128)S(1)} %compare_select_fusion.2.slots, s32[1,2048]{1,0:T(1,128)S(1)} %reshape_squeeze.10.negs), custom_call_target="tpu_custom_call" | custom-call | tf_op jit(solution)/shard_map/prep/pallas_call | solution.py:159
  48.6 2.3 %hot.1.ahead = bf16[512,2176]{1,0:T(8,128)(2,1)} custom-call(s32[1]{0:T(128)} %bitcast.me, s32[1,544]{1,0:T(1,128)S(1)} %pad_add_fusion.1.refs_0_, s32[1,544]{1,0:T(1,128)S(1)} %collective-permute-done.3.refs_1_, s32[1,544]{1,0:T(1,128)S(1)} %collective-permute-done.4.refs_2_, s32[1,544]{1,0:T(1,128)S(1)} %collective-permute-done.5.refs_3_), custom_call_target="tpu_custom_call" | custom-call | tf_op jit(solution)/shard_map/hot/pallas_call | solution.py:334
  50.9 2.6 %collective-permute-done.2 = f32[8,512]{1,0:T(8,128)S(1)} collective-permute-done((f32[8,512]{1,0:T(8,128)S(1)}, f32[8,512]{1,0:T(8,128)S(1)}, u32[]{:S(2)}, u32[]{:S(2)}) %collective-permute-start.2) | collective-permute-done | bytes 16416 | tf_op jit(solution)/shard_map/ppermute | solution.py:22
  53.5 0.2 collective-permute-done
  53.7 2.6 %all-to-all-done.1 = f32[64,25,1,128]{3,2,1,0:T(1,128)S(1)} async-done(((f32[64,25,1,128]{3,2,1,0:T(1,128)}), f32[64,25,1,128]{3,2,1,0:T(1,128)S(1)}, u32[]{:S(2)}, u32[]{:S(2)}) %all-to-all-start.1) | async-done | bytes 819232 | tf_op jit(solution)/shard_map/all_to_all | solution.py:26
  56.4 14.2 %grads.1 = (f32[1792,128]{1,0:T(8,128)}, f32[32,512]{1,0:T(8,128)S(1)}) custom-call(f32[1600,128]{1,0:T(8,128)S(1)} %bitcast.40, f32[32,512]{1,0:T(8,128)S(1)} %pad_maximum_fusion.tails, bf16[2048,640]{1,0:T(8,128)(2,1)} %get-tuple-element.14.by_edge, bf16[544,2048]{1,0:T(8,128)(2,1)} %get-tuple-element.15.by_slot, f32[2,8,512]{2,1,0:T(8,128)S(1)} %copy-done.3, ...), custom_call_target="tpu_custom_call" | custom-call | tf_op jit(solution)/shard_map/grads/pallas_call | solution.py:294
  70.6 9.1 %all-to-all-start.2 = ((f32[256,7,1,128]{3,2,1,0:T(1,128)}), f32[256,7,1,128]{3,2,1,0:T(1,128)S(1)}, u32[]{:S(2)}, u32[]{:S(2)}) async-start(f32[256,7,1,128]{3,2,1,0:T(1,128)} %bitcast.48), calls=%async_computation.2 | async-start | bytes 1835008 | tf_op jit(solution)/shard_map/all_to_all | solution.py:26
  79.7 0.0 copy-start.1
  79.8 0.1 constant_dynamic-slice_fusion.3
  79.8 1.4 %collective-permute-start.8 = (f32[32,128]{1,0:T(8,128)S(1)}, f32[32,128]{1,0:T(8,128)S(1)}, u32[]{:S(2)}, u32[]{:S(2)}) collective-permute-start(f32[32,128]{1,0:T(8,128)S(1)} %bitcast.55), channel_id=1, source_target_pairs={{0,1},{1,2},{2,3},{3,0},{4,5},{5,6},{6,7},{7,4},{8,9},{9,10},{10,1... | collective-permute-start | bytes 49160 | tf_op jit(solution)/shard_map/ppermute | solution.py:22
  81.3 2.4 %collective-permute-start.7 = (f32[32,128]{1,0:T(8,128)S(1)}, f32[32,128]{1,0:T(8,128)S(1)}, u32[]{:S(2)}, u32[]{:S(2)}) collective-permute-start(f32[32,128]{1,0:T(8,128)S(1)} %bitcast.52), channel_id=1, source_target_pairs={{0,2},{1,3},{2,0},{3,1},{4,6},{5,7},{6,4},{7,5},{8,10},{9,11},{10,... | collective-permute-start | bytes 49160 | tf_op jit(solution)/shard_map/ppermute | solution.py:22
  83.7 1.2 collective-permute-start.6
  84.9 0.8 collective-permute-done.7
  85.7 1.1 collective-permute-done.6
  86.8 4.4 %collective-permute-start.11 = (f32[4,8,128]{2,1,0:T(8,128)S(1)}, f32[4,8,128]{2,1,0:T(8,128)S(1)}, u32[]{:S(2)}, u32[]{:S(2)}) collective-permute-start(f32[4,8,128]{2,1,0:T(8,128)S(1)} %get-tuple-element.23), channel_id=1, source_target_pairs={{0,12},{4,16},{8,20},{12,24},{16,28},{20,32},{24,36},{28,40},{32,4... | collective-permute-start | bytes 49160 | tf_op jit(solution)/shard_map/ppermute | solution.py:22
  91.3 1.2 collective-permute-start.10
  92.5 13.5 %collective-permute-done.11 = f32[4,8,128]{2,1,0:T(8,128)S(1)} collective-permute-done((f32[4,8,128]{2,1,0:T(8,128)S(1)}, f32[4,8,128]{2,1,0:T(8,128)S(1)}, u32[]{:S(2)}, u32[]{:S(2)}) %collective-permute-start.11) | collective-permute-done | bytes 16416 | tf_op jit(solution)/shard_map/ppermute | solution.py:22
  106.1 3.7 %all-to-all-done.2 = f32[256,7,1,128]{3,2,1,0:T(1,128)S(1)} async-done(((f32[256,7,1,128]{3,2,1,0:T(1,128)}), f32[256,7,1,128]{3,2,1,0:T(1,128)S(1)}, u32[]{:S(2)}, u32[]{:S(2)}) %all-to-all-start.2) | async-done | bytes 917536 | tf_op jit(solution)/shard_map/all_to_all | solution.py:26
  109.8 3.1 %owner.1.own = f32[104,512]{1,0:T(8,128)S(1)} custom-call(f32[1792,128]{1,0:T(8,128)S(1)} %bitcast.39, f32[128,128]{1,0:T(8,128)S(1)} %bitcast.46, bf16[512,2176]{1,0:T(8,128)(2,1)} %hot.1.ahead), custom_call_target="tpu_custom_call" | custom-call | tf_op jit(solution)/shard_map/owner/pallas_call | solution.py:372
  112.9 0.4 collective-permute-start.12
  113.3 1.8 %collective-permute-start.13 = (f32[104,512]{1,0:T(8,128)S(1)}, f32[104,512]{1,0:T(8,128)S(1)}, u32[]{:S(2)}, u32[]{:S(2)}) collective-permute-start(f32[104,512]{1,0:T(8,128)S(1)} %owner.1.own), channel_id=1, source_target_pairs={{0,2},{1,3},{2,0},{3,1},{4,6},{5,7},{6,4},{7,5},{8,10},{9,11},{10,... | collective-permute-start | bytes 638984 | tf_op jit(solution)/shard_map/ppermute | solution.py:22
  115.0 0.7 collective-permute-start.14
  115.8 9.2 %collective-permute-done.12.next1 = f32[104,512]{1,0:T(8,128)S(1)} collective-permute-done((f32[104,512]{1,0:T(8,128)S(1)}, f32[104,512]{1,0:T(8,128)S(1)}, u32[]{:S(2)}, u32[]{:S(2)}) %collective-permute-start.12) | collective-permute-done | bytes 213024 | tf_op jit(solution)/shard_map/ppermute | solution.py:22
  125.0 0.9 collective-permute-done.14.next3
  125.9 1.7 %update.1 = (f32[400,512]{1,0:T(8,128)}, f32[1,512]{1,0:T(1,128)}) custom-call(s32[1]{0:T(128)} %bitcast.me, f32[104,512]{1,0:T(8,128)S(1)} %owner.1.own, f32[104,512]{1,0:T(8,128)S(1)} %collective-permute-done.12.next1, f32[104,512]{1,0:T(8,128)S(1)} %collective-permute-done.13.next2, f32[104,512]{1,0:T(8,128)S(1)} %collective-permute-done.14.next3, ...), custom_call_target="tpu_custom_call" | custom-call | tf_op jit(solution)/shard_map/update/pallas_call | solution.py:413
  (33 shorter events, 0.2 us)
Async XLA Ops:
  2.0 22.4 %all-to-all-start = ((s32[64,1,16]{2,1,0:T(1,128)}), s32[64,1,16]{2,1,0:T(1,128)S(1)}, u32[]{:S(2)}, u32[]{:S(2)}) async-start(s32[64,1,16]{2,1,0:T(1,128)} %bitcast.1), calls=%async_computation | async-start | bytes 65536 | tf_op jit(solution)/shard_map/all_to_all | solution.py:26
  15.2 1.1 copy-start
  16.3 16.3 %copy-start.6 = (s32[1,1,2,512]{3,2,1,0:T(2,128)S(1)}, s32[1,1,2,512]{3,2,1,0:T(2,128)}, u32[]{:S(2)}) copy-start(s32[1,1,2,512]{3,2,1,0:T(2,128)} %param.10) | copy-start | bytes 12292
  16.3 16.3 %copy-start.7 = (s32[1,1,2,512]{3,2,1,0:T(2,128)S(1)}, s32[1,1,2,512]{3,2,1,0:T(2,128)}, u32[]{:S(2)}) copy-start(s32[1,1,2,512]{3,2,1,0:T(2,128)} %param.9) | copy-start | bytes 12292
  16.3 28.9 %copy-start.5 = (s32[1,1,2,2,512]{4,3,2,1,0:T(2,128)S(1)}, s32[1,1,2,2,512]{4,3,2,1,0:T(2,128)}, u32[]{:S(2)}) copy-start(s32[1,1,2,2,512]{4,3,2,1,0:T(2,128)} %param.11) | copy-start | bytes 24580
  27.9 28.5 %all-to-all-start.1 = ((f32[64,25,1,128]{3,2,1,0:T(1,128)}), f32[64,25,1,128]{3,2,1,0:T(1,128)S(1)}, u32[]{:S(2)}, u32[]{:S(2)}) async-start(f32[64,25,1,128]{3,2,1,0:T(1,128)} %bitcast.49), calls=%async_computation.1 | async-start | bytes 1638400 | tf_op jit(solution)/shard_map/all_to_all | solution.py:26
  33.6 11.0 %collective-permute-start.3 = (s32[1,544]{1,0:T(1,128)S(1)}, s32[1,544]{1,0:T(1,128)S(1)}, u32[]{:S(2)}, u32[]{:S(2)}) collective-permute-start(s32[1,544]{1,0:T(1,128)S(1)} %pad_add_fusion.1.refs_0_), channel_id=1, source_target_pairs={{0,3},{1,0},{2,1},{3,2},{4,7},{5,4},{6,5},{7,6},{8,11},{9,8},{10,9... | collective-permute-start | bytes 6536 | tf_op jit(solution)/shard_map/ppermute | solution.py:22
  36.1 12.5 %collective-permute-start.4 = (s32[1,544]{1,0:T(1,128)S(1)}, s32[1,544]{1,0:T(1,128)S(1)}, u32[]{:S(2)}, u32[]{:S(2)}) collective-permute-start(s32[1,544]{1,0:T(1,128)S(1)} %pad_add_fusion.1.refs_0_), channel_id=1, source_target_pairs={{0,2},{1,3},{2,0},{3,1},{4,6},{5,7},{6,4},{7,5},{8,10},{9,11},{10,... | collective-permute-start | bytes 6536 | tf_op jit(solution)/shard_map/ppermute | solution.py:22
  36.6 12.0 %collective-permute-start.5 = (s32[1,544]{1,0:T(1,128)S(1)}, s32[1,544]{1,0:T(1,128)S(1)}, u32[]{:S(2)}, u32[]{:S(2)}) collective-permute-start(s32[1,544]{1,0:T(1,128)S(1)} %pad_add_fusion.1.refs_0_), channel_id=1, source_target_pairs={{0,1},{1,2},{2,3},{3,0},{4,5},{5,6},{6,7},{7,4},{8,9},{9,10},{10,1... | collective-permute-start | bytes 6536 | tf_op jit(solution)/shard_map/ppermute | solution.py:22
  37.2 16.3 %collective-permute-start.2 = (f32[8,512]{1,0:T(8,128)S(1)}, f32[8,512]{1,0:T(8,128)S(1)}, u32[]{:S(2)}, u32[]{:S(2)}) collective-permute-start(f32[8,512]{1,0:T(8,128)S(1)} %get-tuple-element.31), channel_id=1, source_target_pairs={{0,244},{4,248},{8,252},{12,0},{16,4},{20,8},{24,12},{28,16},{32,2... | collective-permute-start | bytes 49160 | tf_op jit(solution)/shard_map/ppermute | solution.py:22
  43.5 10.1 %collective-permute-start.1 = (f32[8,512]{1,0:T(8,128)S(1)}, f32[8,512]{1,0:T(8,128)S(1)}, u32[]{:S(2)}, u32[]{:S(2)}) collective-permute-start(f32[8,512]{1,0:T(8,128)S(1)} %get-tuple-element.32), channel_id=1, source_target_pairs={{0,248},{4,252},{8,0},{12,4},{16,8},{20,12},{24,16},{28,20},{32,24... | collective-permute-start | bytes 49160 | tf_op jit(solution)/shard_map/ppermute | solution.py:22
  44.6 9.1 %collective-permute-start = (f32[8,512]{1,0:T(8,128)S(1)}, f32[8,512]{1,0:T(8,128)S(1)}, u32[]{:S(2)}, u32[]{:S(2)}) collective-permute-start(f32[8,512]{1,0:T(8,128)S(1)} %get-tuple-element.33), channel_id=1, source_target_pairs={{0,252},{4,0},{8,4},{12,8},{16,12},{20,16},{24,20},{28,24},{32,28}... | collective-permute-start | bytes 49160 | tf_op jit(solution)/shard_map/ppermute | solution.py:22
  48.6 7.8 %copy-start.2 = (f32[2,512,128]{2,1,0:T(8,128)S(1)}, f32[2,512,128]{2,1,0:T(8,128)}, u32[]{:S(2)}) copy-start(f32[2,512,128]{2,1,0:T(8,128)} %get-tuple-element.17.count_col) | copy-start | bytes 1572868
  48.6 7.8 %copy-start.3 = (f32[2,8,512]{2,1,0:T(8,128)S(1)}, f32[2,8,512]{2,1,0:T(8,128)}, u32[]{:S(2)}) copy-start(f32[2,8,512]{2,1,0:T(8,128)} %get-tuple-element.16.count_row) | copy-start | bytes 98308
  70.6 39.2 %all-to-all-start.2 = ((f32[256,7,1,128]{3,2,1,0:T(1,128)}), f32[256,7,1,128]{3,2,1,0:T(1,128)S(1)}, u32[]{:S(2)}, u32[]{:S(2)}) async-start(f32[256,7,1,128]{3,2,1,0:T(1,128)} %bitcast.48), calls=%async_computation.2 | async-start | bytes 1835008 | tf_op jit(solution)/shard_map/all_to_all | solution.py:26
  79.7 46.3 %copy-start.1 = (f32[512,400]{0,1:T(8,128)S(1)}, f32[512,400]{0,1:T(8,128)}, u32[]{:S(2)}) copy-start(f32[512,400]{0,1:T(8,128)} %param.6) | copy-start | bytes 2457604
  79.7 46.2 %copy-start.4 = (f32[512]{0:T(512)S(1)}, f32[512]{0:T(512)}, u32[]{:S(2)}) copy-start(f32[512]{0:T(512)} %param.7) | copy-start | bytes 6148
  79.8 5.0 %collective-permute-start.8 = (f32[32,128]{1,0:T(8,128)S(1)}, f32[32,128]{1,0:T(8,128)S(1)}, u32[]{:S(2)}, u32[]{:S(2)}) collective-permute-start(f32[32,128]{1,0:T(8,128)S(1)} %bitcast.55), channel_id=1, source_target_pairs={{0,1},{1,2},{2,3},{3,0},{4,5},{5,6},{6,7},{7,4},{8,9},{9,10},{10,1... | collective-permute-start | bytes 49160 | tf_op jit(solution)/shard_map/ppermute | solution.py:22
  81.3 4.4 %collective-permute-start.7 = (f32[32,128]{1,0:T(8,128)S(1)}, f32[32,128]{1,0:T(8,128)S(1)}, u32[]{:S(2)}, u32[]{:S(2)}) collective-permute-start(f32[32,128]{1,0:T(8,128)S(1)} %bitcast.52), channel_id=1, source_target_pairs={{0,2},{1,3},{2,0},{3,1},{4,6},{5,7},{6,4},{7,5},{8,10},{9,11},{10,... | collective-permute-start | bytes 49160 | tf_op jit(solution)/shard_map/ppermute | solution.py:22
  83.7 3.1 %collective-permute-start.6 = (f32[32,128]{1,0:T(8,128)S(1)}, f32[32,128]{1,0:T(8,128)S(1)}, u32[]{:S(2)}, u32[]{:S(2)}) collective-permute-start(f32[32,128]{1,0:T(8,128)S(1)} %bitcast.51), channel_id=1, source_target_pairs={{0,3},{1,0},{2,1},{3,2},{4,7},{5,4},{6,5},{7,6},{8,11},{9,8},{10,9... | collective-permute-start | bytes 49160 | tf_op jit(solution)/shard_map/ppermute | solution.py:22
  86.8 19.2 %collective-permute-start.11 = (f32[4,8,128]{2,1,0:T(8,128)S(1)}, f32[4,8,128]{2,1,0:T(8,128)S(1)}, u32[]{:S(2)}, u32[]{:S(2)}) collective-permute-start(f32[4,8,128]{2,1,0:T(8,128)S(1)} %get-tuple-element.23), channel_id=1, source_target_pairs={{0,12},{4,16},{8,20},{12,24},{16,28},{20,32},{24,36},{28,40},{32,4... | collective-permute-start | bytes 49160 | tf_op jit(solution)/shard_map/ppermute | solution.py:22
  91.3 14.8 %collective-permute-start.10 = (f32[4,8,128]{2,1,0:T(8,128)S(1)}, f32[4,8,128]{2,1,0:T(8,128)S(1)}, u32[]{:S(2)}, u32[]{:S(2)}) collective-permute-start(f32[4,8,128]{2,1,0:T(8,128)S(1)} %get-tuple-element.24), channel_id=1, source_target_pairs={{0,8},{4,12},{8,16},{12,20},{16,24},{20,28},{24,32},{28,36},{32,40... | collective-permute-start | bytes 49160 | tf_op jit(solution)/shard_map/ppermute | solution.py:22
  92.5 13.5 %collective-permute-start.9 = (f32[4,8,128]{2,1,0:T(8,128)S(1)}, f32[4,8,128]{2,1,0:T(8,128)S(1)}, u32[]{:S(2)}, u32[]{:S(2)}) collective-permute-start(f32[4,8,128]{2,1,0:T(8,128)S(1)} %get-tuple-element.25), channel_id=1, source_target_pairs={{0,4},{4,8},{8,12},{12,16},{16,20},{20,24},{24,28},{28,32},{32,36}... | collective-permute-start | bytes 49160 | tf_op jit(solution)/shard_map/ppermute | solution.py:22
  112.9 12.1 %collective-permute-start.12 = (f32[104,512]{1,0:T(8,128)S(1)}, f32[104,512]{1,0:T(8,128)S(1)}, u32[]{:S(2)}, u32[]{:S(2)}) collective-permute-start(f32[104,512]{1,0:T(8,128)S(1)} %owner.1.own), channel_id=1, source_target_pairs={{0,1},{1,2},{2,3},{3,0},{4,5},{5,6},{6,7},{7,4},{8,9},{9,10},{10,1... | collective-permute-start | bytes 638984 | tf_op jit(solution)/shard_map/ppermute | solution.py:22
  113.3 11.7 %collective-permute-start.13 = (f32[104,512]{1,0:T(8,128)S(1)}, f32[104,512]{1,0:T(8,128)S(1)}, u32[]{:S(2)}, u32[]{:S(2)}) collective-permute-start(f32[104,512]{1,0:T(8,128)S(1)} %owner.1.own), channel_id=1, source_target_pairs={{0,2},{1,3},{2,0},{3,1},{4,6},{5,7},{6,4},{7,5},{8,10},{9,11},{10,... | collective-permute-start | bytes 638984 | tf_op jit(solution)/shard_map/ppermute | solution.py:22
  115.0 10.9 %collective-permute-start.14 = (f32[104,512]{1,0:T(8,128)S(1)}, f32[104,512]{1,0:T(8,128)S(1)}, u32[]{:S(2)}, u32[]{:S(2)}) collective-permute-start(f32[104,512]{1,0:T(8,128)S(1)} %owner.1.own), channel_id=1, source_target_pairs={{0,3},{1,0},{2,1},{3,2},{4,7},{5,4},{6,5},{7,6},{8,11},{9,8},{10,9... | collective-permute-start | bytes 638984 | tf_op jit(solution)/shard_map/ppermute | solution.py:22

commit v5 on v4

--- a/solution.py
+++ b/solution.py
@@ -8,6 +8,7 @@
 
 HEAVY = 4
 LEARN_RATE = 0.1
+LOG2E = 1.4426950408889634
 LANES = 128
 MAIN = 104
 SPARE = LANES - MAIN
@@ -59,18 +60,18 @@
 
 def spread_body(columns, out):
     depth, rows = columns.shape
-    for c in range(out.shape[1] // LANES):
+    for c in range(out.shape[1]):
         piece = columns[c * LANES : min((c + 1) * LANES, depth), :]
         if piece.shape[0] < LANES:
             piece = jnp.concatenate([piece, jnp.zeros((LANES - piece.shape[0], rows), f32)], axis=0)
-        out[:, c * LANES : (c + 1) * LANES] = piece.T
+        out[:, c, :] = piece.T
 
 
 def spread_rows(columns):
     return pl.pallas_call(
         spread_body,
         out_specs=VMEM,
-        out_shape=pltpu.VMEM((columns.shape[1], LANES * QUARTERS), f32),
+        out_shape=pltpu.VMEM((columns.shape[1], QUARTERS, LANES), f32),
         compiler_params=room(16),
         name="spread",
     )(columns)
@@ -84,17 +85,18 @@
     tall = 8 * blocks + 1
 
     def eight(w, carry):
-        taken = [rows[pl.ds(ids[w, 0, k], 1), :] for k in range(8)]
+        taken = [rows[ids[w, 0, k]] for k in range(8)]
         for k in range(8):
-            for c in range(blocks):
-                picked[pl.ds(w * tall + 8 * c + k, 1), :] = taken[k][:, c * LANES : (c + 1) * LANES]
-            ends[pl.ds(w * 8 + k, 1), :] = taken[k][:, blocks * LANES :]
+            picked[pl.ds(w * tall + k, blocks, stride=8), :] = taken[k][:blocks]
+            ends[pl.ds(w * 8 + k, 1), :] = taken[k][blocks:]
         return carry
 
     for reach in range(HEAVY):
         asker = (here[0] + owners - reach) % owners
         for k in range(8):
-            tails[reach * 8 + k : reach * 8 + k + 1, :] = rows[pl.ds(ids[asker, 0, 8 + k], 1), :]
+            row = rows[ids[asker, 0, 8 + k]]
+            for c in range(QUARTERS):
+                tails[reach * 8 + k : reach * 8 + k + 1, c * LANES : (c + 1) * LANES] = row[c : c + 1]
     copies = []
     for part in range(parts):
         lax.fori_loop(part * each, (part + 1) * each, eight, 0, unroll=4)
@@ -110,7 +112,7 @@
 
 
 def serve(ids, here, rows):
-    width = rows.shape[1]
+    width = QUARTERS * LANES
     owners = ids.shape[0]
     shape = (owners * (8 * (QUARTERS - 1) + 1), LANES)
     return pl.pallas_call(
@@ -148,9 +150,9 @@
         down = lax.broadcasted_iota(jnp.int32, (edges, edges), 0)
         drawn = jnp.where(down == neg, one, zero).astype(bf16)
         if p % 2 == 0:
-            count_row[p // 2] = mm_nt(jnp.ones((8, edges), bf16), drawn)
+            count_row[p // 2] = mm_nt(jnp.ones((8, edges), bf16), drawn) * (1.0 / edges)
         else:
-            count_col[p // 2] = mm(drawn, jnp.ones((edges, LANES), bf16))
+            count_col[p // 2] = mm(drawn, jnp.ones((edges, LANES), bf16)) * (1.0 / edges)
 
 
 def prep(slots, negs, edges, live, padded):
@@ -229,19 +231,20 @@
         return mm_nt(s_high, t_high) + mm_nt(s_high, t_low) + mm_nt(s_low, t_high)
 
     def gained(b, scores):
-        decay = jnp.exp(-jnp.abs(scores))
-        upper = 1.0 / (1.0 + decay)
-        lower = decay * upper
-        sure = scores >= 0
-        weight = jnp.where(sure, upper, lower)
-        missing = jnp.where(sure, lower, upper)
+        decay = jnp.exp2(jnp.minimum(scores * -LOG2E, 126.0))
+        weight = 1.0 / (1.0 + decay)
         counts = count_row[b, 0:1, :] + jnp.concatenate([count_col[b]] * (edges // LANES), axis=1)
-        down = lax.broadcasted_iota(jnp.int32, (edges, edges), 0)
-        across = lax.broadcasted_iota(jnp.int32, (edges, edges), 1)
-        return weight * counts * (1.0 / edges) - jnp.where(down == across, missing, 0.0)
-
-    def pulled(at, gain, high_rows, low_rows):
-        g_high, g_low = halves(gain)
+        gain = weight * counts
+        eye = lanes_of((LANES, LANES)) == lax.broadcasted_iota(jnp.int32, (LANES, LANES), 0)
+        bands = []
+        for i in range(edges // LANES):
+            span = slice(i * LANES, (i + 1) * LANES)
+            missing = jnp.where(eye, decay[span, span] * weight[span, span], 0.0)
+            row = [gain[span, : i * LANES], gain[span, span] - missing, gain[span, (i + 1) * LANES :]]
+            bands.append(jnp.concatenate([part for part in row if part.shape[1]], axis=1))
+        return jnp.concatenate(bands, axis=0)
+
+    def pulled(at, g_high, g_low, high_rows, low_rows):
         moved = mm(g_high, high_rows) + mm(g_high, low_rows) + mm(g_low, high_rows)
         d_high[at : at + edges, :], d_low[at : at + edges, :] = halves(moved)
 
@@ -253,8 +256,9 @@
         gain = gained(b, scores)
         if b + 1 < batches:
             next_scores = scored(next_picks)
-        pulled(2 * b * edges, gain, *picks[1])
-        pulled((2 * b + 1) * edges, gain.T, *picks[0])
+        g_high, g_low = halves(gain)
+        pulled(2 * b * edges, g_high, g_low, *picks[1])
+        pulled((2 * b + 1) * edges, g_high.T, g_low.T, *picks[0])
         if b + 1 < batches:
             picks, scores = next_picks, next_scores
     last.wait()
@@ -350,7 +354,7 @@
     for p, (at, size) in enumerate(spans):
         loads.append(pltpu.make_async_copy(hot.at[:, pl.ds(at, size)], spots.at[:, pl.ds(at, size)], sems.at[p]))
         loads[-1].start()
-    summed = jnp.zeros((hot.shape[0], LANES), f32)
+    total = None
     for p, (at, size) in enumerate(spans):
         if p < parts:
             eighth = jnp.zeros((owners, LANES), f32)
@@ -364,7 +368,8 @@
         both = jnp.concatenate(halves(values), axis=1)
         loads[p].wait()
         part = mm(spots[:, at : at + size], both)
-        summed += part[:, :LANES] + part[:, LANES:]
+        total = part if total is None else total + part
+    summed = total[:, :LANES] + total[:, LANES:]
     out[...] = summed.T[: out.shape[0], :]
 
 

time: 128 us -> 127 us (level)
  no operation moved by 1% of the time
where the time goes in v5:
time: 127 us
  starting transfers between devices  52 us (41%)
  waiting for transfers between devices  42.2 us (33%)
  Pallas kernels  27.7 us (22%)
  local copies, waits for them, and re-layouts  3.25 us (3%)
    ppermute x15, waiting for transfers between devices, passed_along(): return lax.ppermute(value, axis, pairs)  28.4 us
    all_to_all x3, starting transfers between devices, exchanged(): return lax.all_to_all(value, axis, 0, 0, tiled=True)  27 us
    ppermute x15, starting transfers between devices, passed_along(): return lax.ppermute(value, axis, pairs)  25 us
    pallas_call x1, Pallas kernels, grads(): pl.pallas_call(grads_body, in_specs=[VMEM, VMEM, HBM, HBM, VMEM, VMEM, HB...  14 us
    all_to_all x3, waiting for transfers between devices, exchanged(): return lax.all_to_all(value, axis, 0, 0, tiled=True)  13.8 us
    pallas_call x1, Pallas kernels, prep(): pl.pallas_call(prep_body, out_shape=[pltpu.HBM((total, padded), bf16), pl...  3.46 us
    pallas_call x1, Pallas kernels, serve(): pl.pallas_call(serve_body, in_specs=[SMEM, SMEM, VMEM], out_specs=[HBM, V...  2.83 us
    pallas_call x1, Pallas kernels, owner(): pl.pallas_call(owner_body, in_specs=[VMEM, VMEM, HBM], out_specs=VMEM, ou...  2.79 us
  transfers between devices with their start and end apart: 18, of which 10 were waited for; matrix products, arithmetic and copies ran while one was open for 1% of the time, Pallas kernels for 5%

profile of v5, /device:TPU:1, one launch (start us, length us, event | category | flops | bytes accessed | tf_op | source)
XLA Modules:
  0.0 126.7 jit_solution(13689008661099301781)
XLA Ops:
  0.6 1.4 %copy.25 = s32[1,1,64,16]{3,2,1,0:T(8,128)} copy(s32[1,1,64,16]{2,3,1,0:T(8,128)} %param.8) | data formatting | bytes 8192 | tf_op args[2]
  2.0 13.1 %all-to-all-start = ((s32[64,1,16]{2,1,0:T(1,128)}), s32[64,1,16]{2,1,0:T(1,128)S(1)}, u32[]{:S(2)}, u32[]{:S(2)}) async-start(s32[64,1,16]{2,1,0:T(1,128)} %bitcast.1), calls=%async_computation | async-start | bytes 65536 | tf_op jit(solution)/shard_map/all_to_all | solution.py:27
  15.2 0.0 copy-start
  15.2 1.1 copy-done
  16.3 0.6 spread.1.rows
  17.0 7.4 %all-to-all-done.ids = s32[64,1,16]{2,1,0:T(1,128)S(1)} async-done(((s32[64,1,16]{2,1,0:T(1,128)}), s32[64,1,16]{2,1,0:T(1,128)S(1)}, u32[]{:S(2)}, u32[]{:S(2)}) %all-to-all-start) | async-done | bytes 4128 | tf_op jit(solution)/shard_map/all_to_all | solution.py:27
  24.4 2.8 %serve.1 = (f32[1600,128]{1,0:T(8,128)}, f32[32,512]{1,0:T(8,128)S(1)}) custom-call(s32[64,1,16]{2,1,0:T(1,128)S(1)} %all-to-all-done.ids, s32[1]{0:T(128)} %bitcast.2.here, f32[512,4,128]{2,1,0:T(4,128)S(1)} %spread.1.rows), custom_call_target="tpu_custom_call" | custom-call | tf_op jit(solution)/shard_map/serve/pallas_call | solution.py:118
  27.3 4.8 %all-to-all-start.1 = ((f32[64,25,1,128]{3,2,1,0:T(1,128)}), f32[64,25,1,128]{3,2,1,0:T(1,128)S(1)}, u32[]{:S(2)}, u32[]{:S(2)}) async-start(f32[64,25,1,128]{3,2,1,0:T(1,128)} %bitcast.49), calls=%async_computation.1 | async-start | bytes 1638400 | tf_op jit(solution)/shard_map/all_to_all | solution.py:27
  32.1 0.1 iota_compare_fusion
  32.2 0.1 slice.50
  32.3 0.1 copy.28
  32.3 0.2 select_reduce_fusion
  32.5 0.1 reshape.323
  32.6 0.1 reshape.322
  32.7 0.2 slice_reduce_fusion
  32.9 0.1 pad_add_fusion.1.refs_0_
  33.0 2.5 %collective-permute-start.3 = (s32[1,544]{1,0:T(1,128)S(1)}, s32[1,544]{1,0:T(1,128)S(1)}, u32[]{:S(2)}, u32[]{:S(2)}) collective-permute-start(s32[1,544]{1,0:T(1,128)S(1)} %pad_add_fusion.1.refs_0_), channel_id=1, source_target_pairs={{0,3},{1,0},{2,1},{3,2},{4,7},{5,4},{6,5},{7,6},{8,11},{9,8},{10,9... | collective-permute-start | bytes 6536 | tf_op jit(solution)/shard_map/ppermute | solution.py:23
  35.5 0.5 collective-permute-start.4
  36.0 0.6 collective-permute-start.5
  36.6 6.2 %collective-permute-start.2 = (f32[8,512]{1,0:T(8,128)S(1)}, f32[8,512]{1,0:T(8,128)S(1)}, u32[]{:S(2)}, u32[]{:S(2)}) collective-permute-start(f32[8,512]{1,0:T(8,128)S(1)} %get-tuple-element.31), channel_id=1, source_target_pairs={{0,244},{4,248},{8,252},{12,0},{16,4},{20,8},{24,12},{28,16},{32,2... | collective-permute-start | bytes 49160 | tf_op jit(solution)/shard_map/ppermute | solution.py:23
  42.8 1.2 collective-permute-start.1
  44.0 0.4 collective-permute-start
  44.4 0.1 compare_select_fusion.2.slots
  44.6 3.5 %prep.1 = (bf16[2048,640]{1,0:T(8,128)(2,1)}, bf16[544,2048]{1,0:T(8,128)(2,1)}, f32[2,8,512]{2,1,0:T(8,128)}, f32[2,512,128]{2,1,0:T(8,128)}) custom-call(s32[1,2048]{1,0:T(1,128)S(1)} %compare_select_fusion.2.slots, s32[1,2048]{1,0:T(1,128)S(1)} %reshape_squeeze.10.negs), custom_call_target="tpu_custom_call" | custom-call | tf_op jit(solution)/shard_map/prep/pallas_call | solution.py:161
  48.1 2.3 %hot.1.ahead = bf16[512,2176]{1,0:T(8,128)(2,1)} custom-call(s32[1]{0:T(128)} %bitcast.me, s32[1,544]{1,0:T(1,128)S(1)} %pad_add_fusion.1.refs_0_, s32[1,544]{1,0:T(1,128)S(1)} %collective-permute-done.3.refs_1_, s32[1,544]{1,0:T(1,128)S(1)} %collective-permute-done.4.refs_2_, s32[1,544]{1,0:T(1,128)S(1)} %collective-permute-done.5.refs_3_), custom_call_target="tpu_custom_call" | custom-call | tf_op jit(solution)/shard_map/hot/pallas_call | solution.py:338
  50.4 2.5 %collective-permute-done.2 = f32[8,512]{1,0:T(8,128)S(1)} collective-permute-done((f32[8,512]{1,0:T(8,128)S(1)}, f32[8,512]{1,0:T(8,128)S(1)}, u32[]{:S(2)}, u32[]{:S(2)}) %collective-permute-start.2) | collective-permute-done | bytes 16416 | tf_op jit(solution)/shard_map/ppermute | solution.py:23
  52.9 0.2 collective-permute-done
  53.1 2.6 %all-to-all-done.1 = f32[64,25,1,128]{3,2,1,0:T(1,128)S(1)} async-done(((f32[64,25,1,128]{3,2,1,0:T(1,128)}), f32[64,25,1,128]{3,2,1,0:T(1,128)S(1)}, u32[]{:S(2)}, u32[]{:S(2)}) %all-to-all-start.1) | async-done | bytes 819232 | tf_op jit(solution)/shard_map/all_to_all | solution.py:27
  55.7 14.0 %grads.1 = (f32[1792,128]{1,0:T(8,128)}, f32[32,512]{1,0:T(8,128)S(1)}) custom-call(f32[1600,128]{1,0:T(8,128)S(1)} %bitcast.40, f32[32,512]{1,0:T(8,128)S(1)} %pad_maximum_fusion.tails, bf16[2048,640]{1,0:T(8,128)(2,1)} %get-tuple-element.14.by_edge, bf16[544,2048]{1,0:T(8,128)(2,1)} %get-tuple-element.15.by_slot, f32[2,8,512]{2,1,0:T(8,128)S(1)} %copy-done.3, ...), custom_call_target="tpu_custom_call" | custom-call | tf_op jit(solution)/shard_map/grads/pallas_call | solution.py:298
  69.7 9.1 %all-to-all-start.2 = ((f32[256,7,1,128]{3,2,1,0:T(1,128)}), f32[256,7,1,128]{3,2,1,0:T(1,128)S(1)}, u32[]{:S(2)}, u32[]{:S(2)}) async-start(f32[256,7,1,128]{3,2,1,0:T(1,128)} %bitcast.48), calls=%async_computation.2 | async-start | bytes 1835008 | tf_op jit(solution)/shard_map/all_to_all | solution.py:27
  78.9 0.0 copy-start.4
  79.0 0.1 constant_dynamic-slice_fusion.3
  79.1 1.4 %collective-permute-start.8 = (f32[32,128]{1,0:T(8,128)S(1)}, f32[32,128]{1,0:T(8,128)S(1)}, u32[]{:S(2)}, u32[]{:S(2)}) collective-permute-start(f32[32,128]{1,0:T(8,128)S(1)} %bitcast.55), channel_id=1, source_target_pairs={{0,1},{1,2},{2,3},{3,0},{4,5},{5,6},{6,7},{7,4},{8,9},{9,10},{10,1... | collective-permute-start | bytes 49160 | tf_op jit(solution)/shard_map/ppermute | solution.py:23
  80.5 2.4 %collective-permute-start.7 = (f32[32,128]{1,0:T(8,128)S(1)}, f32[32,128]{1,0:T(8,128)S(1)}, u32[]{:S(2)}, u32[]{:S(2)}) collective-permute-start(f32[32,128]{1,0:T(8,128)S(1)} %bitcast.52), channel_id=1, source_target_pairs={{0,2},{1,3},{2,0},{3,1},{4,6},{5,7},{6,4},{7,5},{8,10},{9,11},{10,... | collective-permute-start | bytes 49160 | tf_op jit(solution)/shard_map/ppermute | solution.py:23
  82.9 1.2 collective-permute-start.6
  84.1 0.8 collective-permute-done.7
  84.9 1.1 collective-permute-done.6
  86.0 4.4 %collective-permute-start.11 = (f32[4,8,128]{2,1,0:T(8,128)S(1)}, f32[4,8,128]{2,1,0:T(8,128)S(1)}, u32[]{:S(2)}, u32[]{:S(2)}) collective-permute-start(f32[4,8,128]{2,1,0:T(8,128)S(1)} %get-tuple-element.23), channel_id=1, source_target_pairs={{0,12},{4,16},{8,20},{12,24},{16,28},{20,32},{24,36},{28,40},{32,4... | collective-permute-start | bytes 49160 | tf_op jit(solution)/shard_map/ppermute | solution.py:23
  90.5 1.2 collective-permute-start.10
  91.7 13.5 %collective-permute-done.11 = f32[4,8,128]{2,1,0:T(8,128)S(1)} collective-permute-done((f32[4,8,128]{2,1,0:T(8,128)S(1)}, f32[4,8,128]{2,1,0:T(8,128)S(1)}, u32[]{:S(2)}, u32[]{:S(2)}) %collective-permute-start.11) | collective-permute-done | bytes 16416 | tf_op jit(solution)/shard_map/ppermute | solution.py:23
  105.3 3.7 %all-to-all-done.2 = f32[256,7,1,128]{3,2,1,0:T(1,128)S(1)} async-done(((f32[256,7,1,128]{3,2,1,0:T(1,128)}), f32[256,7,1,128]{3,2,1,0:T(1,128)S(1)}, u32[]{:S(2)}, u32[]{:S(2)}) %all-to-all-start.2) | async-done | bytes 917536 | tf_op jit(solution)/shard_map/all_to_all | solution.py:27
  109.0 2.8 %owner.1.own = f32[104,512]{1,0:T(8,128)S(1)} custom-call(f32[1792,128]{1,0:T(8,128)S(1)} %bitcast.39, f32[128,128]{1,0:T(8,128)S(1)} %bitcast.46, bf16[512,2176]{1,0:T(8,128)(2,1)} %hot.1.ahead), custom_call_target="tpu_custom_call" | custom-call | tf_op jit(solution)/shard_map/owner/pallas_call | solution.py:377
  111.8 0.4 collective-permute-start.12
  112.2 1.8 %collective-permute-start.13 = (f32[104,512]{1,0:T(8,128)S(1)}, f32[104,512]{1,0:T(8,128)S(1)}, u32[]{:S(2)}, u32[]{:S(2)}) collective-permute-start(f32[104,512]{1,0:T(8,128)S(1)} %owner.1.own), channel_id=1, source_target_pairs={{0,2},{1,3},{2,0},{3,1},{4,6},{5,7},{6,4},{7,5},{8,10},{9,11},{10,... | collective-permute-start | bytes 638984 | tf_op jit(solution)/shard_map/ppermute | solution.py:23
  113.9 0.7 collective-permute-start.14
  114.7 9.2 %collective-permute-done.12.next1 = f32[104,512]{1,0:T(8,128)S(1)} collective-permute-done((f32[104,512]{1,0:T(8,128)S(1)}, f32[104,512]{1,0:T(8,128)S(1)}, u32[]{:S(2)}, u32[]{:S(2)}) %collective-permute-start.12) | collective-permute-done | bytes 213024 | tf_op jit(solution)/shard_map/ppermute | solution.py:23
  123.9 0.9 collective-permute-done.14.next3
  124.8 1.7 %update.1 = (f32[400,512]{1,0:T(8,128)}, f32[1,512]{1,0:T(1,128)}) custom-call(s32[1]{0:T(128)} %bitcast.me, f32[104,512]{1,0:T(8,128)S(1)} %owner.1.own, f32[104,512]{1,0:T(8,128)S(1)} %collective-permute-done.12.next1, f32[104,512]{1,0:T(8,128)S(1)} %collective-permute-done.13.next2, f32[104,512]{1,0:T(8,128)S(1)} %collective-permute-done.14.next3, ...), custom_call_target="tpu_custom_call" | custom-call | tf_op jit(solution)/shard_map/update/pallas_call | solution.py:418
  (33 shorter events, 0.2 us)
Async XLA Ops:
  2.0 22.4 %all-to-all-start = ((s32[64,1,16]{2,1,0:T(1,128)}), s32[64,1,16]{2,1,0:T(1,128)S(1)}, u32[]{:S(2)}, u32[]{:S(2)}) async-start(s32[64,1,16]{2,1,0:T(1,128)} %bitcast.1), calls=%async_computation | async-start | bytes 65536 | tf_op jit(solution)/shard_map/all_to_all | solution.py:27
  15.2 1.1 copy-start
  16.3 15.7 %copy-start.6 = (s32[1,1,2,512]{3,2,1,0:T(2,128)S(1)}, s32[1,1,2,512]{3,2,1,0:T(2,128)}, u32[]{:S(2)}) copy-start(s32[1,1,2,512]{3,2,1,0:T(2,128)} %param.10) | copy-start | bytes 12292
  16.3 15.7 %copy-start.7 = (s32[1,1,2,512]{3,2,1,0:T(2,128)S(1)}, s32[1,1,2,512]{3,2,1,0:T(2,128)}, u32[]{:S(2)}) copy-start(s32[1,1,2,512]{3,2,1,0:T(2,128)} %param.9) | copy-start | bytes 12292
  16.3 28.2 %copy-start.5 = (s32[1,1,2,2,512]{4,3,2,1,0:T(2,128)S(1)}, s32[1,1,2,2,512]{4,3,2,1,0:T(2,128)}, u32[]{:S(2)}) copy-start(s32[1,1,2,2,512]{4,3,2,1,0:T(2,128)} %param.11) | copy-start | bytes 24580
  27.3 28.5 %all-to-all-start.1 = ((f32[64,25,1,128]{3,2,1,0:T(1,128)}), f32[64,25,1,128]{3,2,1,0:T(1,128)S(1)}, u32[]{:S(2)}, u32[]{:S(2)}) async-start(f32[64,25,1,128]{3,2,1,0:T(1,128)} %bitcast.49), calls=%async_computation.1 | async-start | bytes 1638400 | tf_op jit(solution)/shard_map/all_to_all | solution.py:27
  33.0 11.0 %collective-permute-start.3 = (s32[1,544]{1,0:T(1,128)S(1)}, s32[1,544]{1,0:T(1,128)S(1)}, u32[]{:S(2)}, u32[]{:S(2)}) collective-permute-start(s32[1,544]{1,0:T(1,128)S(1)} %pad_add_fusion.1.refs_0_), channel_id=1, source_target_pairs={{0,3},{1,0},{2,1},{3,2},{4,7},{5,4},{6,5},{7,6},{8,11},{9,8},{10,9... | collective-permute-start | bytes 6536 | tf_op jit(solution)/shard_map/ppermute | solution.py:23
  35.5 12.6 %collective-permute-start.4 = (s32[1,544]{1,0:T(1,128)S(1)}, s32[1,544]{1,0:T(1,128)S(1)}, u32[]{:S(2)}, u32[]{:S(2)}) collective-permute-start(s32[1,544]{1,0:T(1,128)S(1)} %pad_add_fusion.1.refs_0_), channel_id=1, source_target_pairs={{0,2},{1,3},{2,0},{3,1},{4,6},{5,7},{6,4},{7,5},{8,10},{9,11},{10,... | collective-permute-start | bytes 6536 | tf_op jit(solution)/shard_map/ppermute | solution.py:23
  36.0 12.1 %collective-permute-start.5 = (s32[1,544]{1,0:T(1,128)S(1)}, s32[1,544]{1,0:T(1,128)S(1)}, u32[]{:S(2)}, u32[]{:S(2)}) collective-permute-start(s32[1,544]{1,0:T(1,128)S(1)} %pad_add_fusion.1.refs_0_), channel_id=1, source_target_pairs={{0,1},{1,2},{2,3},{3,0},{4,5},{5,6},{6,7},{7,4},{8,9},{9,10},{10,1... | collective-permute-start | bytes 6536 | tf_op jit(solution)/shard_map/ppermute | solution.py:23
  36.6 16.3 %collective-permute-start.2 = (f32[8,512]{1,0:T(8,128)S(1)}, f32[8,512]{1,0:T(8,128)S(1)}, u32[]{:S(2)}, u32[]{:S(2)}) collective-permute-start(f32[8,512]{1,0:T(8,128)S(1)} %get-tuple-element.31), channel_id=1, source_target_pairs={{0,244},{4,248},{8,252},{12,0},{16,4},{20,8},{24,12},{28,16},{32,2... | collective-permute-start | bytes 49160 | tf_op jit(solution)/shard_map/ppermute | solution.py:23
  42.8 10.1 %collective-permute-start.1 = (f32[8,512]{1,0:T(8,128)S(1)}, f32[8,512]{1,0:T(8,128)S(1)}, u32[]{:S(2)}, u32[]{:S(2)}) collective-permute-start(f32[8,512]{1,0:T(8,128)S(1)} %get-tuple-element.32), channel_id=1, source_target_pairs={{0,248},{4,252},{8,0},{12,4},{16,8},{20,12},{24,16},{28,20},{32,24... | collective-permute-start | bytes 49160 | tf_op jit(solution)/shard_map/ppermute | solution.py:23
  44.0 9.1 %collective-permute-start = (f32[8,512]{1,0:T(8,128)S(1)}, f32[8,512]{1,0:T(8,128)S(1)}, u32[]{:S(2)}, u32[]{:S(2)}) collective-permute-start(f32[8,512]{1,0:T(8,128)S(1)} %get-tuple-element.33), channel_id=1, source_target_pairs={{0,252},{4,0},{8,4},{12,8},{16,12},{20,16},{24,20},{28,24},{32,28}... | collective-permute-start | bytes 49160 | tf_op jit(solution)/shard_map/ppermute | solution.py:23
  48.0 7.7 %copy-start.2 = (f32[2,512,128]{2,1,0:T(8,128)S(1)}, f32[2,512,128]{2,1,0:T(8,128)}, u32[]{:S(2)}) copy-start(f32[2,512,128]{2,1,0:T(8,128)} %get-tuple-element.17.count_col) | copy-start | bytes 1572868
  48.0 7.7 %copy-start.3 = (f32[2,8,512]{2,1,0:T(8,128)S(1)}, f32[2,8,512]{2,1,0:T(8,128)}, u32[]{:S(2)}) copy-start(f32[2,8,512]{2,1,0:T(8,128)} %get-tuple-element.16.count_row) | copy-start | bytes 98308
  69.7 39.3 %all-to-all-start.2 = ((f32[256,7,1,128]{3,2,1,0:T(1,128)}), f32[256,7,1,128]{3,2,1,0:T(1,128)S(1)}, u32[]{:S(2)}, u32[]{:S(2)}) async-start(f32[256,7,1,128]{3,2,1,0:T(1,128)} %bitcast.48), calls=%async_computation.2 | async-start | bytes 1835008 | tf_op jit(solution)/shard_map/all_to_all | solution.py:27
  78.9 46.0 %copy-start.1 = (f32[512,400]{0,1:T(8,128)S(1)}, f32[512,400]{0,1:T(8,128)}, u32[]{:S(2)}) copy-start(f32[512,400]{0,1:T(8,128)} %param.6) | copy-start | bytes 2457604
  78.9 46.0 %copy-start.4 = (f32[512]{0:T(512)S(1)}, f32[512]{0:T(512)}, u32[]{:S(2)}) copy-start(f32[512]{0:T(512)} %param.7) | copy-start | bytes 6148
  79.1 5.0 %collective-permute-start.8 = (f32[32,128]{1,0:T(8,128)S(1)}, f32[32,128]{1,0:T(8,128)S(1)}, u32[]{:S(2)}, u32[]{:S(2)}) collective-permute-start(f32[32,128]{1,0:T(8,128)S(1)} %bitcast.55), channel_id=1, source_target_pairs={{0,1},{1,2},{2,3},{3,0},{4,5},{5,6},{6,7},{7,4},{8,9},{9,10},{10,1... | collective-permute-start | bytes 49160 | tf_op jit(solution)/shard_map/ppermute | solution.py:23
  80.5 4.4 %collective-permute-start.7 = (f32[32,128]{1,0:T(8,128)S(1)}, f32[32,128]{1,0:T(8,128)S(1)}, u32[]{:S(2)}, u32[]{:S(2)}) collective-permute-start(f32[32,128]{1,0:T(8,128)S(1)} %bitcast.52), channel_id=1, source_target_pairs={{0,2},{1,3},{2,0},{3,1},{4,6},{5,7},{6,4},{7,5},{8,10},{9,11},{10,... | collective-permute-start | bytes 49160 | tf_op jit(solution)/shard_map/ppermute | solution.py:23
  82.9 3.1 %collective-permute-start.6 = (f32[32,128]{1,0:T(8,128)S(1)}, f32[32,128]{1,0:T(8,128)S(1)}, u32[]{:S(2)}, u32[]{:S(2)}) collective-permute-start(f32[32,128]{1,0:T(8,128)S(1)} %bitcast.51), channel_id=1, source_target_pairs={{0,3},{1,0},{2,1},{3,2},{4,7},{5,4},{6,5},{7,6},{8,11},{9,8},{10,9... | collective-permute-start | bytes 49160 | tf_op jit(solution)/shard_map/ppermute | solution.py:23
  86.0 19.2 %collective-permute-start.11 = (f32[4,8,128]{2,1,0:T(8,128)S(1)}, f32[4,8,128]{2,1,0:T(8,128)S(1)}, u32[]{:S(2)}, u32[]{:S(2)}) collective-permute-start(f32[4,8,128]{2,1,0:T(8,128)S(1)} %get-tuple-element.23), channel_id=1, source_target_pairs={{0,12},{4,16},{8,20},{12,24},{16,28},{20,32},{24,36},{28,40},{32,4... | collective-permute-start | bytes 49160 | tf_op jit(solution)/shard_map/ppermute | solution.py:23
  90.5 14.8 %collective-permute-start.10 = (f32[4,8,128]{2,1,0:T(8,128)S(1)}, f32[4,8,128]{2,1,0:T(8,128)S(1)}, u32[]{:S(2)}, u32[]{:S(2)}) collective-permute-start(f32[4,8,128]{2,1,0:T(8,128)S(1)} %get-tuple-element.24), channel_id=1, source_target_pairs={{0,8},{4,12},{8,16},{12,20},{16,24},{20,28},{24,32},{28,36},{32,40... | collective-permute-start | bytes 49160 | tf_op jit(solution)/shard_map/ppermute | solution.py:23
  91.7 13.5 %collective-permute-start.9 = (f32[4,8,128]{2,1,0:T(8,128)S(1)}, f32[4,8,128]{2,1,0:T(8,128)S(1)}, u32[]{:S(2)}, u32[]{:S(2)}) collective-permute-start(f32[4,8,128]{2,1,0:T(8,128)S(1)} %get-tuple-element.25), channel_id=1, source_target_pairs={{0,4},{4,8},{8,12},{12,16},{16,20},{20,24},{24,28},{28,32},{32,36}... | collective-permute-start | bytes 49160 | tf_op jit(solution)/shard_map/ppermute | solution.py:23
  111.8 12.1 %collective-permute-start.12 = (f32[104,512]{1,0:T(8,128)S(1)}, f32[104,512]{1,0:T(8,128)S(1)}, u32[]{:S(2)}, u32[]{:S(2)}) collective-permute-start(f32[104,512]{1,0:T(8,128)S(1)} %owner.1.own), channel_id=1, source_target_pairs={{0,1},{1,2},{2,3},{3,0},{4,5},{5,6},{6,7},{7,4},{8,9},{9,10},{10,1... | collective-permute-start | bytes 638984 | tf_op jit(solution)/shard_map/ppermute | solution.py:23
  112.2 11.7 %collective-permute-start.13 = (f32[104,512]{1,0:T(8,128)S(1)}, f32[104,512]{1,0:T(8,128)S(1)}, u32[]{:S(2)}, u32[]{:S(2)}) collective-permute-start(f32[104,512]{1,0:T(8,128)S(1)} %owner.1.own), channel_id=1, source_target_pairs={{0,2},{1,3},{2,0},{3,1},{4,6},{5,7},{6,4},{7,5},{8,10},{9,11},{10,... | collective-permute-start | bytes 638984 | tf_op jit(solution)/shard_map/ppermute | solution.py:23
  113.9 10.9 %collective-permute-start.14 = (f32[104,512]{1,0:T(8,128)S(1)}, f32[104,512]{1,0:T(8,128)S(1)}, u32[]{:S(2)}, u32[]{:S(2)}) collective-permute-start(f32[104,512]{1,0:T(8,128)S(1)} %owner.1.own), channel_id=1, source_target_pairs={{0,3},{1,0},{2,1},{3,2},{4,7},{5,4},{6,5},{7,6},{8,11},{9,8},{10,9... | collective-permute-start | bytes 638984 | tf_op jit(solution)/shard_map/ppermute | solution.py:23

commit v6 on v5

--- a/solution.py
+++ b/solution.py
@@ -142,10 +142,13 @@
         by_slot[:, p * edges : (p + 1) * edges] = jnp.where(down == row, one, zero).astype(bf16)
         column = jnp.broadcast_to(row, (LANES, edges)).T
         across = lax.broadcasted_iota(jnp.int32, (edges, LANES), 1)
-        for c in range(padded // LANES):
-            by_edge[p * edges : (p + 1) * edges, c * LANES : (c + 1) * LANES] = jnp.where(
-                across + c * LANES == column, one, zero
-            ).astype(bf16)
+        blocks = padded // LANES
+        for c in range(blocks):
+            hit = across + c * LANES == column
+            if c == blocks - 1:
+                count = HEAVY * 8
+                hit = hit | ((across >= count) & (across + (c * LANES - count) == column))
+            by_edge[p * edges : (p + 1) * edges, c * LANES : (c + 1) * LANES] = jnp.where(hit, one, zero).astype(bf16)
         neg = negs[:, p * edges : (p + 1) * edges]
         down = lax.broadcasted_iota(jnp.int32, (edges, edges), 0)
         drawn = jnp.where(down == neg, one, zero).astype(bf16)
@@ -187,7 +190,7 @@
 
 
 def grads_body(heads, tails, by_edge, by_slot, count_row, count_col, ahead, out_heads, out_tails,
-               high, low, d_high, d_low, edge_part, slot_part, summed, packed, in_sems, out_sems):
+               high, low, extra, d_high, d_low, edge_part, slot_part, summed, packed, in_sems, out_sems):
     live = by_slot.shape[0]
     head_count = live - tails.shape[0]
     owners = head_count // 8
@@ -213,54 +216,40 @@
                 block = pltpu.roll(ends, (LANES - 16 * k) % LANES, 1) if k else ends
                 block = jnp.where(lanes_of(block.shape) < 16, block, 0.0)
             high[span, lanes], low[span, lanes] = halves(block)
-    high[head_count:live, :], low[head_count:live, :] = halves(tails[...])
-    high[live:, :] = jnp.zeros((padded - live, width), bf16)
-    low[live:, :] = jnp.zeros((padded - live, width), bf16)
+    pieces = list(halves(tails[...]))
+    pieces.append(jnp.zeros((padded - head_count - 2 * tails.shape[0], width), bf16))
+    extra[...] = jnp.concatenate(pieces, axis=0)
 
     def gathered(b):
         picks = []
         for side in range(2):
             at = (2 * b + side) * edges
             loads[2 * b + side].wait()
-            chosen = edge_part[at : at + edges, :]
-            picks.append((mm(chosen, high[...]).astype(bf16), mm(chosen, low[...]).astype(bf16)))
+            chosen = edge_part[at : at + edges, :head_count]
+            rest = edge_part[at : at + edges, head_count:]
+            picks.append(mm(chosen, high[...]) + mm(chosen, low[...]) + mm(rest, extra[...]))
         return picks
-
-    def scored(picks):
-        (s_high, s_low), (t_high, t_low) = picks
-        return mm_nt(s_high, t_high) + mm_nt(s_high, t_low) + mm_nt(s_low, t_high)
 
     def gained(b, scores):
         decay = jnp.exp2(jnp.minimum(scores * -LOG2E, 126.0))
         weight = 1.0 / (1.0 + decay)
         counts = count_row[b, 0:1, :] + jnp.concatenate([count_col[b]] * (edges // LANES), axis=1)
-        gain = weight * counts
-        eye = lanes_of((LANES, LANES)) == lax.broadcasted_iota(jnp.int32, (LANES, LANES), 0)
-        bands = []
-        for i in range(edges // LANES):
-            span = slice(i * LANES, (i + 1) * LANES)
-            missing = jnp.where(eye, decay[span, span] * weight[span, span], 0.0)
-            row = [gain[span, : i * LANES], gain[span, span] - missing, gain[span, (i + 1) * LANES :]]
-            bands.append(jnp.concatenate([part for part in row if part.shape[1]], axis=1))
-        return jnp.concatenate(bands, axis=0)
-
-    def pulled(at, g_high, g_low, high_rows, low_rows):
-        moved = mm(g_high, high_rows) + mm(g_high, low_rows) + mm(g_low, high_rows)
+        return (weight * counts).astype(bf16)
+
+    def pulled(at, gain, pull, rows_high, rows_low, rows):
+        moved = mm(gain, rows_high) + mm(gain, rows_low) + pull * rows
         d_high[at : at + edges, :], d_low[at : at + edges, :] = halves(moved)
 
-    picks = gathered(0)
-    scores = scored(picks)
     for b in range(batches):
-        if b + 1 < batches:
-            next_picks = gathered(b + 1)
-        gain = gained(b, scores)
-        if b + 1 < batches:
-            next_scores = scored(next_picks)
-        g_high, g_low = halves(gain)
-        pulled(2 * b * edges, g_high, g_low, *picks[1])
-        pulled((2 * b + 1) * edges, g_high.T, g_low.T, *picks[0])
-        if b + 1 < batches:
-            picks, scores = next_picks, next_scores
+        s_rows, t_rows = gathered(b)
+        s_high, s_low = halves(s_rows)
+        t_high, t_low = halves(t_rows)
+        positive = jnp.sum(s_rows * t_rows, axis=1, keepdims=True)
+        falling = jnp.exp(-jnp.abs(positive))
+        pull = -jnp.where(positive >= 0, falling, 1.0) / (1.0 + falling)
+        gain = gained(b, mm_nt(s_high, t_high))
+        pulled(2 * b * edges, gain, pull, t_high, t_low, t_rows)
+        pulled((2 * b + 1) * edges, gain.T, pull, s_high, s_low, s_rows)
     last.wait()
     stores = []
     block = 2 * LANES
@@ -301,8 +290,9 @@
         out_specs=[HBM, VMEM],
         out_shape=[pltpu.HBM(shape, f32), jax.ShapeDtypeStruct(tails.shape, f32)],
         scratch_shapes=[
-            pltpu.VMEM((padded, width), bf16),
-            pltpu.VMEM((padded, width), bf16),
+            pltpu.VMEM((live - tails.shape[0], width), bf16),
+            pltpu.VMEM((live - tails.shape[0], width), bf16),
+            pltpu.VMEM((padded - live + tails.shape[0], width), bf16),
             pltpu.VMEM((total, width), bf16),
             pltpu.VMEM((total, width), bf16),
             pltpu.VMEM(by_edge.shape, bf16),

time: 127 us -> 125 us (0.984)
  Pallas kernels: 27.7 us -> 25.3 us
    pallas_call x1, Pallas kernels: 14 us -> 11.5 us  [grads(): pl.pallas_call(grads_body, in_specs=[VMEM, VMEM, HBM, HBM, VMEM, VMEM, HB...]
where the time goes in v6:
time: 125 us; the launch traced here: 124 us
  starting transfers between devices  52.4 us (42%)
  waiting for transfers between devices  41.7 us (33%)
  Pallas kernels  25.3 us (20%)
  local copies, waits for them, and re-layouts  3.25 us (3%)
    ppermute x15, waiting for transfers between devices, passed_along(): return lax.ppermute(value, axis, pairs)  27.9 us
    all_to_all x3, starting transfers between devices, exchanged(): return lax.all_to_all(value, axis, 0, 0, tiled=True)  27 us
    ppermute x15, starting transfers between devices, passed_along(): return lax.ppermute(value, axis, pairs)  25.4 us
    all_to_all x3, waiting for transfers between devices, exchanged(): return lax.all_to_all(value, axis, 0, 0, tiled=True)  13.8 us
    pallas_call x1, Pallas kernels, grads(): pl.pallas_call(grads_body, in_specs=[VMEM, VMEM, HBM, HBM, VMEM, VMEM, HB...  11.5 us
    pallas_call x1, Pallas kernels, prep(): pl.pallas_call(prep_body, out_shape=[pltpu.HBM((total, padded), bf16), pl...  3.55 us
    pallas_call x1, Pallas kernels, serve(): pl.pallas_call(serve_body, in_specs=[SMEM, SMEM, VMEM], out_specs=[HBM, V...  2.83 us
    pallas_call x1, Pallas kernels, owner(): pl.pallas_call(owner_body, in_specs=[VMEM, VMEM, HBM], out_specs=VMEM, ou...  2.79 us
  transfers between devices with their start and end apart: 18, of which 10 were waited for; matrix products, arithmetic and copies ran while one was open for 1% of the time, Pallas kernels for 5%

profile of v6, /device:TPU:1, one launch (start us, length us, event | category | flops | bytes accessed | tf_op | source)
XLA Modules:
  0.0 124.2 jit_solution(14476839554723831716)
XLA Ops:
  0.6 1.4 %copy.25 = s32[1,1,64,16]{3,2,1,0:T(8,128)} copy(s32[1,1,64,16]{2,3,1,0:T(8,128)} %param.8) | data formatting | bytes 8192 | tf_op args[2]
  2.0 13.1 %all-to-all-start = ((s32[64,1,16]{2,1,0:T(1,128)}), s32[64,1,16]{2,1,0:T(1,128)S(1)}, u32[]{:S(2)}, u32[]{:S(2)}) async-start(s32[64,1,16]{2,1,0:T(1,128)} %bitcast.1), calls=%async_computation | async-start | bytes 65536 | tf_op jit(solution)/shard_map/all_to_all | solution.py:27
  15.2 0.0 copy-start
  15.2 1.1 copy-done
  16.3 0.6 spread.1.rows
  17.0 7.4 %all-to-all-done.ids = s32[64,1,16]{2,1,0:T(1,128)S(1)} async-done(((s32[64,1,16]{2,1,0:T(1,128)}), s32[64,1,16]{2,1,0:T(1,128)S(1)}, u32[]{:S(2)}, u32[]{:S(2)}) %all-to-all-start) | async-done | bytes 4128 | tf_op jit(solution)/shard_map/all_to_all | solution.py:27
  24.4 2.8 %serve.1 = (f32[1600,128]{1,0:T(8,128)}, f32[32,512]{1,0:T(8,128)S(1)}) custom-call(s32[64,1,16]{2,1,0:T(1,128)S(1)} %all-to-all-done.ids, s32[1]{0:T(128)} %bitcast.2.here, f32[512,4,128]{2,1,0:T(4,128)S(1)} %spread.1.rows), custom_call_target="tpu_custom_call" | custom-call | tf_op jit(solution)/shard_map/serve/pallas_call | solution.py:118
  27.3 4.8 %all-to-all-start.1 = ((f32[64,25,1,128]{3,2,1,0:T(1,128)}), f32[64,25,1,128]{3,2,1,0:T(1,128)S(1)}, u32[]{:S(2)}, u32[]{:S(2)}) async-start(f32[64,25,1,128]{3,2,1,0:T(1,128)} %bitcast.49), calls=%async_computation.1 | async-start | bytes 1638400 | tf_op jit(solution)/shard_map/all_to_all | solution.py:27
  32.1 0.1 iota_compare_fusion
  32.2 0.1 slice.50
  32.3 0.1 copy.28
  32.3 0.2 select_reduce_fusion
  32.5 0.1 reshape.323
  32.6 0.1 reshape.322
  32.7 0.2 slice_reduce_fusion
  32.9 0.1 pad_add_fusion.1.refs_0_
  33.0 2.5 %collective-permute-start.3 = (s32[1,544]{1,0:T(1,128)S(1)}, s32[1,544]{1,0:T(1,128)S(1)}, u32[]{:S(2)}, u32[]{:S(2)}) collective-permute-start(s32[1,544]{1,0:T(1,128)S(1)} %pad_add_fusion.1.refs_0_), channel_id=1, source_target_pairs={{0,3},{1,0},{2,1},{3,2},{4,7},{5,4},{6,5},{7,6},{8,11},{9,8},{10,9... | collective-permute-start | bytes 6536 | tf_op jit(solution)/shard_map/ppermute | solution.py:23
  35.5 0.5 collective-permute-start.4
  36.0 0.6 collective-permute-start.5
  36.6 6.2 %collective-permute-start.2 = (f32[8,512]{1,0:T(8,128)S(1)}, f32[8,512]{1,0:T(8,128)S(1)}, u32[]{:S(2)}, u32[]{:S(2)}) collective-permute-start(f32[8,512]{1,0:T(8,128)S(1)} %get-tuple-element.31), channel_id=1, source_target_pairs={{0,244},{4,248},{8,252},{12,0},{16,4},{20,8},{24,12},{28,16},{32,2... | collective-permute-start | bytes 49160 | tf_op jit(solution)/shard_map/ppermute | solution.py:23
  42.8 1.2 collective-permute-start.1
  44.0 0.4 collective-permute-start
  44.4 0.1 compare_select_fusion.2.slots
  44.6 3.5 %prep.1 = (bf16[2048,640]{1,0:T(8,128)(2,1)}, bf16[544,2048]{1,0:T(8,128)(2,1)}, f32[2,8,512]{2,1,0:T(8,128)}, f32[2,512,128]{2,1,0:T(8,128)}) custom-call(s32[1,2048]{1,0:T(1,128)S(1)} %compare_select_fusion.2.slots, s32[1,2048]{1,0:T(1,128)S(1)} %reshape_squeeze.10.negs), custom_call_target="tpu_custom_call" | custom-call | tf_op jit(solution)/shard_map/prep/pallas_call | solution.py:164
  48.1 2.3 %hot.1.ahead = bf16[512,2176]{1,0:T(8,128)(2,1)} custom-call(s32[1]{0:T(128)} %bitcast.me, s32[1,544]{1,0:T(1,128)S(1)} %pad_add_fusion.1.refs_0_, s32[1,544]{1,0:T(1,128)S(1)} %collective-permute-done.3.refs_1_, s32[1,544]{1,0:T(1,128)S(1)} %collective-permute-done.4.refs_2_, s32[1,544]{1,0:T(1,128)S(1)} %collective-permute-done.5.refs_3_), custom_call_target="tpu_custom_call" | custom-call | tf_op jit(solution)/shard_map/hot/pallas_call | solution.py:328
  50.5 2.4 %collective-permute-done.2 = f32[8,512]{1,0:T(8,128)S(1)} collective-permute-done((f32[8,512]{1,0:T(8,128)S(1)}, f32[8,512]{1,0:T(8,128)S(1)}, u32[]{:S(2)}, u32[]{:S(2)}) %collective-permute-start.2) | collective-permute-done | bytes 16416 | tf_op jit(solution)/shard_map/ppermute | solution.py:23
  52.9 0.2 collective-permute-done
  53.1 2.6 %all-to-all-done.1 = f32[64,25,1,128]{3,2,1,0:T(1,128)S(1)} async-done(((f32[64,25,1,128]{3,2,1,0:T(1,128)}), f32[64,25,1,128]{3,2,1,0:T(1,128)S(1)}, u32[]{:S(2)}, u32[]{:S(2)}) %all-to-all-start.1) | async-done | bytes 819232 | tf_op jit(solution)/shard_map/all_to_all | solution.py:27
  55.7 11.5 %grads.1 = (f32[1792,128]{1,0:T(8,128)}, f32[32,512]{1,0:T(8,128)S(1)}) custom-call(f32[1600,128]{1,0:T(8,128)S(1)} %bitcast.40, f32[32,512]{1,0:T(8,128)S(1)} %pad_maximum_fusion.tails, bf16[2048,640]{1,0:T(8,128)(2,1)} %get-tuple-element.14.by_edge, bf16[544,2048]{1,0:T(8,128)(2,1)} %get-tuple-element.15.by_slot, f32[2,8,512]{2,1,0:T(8,128)S(1)} %copy-done.3, ...), custom_call_target="tpu_custom_call" | custom-call | tf_op jit(solution)/shard_map/grads/pallas_call | solution.py:287
  67.2 9.1 %all-to-all-start.2 = ((f32[256,7,1,128]{3,2,1,0:T(1,128)}), f32[256,7,1,128]{3,2,1,0:T(1,128)S(1)}, u32[]{:S(2)}, u32[]{:S(2)}) async-start(f32[256,7,1,128]{3,2,1,0:T(1,128)} %bitcast.48), calls=%async_computation.2 | async-start | bytes 1835008 | tf_op jit(solution)/shard_map/all_to_all | solution.py:27
  76.3 0.0 copy-start.1
  76.4 0.1 constant_dynamic-slice_fusion.3
  76.5 1.6 %collective-permute-start.8 = (f32[32,128]{1,0:T(8,128)S(1)}, f32[32,128]{1,0:T(8,128)S(1)}, u32[]{:S(2)}, u32[]{:S(2)}) collective-permute-start(f32[32,128]{1,0:T(8,128)S(1)} %bitcast.55), channel_id=1, source_target_pairs={{0,1},{1,2},{2,3},{3,0},{4,5},{5,6},{6,7},{7,4},{8,9},{9,10},{10,1... | collective-permute-start | bytes 49160 | tf_op jit(solution)/shard_map/ppermute | solution.py:23
  78.2 2.4 %collective-permute-start.7 = (f32[32,128]{1,0:T(8,128)S(1)}, f32[32,128]{1,0:T(8,128)S(1)}, u32[]{:S(2)}, u32[]{:S(2)}) collective-permute-start(f32[32,128]{1,0:T(8,128)S(1)} %bitcast.52), channel_id=1, source_target_pairs={{0,2},{1,3},{2,0},{3,1},{4,6},{5,7},{6,4},{7,5},{8,10},{9,11},{10,... | collective-permute-start | bytes 49160 | tf_op jit(solution)/shard_map/ppermute | solution.py:23
  80.6 1.2 collective-permute-start.6
  81.7 0.8 collective-permute-done.7
  82.6 0.9 collective-permute-done.6
  83.5 4.5 %collective-permute-start.11 = (f32[4,8,128]{2,1,0:T(8,128)S(1)}, f32[4,8,128]{2,1,0:T(8,128)S(1)}, u32[]{:S(2)}, u32[]{:S(2)}) collective-permute-start(f32[4,8,128]{2,1,0:T(8,128)S(1)} %get-tuple-element.23), channel_id=1, source_target_pairs={{0,12},{4,16},{8,20},{12,24},{16,28},{20,32},{24,36},{28,40},{32,4... | collective-permute-start | bytes 49160 | tf_op jit(solution)/shard_map/ppermute | solution.py:23
  88.0 1.4 %collective-permute-start.10 = (f32[4,8,128]{2,1,0:T(8,128)S(1)}, f32[4,8,128]{2,1,0:T(8,128)S(1)}, u32[]{:S(2)}, u32[]{:S(2)}) collective-permute-start(f32[4,8,128]{2,1,0:T(8,128)S(1)} %get-tuple-element.24), channel_id=1, source_target_pairs={{0,8},{4,12},{8,16},{12,20},{16,24},{20,28},{24,32},{28,36},{32,40... | collective-permute-start | bytes 49160 | tf_op jit(solution)/shard_map/ppermute | solution.py:23
  89.3 13.4 %collective-permute-done.11 = f32[4,8,128]{2,1,0:T(8,128)S(1)} collective-permute-done((f32[4,8,128]{2,1,0:T(8,128)S(1)}, f32[4,8,128]{2,1,0:T(8,128)S(1)}, u32[]{:S(2)}, u32[]{:S(2)}) %collective-permute-start.11) | collective-permute-done | bytes 16416 | tf_op jit(solution)/shard_map/ppermute | solution.py:23
  102.7 3.7 %all-to-all-done.2 = f32[256,7,1,128]{3,2,1,0:T(1,128)S(1)} async-done(((f32[256,7,1,128]{3,2,1,0:T(1,128)}), f32[256,7,1,128]{3,2,1,0:T(1,128)S(1)}, u32[]{:S(2)}, u32[]{:S(2)}) %all-to-all-start.2) | async-done | bytes 917536 | tf_op jit(solution)/shard_map/all_to_all | solution.py:27
  106.5 2.8 %owner.1.own = f32[104,512]{1,0:T(8,128)S(1)} custom-call(f32[1792,128]{1,0:T(8,128)S(1)} %bitcast.39, f32[128,128]{1,0:T(8,128)S(1)} %bitcast.46, bf16[512,2176]{1,0:T(8,128)(2,1)} %hot.1.ahead), custom_call_target="tpu_custom_call" | custom-call | tf_op jit(solution)/shard_map/owner/pallas_call | solution.py:367
  109.3 0.4 collective-permute-start.12
  109.7 1.8 %collective-permute-start.13 = (f32[104,512]{1,0:T(8,128)S(1)}, f32[104,512]{1,0:T(8,128)S(1)}, u32[]{:S(2)}, u32[]{:S(2)}) collective-permute-start(f32[104,512]{1,0:T(8,128)S(1)} %owner.1.own), channel_id=1, source_target_pairs={{0,2},{1,3},{2,0},{3,1},{4,6},{5,7},{6,4},{7,5},{8,10},{9,11},{10,... | collective-permute-start | bytes 638984 | tf_op jit(solution)/shard_map/ppermute | solution.py:23
  111.4 0.7 collective-permute-start.14
  112.1 9.2 %collective-permute-done.12.next1 = f32[104,512]{1,0:T(8,128)S(1)} collective-permute-done((f32[104,512]{1,0:T(8,128)S(1)}, f32[104,512]{1,0:T(8,128)S(1)}, u32[]{:S(2)}, u32[]{:S(2)}) %collective-permute-start.12) | collective-permute-done | bytes 213024 | tf_op jit(solution)/shard_map/ppermute | solution.py:23
  121.4 0.9 collective-permute-done.14.next3
  122.3 1.7 %update.1 = (f32[400,512]{1,0:T(8,128)}, f32[1,512]{1,0:T(1,128)}) custom-call(s32[1]{0:T(128)} %bitcast.me, f32[104,512]{1,0:T(8,128)S(1)} %owner.1.own, f32[104,512]{1,0:T(8,128)S(1)} %collective-permute-done.12.next1, f32[104,512]{1,0:T(8,128)S(1)} %collective-permute-done.13.next2, f32[104,512]{1,0:T(8,128)S(1)} %collective-permute-done.14.next3, ...), custom_call_target="tpu_custom_call" | custom-call | tf_op jit(solution)/shard_map/update/pallas_call | solution.py:408
  (33 shorter events, 0.2 us)
Async XLA Ops:
  2.0 22.4 %all-to-all-start = ((s32[64,1,16]{2,1,0:T(1,128)}), s32[64,1,16]{2,1,0:T(1,128)S(1)}, u32[]{:S(2)}, u32[]{:S(2)}) async-start(s32[64,1,16]{2,1,0:T(1,128)} %bitcast.1), calls=%async_computation | async-start | bytes 65536 | tf_op jit(solution)/shard_map/all_to_all | solution.py:27
  15.2 1.1 copy-start
  16.3 15.7 %copy-start.6 = (s32[1,1,2,512]{3,2,1,0:T(2,128)S(1)}, s32[1,1,2,512]{3,2,1,0:T(2,128)}, u32[]{:S(2)}) copy-start(s32[1,1,2,512]{3,2,1,0:T(2,128)} %param.10) | copy-start | bytes 12292
  16.3 15.7 %copy-start.7 = (s32[1,1,2,512]{3,2,1,0:T(2,128)S(1)}, s32[1,1,2,512]{3,2,1,0:T(2,128)}, u32[]{:S(2)}) copy-start(s32[1,1,2,512]{3,2,1,0:T(2,128)} %param.9) | copy-start | bytes 12292
  16.3 28.2 %copy-start.5 = (s32[1,1,2,2,512]{4,3,2,1,0:T(2,128)S(1)}, s32[1,1,2,2,512]{4,3,2,1,0:T(2,128)}, u32[]{:S(2)}) copy-start(s32[1,1,2,2,512]{4,3,2,1,0:T(2,128)} %param.11) | copy-start | bytes 24580
  27.3 28.5 %all-to-all-start.1 = ((f32[64,25,1,128]{3,2,1,0:T(1,128)}), f32[64,25,1,128]{3,2,1,0:T(1,128)S(1)}, u32[]{:S(2)}, u32[]{:S(2)}) async-start(f32[64,25,1,128]{3,2,1,0:T(1,128)} %bitcast.49), calls=%async_computation.1 | async-start | bytes 1638400 | tf_op jit(solution)/shard_map/all_to_all | solution.py:27
  33.0 11.0 %collective-permute-start.3 = (s32[1,544]{1,0:T(1,128)S(1)}, s32[1,544]{1,0:T(1,128)S(1)}, u32[]{:S(2)}, u32[]{:S(2)}) collective-permute-start(s32[1,544]{1,0:T(1,128)S(1)} %pad_add_fusion.1.refs_0_), channel_id=1, source_target_pairs={{0,3},{1,0},{2,1},{3,2},{4,7},{5,4},{6,5},{7,6},{8,11},{9,8},{10,9... | collective-permute-start | bytes 6536 | tf_op jit(solution)/shard_map/ppermute | solution.py:23
  35.5 12.7 %collective-permute-start.4 = (s32[1,544]{1,0:T(1,128)S(1)}, s32[1,544]{1,0:T(1,128)S(1)}, u32[]{:S(2)}, u32[]{:S(2)}) collective-permute-start(s32[1,544]{1,0:T(1,128)S(1)} %pad_add_fusion.1.refs_0_), channel_id=1, source_target_pairs={{0,2},{1,3},{2,0},{3,1},{4,6},{5,7},{6,4},{7,5},{8,10},{9,11},{10,... | collective-permute-start | bytes 6536 | tf_op jit(solution)/shard_map/ppermute | solution.py:23
  36.0 12.2 %collective-permute-start.5 = (s32[1,544]{1,0:T(1,128)S(1)}, s32[1,544]{1,0:T(1,128)S(1)}, u32[]{:S(2)}, u32[]{:S(2)}) collective-permute-start(s32[1,544]{1,0:T(1,128)S(1)} %pad_add_fusion.1.refs_0_), channel_id=1, source_target_pairs={{0,1},{1,2},{2,3},{3,0},{4,5},{5,6},{6,7},{7,4},{8,9},{9,10},{10,1... | collective-permute-start | bytes 6536 | tf_op jit(solution)/shard_map/ppermute | solution.py:23
  36.6 16.3 %collective-permute-start.2 = (f32[8,512]{1,0:T(8,128)S(1)}, f32[8,512]{1,0:T(8,128)S(1)}, u32[]{:S(2)}, u32[]{:S(2)}) collective-permute-start(f32[8,512]{1,0:T(8,128)S(1)} %get-tuple-element.31), channel_id=1, source_target_pairs={{0,244},{4,248},{8,252},{12,0},{16,4},{20,8},{24,12},{28,16},{32,2... | collective-permute-start | bytes 49160 | tf_op jit(solution)/shard_map/ppermute | solution.py:23
  42.8 10.1 %collective-permute-start.1 = (f32[8,512]{1,0:T(8,128)S(1)}, f32[8,512]{1,0:T(8,128)S(1)}, u32[]{:S(2)}, u32[]{:S(2)}) collective-permute-start(f32[8,512]{1,0:T(8,128)S(1)} %get-tuple-element.32), channel_id=1, source_target_pairs={{0,248},{4,252},{8,0},{12,4},{16,8},{20,12},{24,16},{28,20},{32,24... | collective-permute-start | bytes 49160 | tf_op jit(solution)/shard_map/ppermute | solution.py:23
  44.0 9.1 %collective-permute-start = (f32[8,512]{1,0:T(8,128)S(1)}, f32[8,512]{1,0:T(8,128)S(1)}, u32[]{:S(2)}, u32[]{:S(2)}) collective-permute-start(f32[8,512]{1,0:T(8,128)S(1)} %get-tuple-element.33), channel_id=1, source_target_pairs={{0,252},{4,0},{8,4},{12,8},{16,12},{20,16},{24,20},{28,24},{32,28}... | collective-permute-start | bytes 49160 | tf_op jit(solution)/shard_map/ppermute | solution.py:23
  48.1 7.6 %copy-start.2 = (f32[2,512,128]{2,1,0:T(8,128)S(1)}, f32[2,512,128]{2,1,0:T(8,128)}, u32[]{:S(2)}) copy-start(f32[2,512,128]{2,1,0:T(8,128)} %get-tuple-element.17.count_col) | copy-start | bytes 1572868
  48.1 7.6 %copy-start.3 = (f32[2,8,512]{2,1,0:T(8,128)S(1)}, f32[2,8,512]{2,1,0:T(8,128)}, u32[]{:S(2)}) copy-start(f32[2,8,512]{2,1,0:T(8,128)} %get-tuple-element.16.count_row) | copy-start | bytes 98308
  67.2 39.2 %all-to-all-start.2 = ((f32[256,7,1,128]{3,2,1,0:T(1,128)}), f32[256,7,1,128]{3,2,1,0:T(1,128)S(1)}, u32[]{:S(2)}, u32[]{:S(2)}) async-start(f32[256,7,1,128]{3,2,1,0:T(1,128)} %bitcast.48), calls=%async_computation.2 | async-start | bytes 1835008 | tf_op jit(solution)/shard_map/all_to_all | solution.py:27
  76.3 46.0 %copy-start.1 = (f32[512,400]{0,1:T(8,128)S(1)}, f32[512,400]{0,1:T(8,128)}, u32[]{:S(2)}) copy-start(f32[512,400]{0,1:T(8,128)} %param.6) | copy-start | bytes 2457604
  76.3 46.0 %copy-start.4 = (f32[512]{0:T(512)S(1)}, f32[512]{0:T(512)}, u32[]{:S(2)}) copy-start(f32[512]{0:T(512)} %param.7) | copy-start | bytes 6148
  76.5 5.2 %collective-permute-start.8 = (f32[32,128]{1,0:T(8,128)S(1)}, f32[32,128]{1,0:T(8,128)S(1)}, u32[]{:S(2)}, u32[]{:S(2)}) collective-permute-start(f32[32,128]{1,0:T(8,128)S(1)} %bitcast.55), channel_id=1, source_target_pairs={{0,1},{1,2},{2,3},{3,0},{4,5},{5,6},{6,7},{7,4},{8,9},{9,10},{10,1... | collective-permute-start | bytes 49160 | tf_op jit(solution)/shard_map/ppermute | solution.py:23
  78.2 4.4 %collective-permute-start.7 = (f32[32,128]{1,0:T(8,128)S(1)}, f32[32,128]{1,0:T(8,128)S(1)}, u32[]{:S(2)}, u32[]{:S(2)}) collective-permute-start(f32[32,128]{1,0:T(8,128)S(1)} %bitcast.52), channel_id=1, source_target_pairs={{0,2},{1,3},{2,0},{3,1},{4,6},{5,7},{6,4},{7,5},{8,10},{9,11},{10,... | collective-permute-start | bytes 49160 | tf_op jit(solution)/shard_map/ppermute | solution.py:23
  80.6 2.9 %collective-permute-start.6 = (f32[32,128]{1,0:T(8,128)S(1)}, f32[32,128]{1,0:T(8,128)S(1)}, u32[]{:S(2)}, u32[]{:S(2)}) collective-permute-start(f32[32,128]{1,0:T(8,128)S(1)} %bitcast.51), channel_id=1, source_target_pairs={{0,3},{1,0},{2,1},{3,2},{4,7},{5,4},{6,5},{7,6},{8,11},{9,8},{10,9... | collective-permute-start | bytes 49160 | tf_op jit(solution)/shard_map/ppermute | solution.py:23
  83.5 19.2 %collective-permute-start.11 = (f32[4,8,128]{2,1,0:T(8,128)S(1)}, f32[4,8,128]{2,1,0:T(8,128)S(1)}, u32[]{:S(2)}, u32[]{:S(2)}) collective-permute-start(f32[4,8,128]{2,1,0:T(8,128)S(1)} %get-tuple-element.23), channel_id=1, source_target_pairs={{0,12},{4,16},{8,20},{12,24},{16,28},{20,32},{24,36},{28,40},{32,4... | collective-permute-start | bytes 49160 | tf_op jit(solution)/shard_map/ppermute | solution.py:23
  88.0 14.8 %collective-permute-start.10 = (f32[4,8,128]{2,1,0:T(8,128)S(1)}, f32[4,8,128]{2,1,0:T(8,128)S(1)}, u32[]{:S(2)}, u32[]{:S(2)}) collective-permute-start(f32[4,8,128]{2,1,0:T(8,128)S(1)} %get-tuple-element.24), channel_id=1, source_target_pairs={{0,8},{4,12},{8,16},{12,20},{16,24},{20,28},{24,32},{28,36},{32,40... | collective-permute-start | bytes 49160 | tf_op jit(solution)/shard_map/ppermute | solution.py:23
  89.3 13.4 %collective-permute-start.9 = (f32[4,8,128]{2,1,0:T(8,128)S(1)}, f32[4,8,128]{2,1,0:T(8,128)S(1)}, u32[]{:S(2)}, u32[]{:S(2)}) collective-permute-start(f32[4,8,128]{2,1,0:T(8,128)S(1)} %get-tuple-element.25), channel_id=1, source_target_pairs={{0,4},{4,8},{8,12},{12,16},{16,20},{20,24},{24,28},{28,32},{32,36}... | collective-permute-start | bytes 49160 | tf_op jit(solution)/shard_map/ppermute | solution.py:23
  109.3 12.1 %collective-permute-start.12 = (f32[104,512]{1,0:T(8,128)S(1)}, f32[104,512]{1,0:T(8,128)S(1)}, u32[]{:S(2)}, u32[]{:S(2)}) collective-permute-start(f32[104,512]{1,0:T(8,128)S(1)} %owner.1.own), channel_id=1, source_target_pairs={{0,1},{1,2},{2,3},{3,0},{4,5},{5,6},{6,7},{7,4},{8,9},{9,10},{10,1... | collective-permute-start | bytes 638984 | tf_op jit(solution)/shard_map/ppermute | solution.py:23
  109.7 11.7 %collective-permute-start.13 = (f32[104,512]{1,0:T(8,128)S(1)}, f32[104,512]{1,0:T(8,128)S(1)}, u32[]{:S(2)}, u32[]{:S(2)}) collective-permute-start(f32[104,512]{1,0:T(8,128)S(1)} %owner.1.own), channel_id=1, source_target_pairs={{0,2},{1,3},{2,0},{3,1},{4,6},{5,7},{6,4},{7,5},{8,10},{9,11},{10,... | collective-permute-start | bytes 638984 | tf_op jit(solution)/shard_map/ppermute | solution.py:23
  111.4 10.9 %collective-permute-start.14 = (f32[104,512]{1,0:T(8,128)S(1)}, f32[104,512]{1,0:T(8,128)S(1)}, u32[]{:S(2)}, u32[]{:S(2)}) collective-permute-start(f32[104,512]{1,0:T(8,128)S(1)} %owner.1.own), channel_id=1, source_target_pairs={{0,3},{1,0},{2,1},{3,2},{4,7},{5,4},{6,5},{7,6},{8,11},{9,8},{10,9... | collective-permute-start | bytes 638984 | tf_op jit(solution)/shard_map/ppermute | solution.py:23

commit v7 on v6

--- a/solution.py
+++ b/solution.py
@@ -180,12 +180,9 @@
 
 def leftover(blocks):
     lane = lanes_of(blocks[0].shape)
-    out = jnp.zeros(blocks[0].shape, f32)
-    for c, block in enumerate(blocks):
-        at = SPARE * c
-        wide = SPARE if c < QUARTERS - 1 else 16
-        moved = pltpu.roll(block, (at - (MAIN if c < QUARTERS - 1 else 0)) % LANES, 1)
-        out = jnp.where((lane >= at) & (lane < at + wide), moved, out)
+    out = blocks[-1]
+    for block in blocks[-2::-1]:
+        out = pltpu.roll(jnp.where(lane < MAIN, out, block), SPARE, 1)
     return out
 
 
@@ -234,10 +231,10 @@
         decay = jnp.exp2(jnp.minimum(scores * -LOG2E, 126.0))
         weight = 1.0 / (1.0 + decay)
         counts = count_row[b, 0:1, :] + jnp.concatenate([count_col[b]] * (edges // LANES), axis=1)
-        return (weight * counts).astype(bf16)
-
-    def pulled(at, gain, pull, rows_high, rows_low, rows):
-        moved = mm(gain, rows_high) + mm(gain, rows_low) + pull * rows
+        return halves(weight * counts)
+
+    def pulled(at, gain, rest, pull, rows_high, rows_low, rows):
+        moved = mm(gain, rows_high) + mm(gain, rows_low) + mm(rest, rows_high) + pull * rows
         d_high[at : at + edges, :], d_low[at : at + edges, :] = halves(moved)
 
     for b in range(batches):
@@ -247,9 +244,9 @@
         positive = jnp.sum(s_rows * t_rows, axis=1, keepdims=True)
         falling = jnp.exp(-jnp.abs(positive))
         pull = -jnp.where(positive >= 0, falling, 1.0) / (1.0 + falling)
-        gain = gained(b, mm_nt(s_high, t_high))
-        pulled(2 * b * edges, gain, pull, t_high, t_low, t_rows)
-        pulled((2 * b + 1) * edges, gain.T, pull, s_high, s_low, s_rows)
+        gain, rest = gained(b, mm_nt(s_high, t_high) + mm_nt(s_high, t_low) + mm_nt(s_low, t_high))
+        pulled(2 * b * edges, gain, rest, pull, t_high, t_low, t_rows)
+        pulled((2 * b + 1) * edges, gain.T, rest.T, pull, s_high, s_low, s_rows)
     last.wait()
     stores = []
     block = 2 * LANES

time: 125 us -> 127 us (1.016)
  Pallas kernels: 25.3 us -> 27.3 us
    pallas_call x1, Pallas kernels: 11.5 us -> 13.5 us  [grads(): pl.pallas_call(grads_body, in_specs=[VMEM, VMEM, HBM, HBM, VMEM, VMEM, HB...]
where the time goes in v7:
time: 127 us; the launch traced here: 126 us
  starting transfers between devices  52 us (41%)
  waiting for transfers between devices  42.1 us (33%)
  Pallas kernels  27.3 us (21%)
  local copies, waits for them, and re-layouts  3.25 us (3%)
    ppermute x15, waiting for transfers between devices, passed_along(): return lax.ppermute(value, axis, pairs)  28.3 us
    all_to_all x3, starting transfers between devices, exchanged(): return lax.all_to_all(value, axis, 0, 0, tiled=True)  27 us
    ppermute x15, starting transfers between devices, passed_along(): return lax.ppermute(value, axis, pairs)  25 us
    all_to_all x3, waiting for transfers between devices, exchanged(): return lax.all_to_all(value, axis, 0, 0, tiled=True)  13.8 us
    pallas_call x1, Pallas kernels, grads(): pl.pallas_call(grads_body, in_specs=[VMEM, VMEM, HBM, HBM, VMEM, VMEM, HB...  13.5 us
    pallas_call x1, Pallas kernels, prep(): pl.pallas_call(prep_body, out_shape=[pltpu.HBM((total, padded), bf16), pl...  3.55 us
    pallas_call x1, Pallas kernels, serve(): pl.pallas_call(serve_body, in_specs=[SMEM, SMEM, VMEM], out_specs=[HBM, V...  2.83 us
    pallas_call x1, Pallas kernels, owner(): pl.pallas_call(owner_body, in_specs=[VMEM, VMEM, HBM], out_specs=VMEM, ou...  2.79 us
  transfers between devices with their start and end apart: 18, of which 10 were waited for; matrix products, arithmetic and copies ran while one was open for 1% of the time, Pallas kernels for 5%

profile of v7, /device:TPU:1, one launch (start us, length us, event | category | flops | bytes accessed | tf_op | source)
XLA Modules:
  0.0 126.1 jit_solution(10532465899469634218)
XLA Ops:
  0.6 1.4 %copy.25 = s32[1,1,64,16]{3,2,1,0:T(8,128)} copy(s32[1,1,64,16]{2,3,1,0:T(8,128)} %param.8) | data formatting | bytes 8192 | tf_op args[2]
  2.0 13.1 %all-to-all-start = ((s32[64,1,16]{2,1,0:T(1,128)}), s32[64,1,16]{2,1,0:T(1,128)S(1)}, u32[]{:S(2)}, u32[]{:S(2)}) async-start(s32[64,1,16]{2,1,0:T(1,128)} %bitcast.1), calls=%async_computation | async-start | bytes 65536 | tf_op jit(solution)/shard_map/all_to_all | solution.py:27
  15.2 0.0 copy-start
  15.2 1.1 copy-done
  16.3 0.6 spread.1.rows
  17.0 7.4 %all-to-all-done.ids = s32[64,1,16]{2,1,0:T(1,128)S(1)} async-done(((s32[64,1,16]{2,1,0:T(1,128)}), s32[64,1,16]{2,1,0:T(1,128)S(1)}, u32[]{:S(2)}, u32[]{:S(2)}) %all-to-all-start) | async-done | bytes 4128 | tf_op jit(solution)/shard_map/all_to_all | solution.py:27
  24.4 2.8 %serve.1 = (f32[1600,128]{1,0:T(8,128)}, f32[32,512]{1,0:T(8,128)S(1)}) custom-call(s32[64,1,16]{2,1,0:T(1,128)S(1)} %all-to-all-done.ids, s32[1]{0:T(128)} %bitcast.2.here, f32[512,4,128]{2,1,0:T(4,128)S(1)} %spread.1.rows), custom_call_target="tpu_custom_call" | custom-call | tf_op jit(solution)/shard_map/serve/pallas_call | solution.py:118
  27.3 4.8 %all-to-all-start.1 = ((f32[64,25,1,128]{3,2,1,0:T(1,128)}), f32[64,25,1,128]{3,2,1,0:T(1,128)S(1)}, u32[]{:S(2)}, u32[]{:S(2)}) async-start(f32[64,25,1,128]{3,2,1,0:T(1,128)} %bitcast.49), calls=%async_computation.1 | async-start | bytes 1638400 | tf_op jit(solution)/shard_map/all_to_all | solution.py:27
  32.1 0.1 iota_compare_fusion
  32.2 0.1 slice.50
  32.3 0.1 copy.28
  32.3 0.2 select_reduce_fusion
  32.5 0.1 reshape.323
  32.6 0.1 reshape.322
  32.7 0.2 slice_reduce_fusion
  32.9 0.1 pad_add_fusion.1.refs_0_
  33.0 2.5 %collective-permute-start.3 = (s32[1,544]{1,0:T(1,128)S(1)}, s32[1,544]{1,0:T(1,128)S(1)}, u32[]{:S(2)}, u32[]{:S(2)}) collective-permute-start(s32[1,544]{1,0:T(1,128)S(1)} %pad_add_fusion.1.refs_0_), channel_id=1, source_target_pairs={{0,3},{1,0},{2,1},{3,2},{4,7},{5,4},{6,5},{7,6},{8,11},{9,8},{10,9... | collective-permute-start | bytes 6536 | tf_op jit(solution)/shard_map/ppermute | solution.py:23
  35.5 0.5 collective-permute-start.4
  36.0 0.6 collective-permute-start.5
  36.6 6.2 %collective-permute-start.2 = (f32[8,512]{1,0:T(8,128)S(1)}, f32[8,512]{1,0:T(8,128)S(1)}, u32[]{:S(2)}, u32[]{:S(2)}) collective-permute-start(f32[8,512]{1,0:T(8,128)S(1)} %get-tuple-element.31), channel_id=1, source_target_pairs={{0,244},{4,248},{8,252},{12,0},{16,4},{20,8},{24,12},{28,16},{32,2... | collective-permute-start | bytes 49160 | tf_op jit(solution)/shard_map/ppermute | solution.py:23
  42.8 1.2 collective-permute-start.1
  44.0 0.4 collective-permute-start
  44.4 0.1 compare_select_fusion.2.slots
  44.6 3.5 %prep.1 = (bf16[2048,640]{1,0:T(8,128)(2,1)}, bf16[544,2048]{1,0:T(8,128)(2,1)}, f32[2,8,512]{2,1,0:T(8,128)}, f32[2,512,128]{2,1,0:T(8,128)}) custom-call(s32[1,2048]{1,0:T(1,128)S(1)} %compare_select_fusion.2.slots, s32[1,2048]{1,0:T(1,128)S(1)} %reshape_squeeze.10.negs), custom_call_target="tpu_custom_call" | custom-call | tf_op jit(solution)/shard_map/prep/pallas_call | solution.py:164
  48.1 2.3 %hot.1.ahead = bf16[512,2176]{1,0:T(8,128)(2,1)} custom-call(s32[1]{0:T(128)} %bitcast.me, s32[1,544]{1,0:T(1,128)S(1)} %pad_add_fusion.1.refs_0_, s32[1,544]{1,0:T(1,128)S(1)} %collective-permute-done.3.refs_1_, s32[1,544]{1,0:T(1,128)S(1)} %collective-permute-done.4.refs_2_, s32[1,544]{1,0:T(1,128)S(1)} %collective-permute-done.5.refs_3_), custom_call_target="tpu_custom_call" | custom-call | tf_op jit(solution)/shard_map/hot/pallas_call | solution.py:325
  50.5 2.4 %collective-permute-done.2 = f32[8,512]{1,0:T(8,128)S(1)} collective-permute-done((f32[8,512]{1,0:T(8,128)S(1)}, f32[8,512]{1,0:T(8,128)S(1)}, u32[]{:S(2)}, u32[]{:S(2)}) %collective-permute-start.2) | collective-permute-done | bytes 16416 | tf_op jit(solution)/shard_map/ppermute | solution.py:23
  52.9 0.2 collective-permute-done
  53.1 2.6 %all-to-all-done.1 = f32[64,25,1,128]{3,2,1,0:T(1,128)S(1)} async-done(((f32[64,25,1,128]{3,2,1,0:T(1,128)}), f32[64,25,1,128]{3,2,1,0:T(1,128)S(1)}, u32[]{:S(2)}, u32[]{:S(2)}) %all-to-all-start.1) | async-done | bytes 819232 | tf_op jit(solution)/shard_map/all_to_all | solution.py:27
  55.7 13.5 %grads.1 = (f32[1792,128]{1,0:T(8,128)}, f32[32,512]{1,0:T(8,128)S(1)}) custom-call(f32[1600,128]{1,0:T(8,128)S(1)} %bitcast.40, f32[32,512]{1,0:T(8,128)S(1)} %pad_maximum_fusion.tails, bf16[2048,640]{1,0:T(8,128)(2,1)} %get-tuple-element.14.by_edge, bf16[544,2048]{1,0:T(8,128)(2,1)} %get-tuple-element.15.by_slot, f32[2,8,512]{2,1,0:T(8,128)S(1)} %copy-done.3, ...), custom_call_target="tpu_custom_call" | custom-call | tf_op jit(solution)/shard_map/grads/pallas_call | solution.py:284
  69.2 9.1 %all-to-all-start.2 = ((f32[256,7,1,128]{3,2,1,0:T(1,128)}), f32[256,7,1,128]{3,2,1,0:T(1,128)S(1)}, u32[]{:S(2)}, u32[]{:S(2)}) async-start(f32[256,7,1,128]{3,2,1,0:T(1,128)} %bitcast.48), calls=%async_computation.2 | async-start | bytes 1835008 | tf_op jit(solution)/shard_map/all_to_all | solution.py:27
  78.3 0.0 copy-start.1
  78.4 0.1 constant_dynamic-slice_fusion.3
  78.5 1.4 %collective-permute-start.8 = (f32[32,128]{1,0:T(8,128)S(1)}, f32[32,128]{1,0:T(8,128)S(1)}, u32[]{:S(2)}, u32[]{:S(2)}) collective-permute-start(f32[32,128]{1,0:T(8,128)S(1)} %bitcast.55), channel_id=1, source_target_pairs={{0,1},{1,2},{2,3},{3,0},{4,5},{5,6},{6,7},{7,4},{8,9},{9,10},{10,1... | collective-permute-start | bytes 49160 | tf_op jit(solution)/shard_map/ppermute | solution.py:23
  79.9 2.4 %collective-permute-start.7 = (f32[32,128]{1,0:T(8,128)S(1)}, f32[32,128]{1,0:T(8,128)S(1)}, u32[]{:S(2)}, u32[]{:S(2)}) collective-permute-start(f32[32,128]{1,0:T(8,128)S(1)} %bitcast.52), channel_id=1, source_target_pairs={{0,2},{1,3},{2,0},{3,1},{4,6},{5,7},{6,4},{7,5},{8,10},{9,11},{10,... | collective-permute-start | bytes 49160 | tf_op jit(solution)/shard_map/ppermute | solution.py:23
  82.3 1.2 collective-permute-start.6
  83.5 0.8 collective-permute-done.7
  84.3 1.1 collective-permute-done.6
  85.5 4.4 %collective-permute-start.11 = (f32[4,8,128]{2,1,0:T(8,128)S(1)}, f32[4,8,128]{2,1,0:T(8,128)S(1)}, u32[]{:S(2)}, u32[]{:S(2)}) collective-permute-start(f32[4,8,128]{2,1,0:T(8,128)S(1)} %get-tuple-element.23), channel_id=1, source_target_pairs={{0,12},{4,16},{8,20},{12,24},{16,28},{20,32},{24,36},{28,40},{32,4... | collective-permute-start | bytes 49160 | tf_op jit(solution)/shard_map/ppermute | solution.py:23
  89.9 1.2 collective-permute-start.10
  91.1 13.5 %collective-permute-done.11 = f32[4,8,128]{2,1,0:T(8,128)S(1)} collective-permute-done((f32[4,8,128]{2,1,0:T(8,128)S(1)}, f32[4,8,128]{2,1,0:T(8,128)S(1)}, u32[]{:S(2)}, u32[]{:S(2)}) %collective-permute-start.11) | collective-permute-done | bytes 16416 | tf_op jit(solution)/shard_map/ppermute | solution.py:23
  104.7 3.7 %all-to-all-done.2 = f32[256,7,1,128]{3,2,1,0:T(1,128)S(1)} async-done(((f32[256,7,1,128]{3,2,1,0:T(1,128)}), f32[256,7,1,128]{3,2,1,0:T(1,128)S(1)}, u32[]{:S(2)}, u32[]{:S(2)}) %all-to-all-start.2) | async-done | bytes 917536 | tf_op jit(solution)/shard_map/all_to_all | solution.py:27
  108.4 2.8 %owner.1.own = f32[104,512]{1,0:T(8,128)S(1)} custom-call(f32[1792,128]{1,0:T(8,128)S(1)} %bitcast.39, f32[128,128]{1,0:T(8,128)S(1)} %bitcast.46, bf16[512,2176]{1,0:T(8,128)(2,1)} %hot.1.ahead), custom_call_target="tpu_custom_call" | custom-call | tf_op jit(solution)/shard_map/owner/pallas_call | solution.py:364
  111.3 0.4 collective-permute-start.12
  111.6 1.8 %collective-permute-start.13 = (f32[104,512]{1,0:T(8,128)S(1)}, f32[104,512]{1,0:T(8,128)S(1)}, u32[]{:S(2)}, u32[]{:S(2)}) collective-permute-start(f32[104,512]{1,0:T(8,128)S(1)} %owner.1.own), channel_id=1, source_target_pairs={{0,2},{1,3},{2,0},{3,1},{4,6},{5,7},{6,4},{7,5},{8,10},{9,11},{10,... | collective-permute-start | bytes 638984 | tf_op jit(solution)/shard_map/ppermute | solution.py:23
  113.4 0.7 collective-permute-start.14
  114.1 9.2 %collective-permute-done.12.next1 = f32[104,512]{1,0:T(8,128)S(1)} collective-permute-done((f32[104,512]{1,0:T(8,128)S(1)}, f32[104,512]{1,0:T(8,128)S(1)}, u32[]{:S(2)}, u32[]{:S(2)}) %collective-permute-start.12) | collective-permute-done | bytes 213024 | tf_op jit(solution)/shard_map/ppermute | solution.py:23
  123.4 0.9 collective-permute-done.14.next3
  124.3 1.7 %update.1 = (f32[400,512]{1,0:T(8,128)}, f32[1,512]{1,0:T(1,128)}) custom-call(s32[1]{0:T(128)} %bitcast.me, f32[104,512]{1,0:T(8,128)S(1)} %owner.1.own, f32[104,512]{1,0:T(8,128)S(1)} %collective-permute-done.12.next1, f32[104,512]{1,0:T(8,128)S(1)} %collective-permute-done.13.next2, f32[104,512]{1,0:T(8,128)S(1)} %collective-permute-done.14.next3, ...), custom_call_target="tpu_custom_call" | custom-call | tf_op jit(solution)/shard_map/update/pallas_call | solution.py:405
  (33 shorter events, 0.2 us)
Async XLA Ops:
  2.0 22.4 %all-to-all-start = ((s32[64,1,16]{2,1,0:T(1,128)}), s32[64,1,16]{2,1,0:T(1,128)S(1)}, u32[]{:S(2)}, u32[]{:S(2)}) async-start(s32[64,1,16]{2,1,0:T(1,128)} %bitcast.1), calls=%async_computation | async-start | bytes 65536 | tf_op jit(solution)/shard_map/all_to_all | solution.py:27
  15.2 1.1 copy-start
  16.3 15.7 %copy-start.6 = (s32[1,1,2,512]{3,2,1,0:T(2,128)S(1)}, s32[1,1,2,512]{3,2,1,0:T(2,128)}, u32[]{:S(2)}) copy-start(s32[1,1,2,512]{3,2,1,0:T(2,128)} %param.10) | copy-start | bytes 12292
  16.3 15.7 %copy-start.7 = (s32[1,1,2,512]{3,2,1,0:T(2,128)S(1)}, s32[1,1,2,512]{3,2,1,0:T(2,128)}, u32[]{:S(2)}) copy-start(s32[1,1,2,512]{3,2,1,0:T(2,128)} %param.9) | copy-start | bytes 12292
  16.3 28.2 %copy-start.5 = (s32[1,1,2,2,512]{4,3,2,1,0:T(2,128)S(1)}, s32[1,1,2,2,512]{4,3,2,1,0:T(2,128)}, u32[]{:S(2)}) copy-start(s32[1,1,2,2,512]{4,3,2,1,0:T(2,128)} %param.11) | copy-start | bytes 24580
  27.3 28.5 %all-to-all-start.1 = ((f32[64,25,1,128]{3,2,1,0:T(1,128)}), f32[64,25,1,128]{3,2,1,0:T(1,128)S(1)}, u32[]{:S(2)}, u32[]{:S(2)}) async-start(f32[64,25,1,128]{3,2,1,0:T(1,128)} %bitcast.49), calls=%async_computation.1 | async-start | bytes 1638400 | tf_op jit(solution)/shard_map/all_to_all | solution.py:27
  33.0 11.0 %collective-permute-start.3 = (s32[1,544]{1,0:T(1,128)S(1)}, s32[1,544]{1,0:T(1,128)S(1)}, u32[]{:S(2)}, u32[]{:S(2)}) collective-permute-start(s32[1,544]{1,0:T(1,128)S(1)} %pad_add_fusion.1.refs_0_), channel_id=1, source_target_pairs={{0,3},{1,0},{2,1},{3,2},{4,7},{5,4},{6,5},{7,6},{8,11},{9,8},{10,9... | collective-permute-start | bytes 6536 | tf_op jit(solution)/shard_map/ppermute | solution.py:23
  35.5 12.7 %collective-permute-start.4 = (s32[1,544]{1,0:T(1,128)S(1)}, s32[1,544]{1,0:T(1,128)S(1)}, u32[]{:S(2)}, u32[]{:S(2)}) collective-permute-start(s32[1,544]{1,0:T(1,128)S(1)} %pad_add_fusion.1.refs_0_), channel_id=1, source_target_pairs={{0,2},{1,3},{2,0},{3,1},{4,6},{5,7},{6,4},{7,5},{8,10},{9,11},{10,... | collective-permute-start | bytes 6536 | tf_op jit(solution)/shard_map/ppermute | solution.py:23
  36.0 12.2 %collective-permute-start.5 = (s32[1,544]{1,0:T(1,128)S(1)}, s32[1,544]{1,0:T(1,128)S(1)}, u32[]{:S(2)}, u32[]{:S(2)}) collective-permute-start(s32[1,544]{1,0:T(1,128)S(1)} %pad_add_fusion.1.refs_0_), channel_id=1, source_target_pairs={{0,1},{1,2},{2,3},{3,0},{4,5},{5,6},{6,7},{7,4},{8,9},{9,10},{10,1... | collective-permute-start | bytes 6536 | tf_op jit(solution)/shard_map/ppermute | solution.py:23
  36.6 16.3 %collective-permute-start.2 = (f32[8,512]{1,0:T(8,128)S(1)}, f32[8,512]{1,0:T(8,128)S(1)}, u32[]{:S(2)}, u32[]{:S(2)}) collective-permute-start(f32[8,512]{1,0:T(8,128)S(1)} %get-tuple-element.31), channel_id=1, source_target_pairs={{0,244},{4,248},{8,252},{12,0},{16,4},{20,8},{24,12},{28,16},{32,2... | collective-permute-start | bytes 49160 | tf_op jit(solution)/shard_map/ppermute | solution.py:23
  42.8 10.1 %collective-permute-start.1 = (f32[8,512]{1,0:T(8,128)S(1)}, f32[8,512]{1,0:T(8,128)S(1)}, u32[]{:S(2)}, u32[]{:S(2)}) collective-permute-start(f32[8,512]{1,0:T(8,128)S(1)} %get-tuple-element.32), channel_id=1, source_target_pairs={{0,248},{4,252},{8,0},{12,4},{16,8},{20,12},{24,16},{28,20},{32,24... | collective-permute-start | bytes 49160 | tf_op jit(solution)/shard_map/ppermute | solution.py:23
  44.0 9.1 %collective-permute-start = (f32[8,512]{1,0:T(8,128)S(1)}, f32[8,512]{1,0:T(8,128)S(1)}, u32[]{:S(2)}, u32[]{:S(2)}) collective-permute-start(f32[8,512]{1,0:T(8,128)S(1)} %get-tuple-element.33), channel_id=1, source_target_pairs={{0,252},{4,0},{8,4},{12,8},{16,12},{20,16},{24,20},{28,24},{32,28}... | collective-permute-start | bytes 49160 | tf_op jit(solution)/shard_map/ppermute | solution.py:23
  48.1 7.6 %copy-start.2 = (f32[2,512,128]{2,1,0:T(8,128)S(1)}, f32[2,512,128]{2,1,0:T(8,128)}, u32[]{:S(2)}) copy-start(f32[2,512,128]{2,1,0:T(8,128)} %get-tuple-element.17.count_col) | copy-start | bytes 1572868
  48.1 7.6 %copy-start.3 = (f32[2,8,512]{2,1,0:T(8,128)S(1)}, f32[2,8,512]{2,1,0:T(8,128)}, u32[]{:S(2)}) copy-start(f32[2,8,512]{2,1,0:T(8,128)} %get-tuple-element.16.count_row) | copy-start | bytes 98308
  69.2 39.2 %all-to-all-start.2 = ((f32[256,7,1,128]{3,2,1,0:T(1,128)}), f32[256,7,1,128]{3,2,1,0:T(1,128)S(1)}, u32[]{:S(2)}, u32[]{:S(2)}) async-start(f32[256,7,1,128]{3,2,1,0:T(1,128)} %bitcast.48), calls=%async_computation.2 | async-start | bytes 1835008 | tf_op jit(solution)/shard_map/all_to_all | solution.py:27
  78.3 46.0 %copy-start.1 = (f32[512,400]{0,1:T(8,128)S(1)}, f32[512,400]{0,1:T(8,128)}, u32[]{:S(2)}) copy-start(f32[512,400]{0,1:T(8,128)} %param.6) | copy-start | bytes 2457604
  78.3 46.0 %copy-start.4 = (f32[512]{0:T(512)S(1)}, f32[512]{0:T(512)}, u32[]{:S(2)}) copy-start(f32[512]{0:T(512)} %param.7) | copy-start | bytes 6148
  78.5 5.0 %collective-permute-start.8 = (f32[32,128]{1,0:T(8,128)S(1)}, f32[32,128]{1,0:T(8,128)S(1)}, u32[]{:S(2)}, u32[]{:S(2)}) collective-permute-start(f32[32,128]{1,0:T(8,128)S(1)} %bitcast.55), channel_id=1, source_target_pairs={{0,1},{1,2},{2,3},{3,0},{4,5},{5,6},{6,7},{7,4},{8,9},{9,10},{10,1... | collective-permute-start | bytes 49160 | tf_op jit(solution)/shard_map/ppermute | solution.py:23
  79.9 4.4 %collective-permute-start.7 = (f32[32,128]{1,0:T(8,128)S(1)}, f32[32,128]{1,0:T(8,128)S(1)}, u32[]{:S(2)}, u32[]{:S(2)}) collective-permute-start(f32[32,128]{1,0:T(8,128)S(1)} %bitcast.52), channel_id=1, source_target_pairs={{0,2},{1,3},{2,0},{3,1},{4,6},{5,7},{6,4},{7,5},{8,10},{9,11},{10,... | collective-permute-start | bytes 49160 | tf_op jit(solution)/shard_map/ppermute | solution.py:23
  82.3 3.1 %collective-permute-start.6 = (f32[32,128]{1,0:T(8,128)S(1)}, f32[32,128]{1,0:T(8,128)S(1)}, u32[]{:S(2)}, u32[]{:S(2)}) collective-permute-start(f32[32,128]{1,0:T(8,128)S(1)} %bitcast.51), channel_id=1, source_target_pairs={{0,3},{1,0},{2,1},{3,2},{4,7},{5,4},{6,5},{7,6},{8,11},{9,8},{10,9... | collective-permute-start | bytes 49160 | tf_op jit(solution)/shard_map/ppermute | solution.py:23
  85.5 19.2 %collective-permute-start.11 = (f32[4,8,128]{2,1,0:T(8,128)S(1)}, f32[4,8,128]{2,1,0:T(8,128)S(1)}, u32[]{:S(2)}, u32[]{:S(2)}) collective-permute-start(f32[4,8,128]{2,1,0:T(8,128)S(1)} %get-tuple-element.23), channel_id=1, source_target_pairs={{0,12},{4,16},{8,20},{12,24},{16,28},{20,32},{24,36},{28,40},{32,4... | collective-permute-start | bytes 49160 | tf_op jit(solution)/shard_map/ppermute | solution.py:23
  89.9 14.8 %collective-permute-start.10 = (f32[4,8,128]{2,1,0:T(8,128)S(1)}, f32[4,8,128]{2,1,0:T(8,128)S(1)}, u32[]{:S(2)}, u32[]{:S(2)}) collective-permute-start(f32[4,8,128]{2,1,0:T(8,128)S(1)} %get-tuple-element.24), channel_id=1, source_target_pairs={{0,8},{4,12},{8,16},{12,20},{16,24},{20,28},{24,32},{28,36},{32,40... | collective-permute-start | bytes 49160 | tf_op jit(solution)/shard_map/ppermute | solution.py:23
  91.1 13.5 %collective-permute-start.9 = (f32[4,8,128]{2,1,0:T(8,128)S(1)}, f32[4,8,128]{2,1,0:T(8,128)S(1)}, u32[]{:S(2)}, u32[]{:S(2)}) collective-permute-start(f32[4,8,128]{2,1,0:T(8,128)S(1)} %get-tuple-element.25), channel_id=1, source_target_pairs={{0,4},{4,8},{8,12},{12,16},{16,20},{20,24},{24,28},{28,32},{32,36}... | collective-permute-start | bytes 49160 | tf_op jit(solution)/shard_map/ppermute | solution.py:23
  111.3 12.1 %collective-permute-start.12 = (f32[104,512]{1,0:T(8,128)S(1)}, f32[104,512]{1,0:T(8,128)S(1)}, u32[]{:S(2)}, u32[]{:S(2)}) collective-permute-start(f32[104,512]{1,0:T(8,128)S(1)} %owner.1.own), channel_id=1, source_target_pairs={{0,1},{1,2},{2,3},{3,0},{4,5},{5,6},{6,7},{7,4},{8,9},{9,10},{10,1... | collective-permute-start | bytes 638984 | tf_op jit(solution)/shard_map/ppermute | solution.py:23
  111.6 11.7 %collective-permute-start.13 = (f32[104,512]{1,0:T(8,128)S(1)}, f32[104,512]{1,0:T(8,128)S(1)}, u32[]{:S(2)}, u32[]{:S(2)}) collective-permute-start(f32[104,512]{1,0:T(8,128)S(1)} %owner.1.own), channel_id=1, source_target_pairs={{0,2},{1,3},{2,0},{3,1},{4,6},{5,7},{6,4},{7,5},{8,10},{9,11},{10,... | collective-permute-start | bytes 638984 | tf_op jit(solution)/shard_map/ppermute | solution.py:23
  113.4 10.9 %collective-permute-start.14 = (f32[104,512]{1,0:T(8,128)S(1)}, f32[104,512]{1,0:T(8,128)S(1)}, u32[]{:S(2)}, u32[]{:S(2)}) collective-permute-start(f32[104,512]{1,0:T(8,128)S(1)} %owner.1.own), channel_id=1, source_target_pairs={{0,3},{1,0},{2,1},{3,2},{4,7},{5,4},{6,5},{7,6},{8,11},{9,8},{10,9... | collective-permute-start | bytes 638984 | tf_op jit(solution)/shard_map/ppermute | solution.py:23

commit v8 on v7

--- a/solution.py
+++ b/solution.py
@@ -13,6 +13,7 @@
 MAIN = 104
 SPARE = LANES - MAIN
 QUARTERS = 4
+CUT = 56
 f32 = jnp.float32
 bf16 = jnp.bfloat16
 
@@ -331,7 +332,7 @@
     )(me, *lists)
 
 
-def owner_body(back, tails, hot, out, spots, sems):
+def owner_body(back, tails, hot, first, second, spots, sems):
     parts = sems.shape[0] - 1
     short = back.shape[0] // parts
     each = short // 7 * 8
@@ -357,24 +358,32 @@
         part = mm(spots[:, at : at + size], both)
         total = part if total is None else total + part
     summed = total[:, :LANES] + total[:, LANES:]
-    out[...] = summed.T[: out.shape[0], :]
+    turned = summed.T
+    first[...] = turned[:CUT, :]
+    second[...] = turned[CUT:MAIN, :]
 
 
 def owner(back, tails, hot):
     return pl.pallas_call(
         owner_body,
         in_specs=[VMEM, VMEM, HBM],
-        out_specs=VMEM,
-        out_shape=jax.ShapeDtypeStruct((MAIN, hot.shape[0]), f32),
+        out_specs=[VMEM, VMEM],
+        out_shape=[
+            jax.ShapeDtypeStruct((CUT, hot.shape[0]), f32),
+            jax.ShapeDtypeStruct((MAIN - CUT, hot.shape[0]), f32),
+        ],
         scratch_shapes=[pltpu.VMEM(hot.shape, bf16), pltpu.SemaphoreType.DMA((5,))],
         compiler_params=room(16),
         name="owner",
     )(near(back), tails, far(hot))
 
 
-def update_body(me, own, next1, next2, next3, rows, sums, new_rows, new_sums, quarters, fresh_rows, sems):
-    for s, piece in enumerate((own, next1, next2, next3)):
-        quarters[(me[0] + 4 - s) % 4] = piece[...]
+def update_body(me, *refs):
+    pieces, (rows, sums, new_rows, new_sums, quarters, fresh_rows, sems) = refs[:-7], refs[-7:]
+    for s in range(QUARTERS):
+        spot = (me[0] + QUARTERS - s) % QUARTERS
+        quarters[spot, :CUT, :] = pieces[2 * s][...]
+        quarters[spot, CUT:, :] = pieces[2 * s + 1][...]
     squares = jnp.zeros(sums.shape, f32)
     for q in range(QUARTERS):
         squares += jnp.sum(quarters[q] * quarters[q], axis=0, keepdims=True)
@@ -411,9 +420,9 @@
             jax.ShapeDtypeStruct(sums.shape, f32),
         ],
         scratch_shapes=[
-            pltpu.VMEM((len(pieces), *pieces[0].shape), f32),
+            pltpu.VMEM((QUARTERS, MAIN, rows.shape[1]), f32),
             pltpu.VMEM(rows.shape, f32),
-            pltpu.SemaphoreType.DMA((len(pieces),)),
+            pltpu.SemaphoreType.DMA((QUARTERS,)),
         ],
         compiler_params=room(16),
         name="update",
@@ -471,8 +480,14 @@
     ).reshape(groups, HEAVY, half, LANES)
     tail_back = [tail_grads[:, 0]] + [passed_along(tail_grads[:, r], "dom", r) for r in range(1, HEAVY)]
     tail_back = jnp.stack(tail_back, axis=1).reshape(-1, LANES)
-    quarter = owner(back.reshape(-1, LANES), tail_back, hot)
-    pieces = [quarter] + [passed_along(quarter, "rep", s) for s in range(1, groups)]
+    first, second = owner(back.reshape(-1, LANES), tail_back, hot)
+    down_second = passed_along(second, "rep", -1)
+    down_first = passed_along(first, "rep", -1)
+    up_first = passed_along(first, "rep", 1)
+    over_first = passed_along(first, "rep", 2)
+    up_second = passed_along(second, "rep", 1)
+    over_second = passed_along(down_second, "rep", -1)
+    pieces = [first, second, up_first, up_second, over_first, over_second, down_first, down_second]
     new_rows, new_sums = update(mine, pieces, columns, adagrad_sum.reshape(1, -1))
     return new_rows.T, new_sums.reshape(-1)
 

time: 127 us -> 126 us (level)
  waiting for transfers between devices: 42.1 us -> 37.2 us
  starting transfers between devices: 52 us -> 56 us
    ppermute x15 -> x18, waiting for transfers between devices: 28.3 us -> 23.4 us  [passed_along(): return lax.ppermute(value, axis, pairs)]
    ppermute x15 -> x18, starting transfers between devices: 25 us -> 29 us  [passed_along(): return lax.ppermute(value, axis, pairs)]
  transfers between devices with their start and end apart: 18 -> 21, of which waited for: 10 -> 10; matrix products, arithmetic and copies ran while one was open for 1% -> 1% of each run, Pallas kernels for 5% -> 5%
where the time goes in v8:
time: 126 us; the launch traced here: 125 us
  starting transfers between devices  56 us (44%)
  waiting for transfers between devices  37.2 us (30%)
  Pallas kernels  27.3 us (22%)
  local copies, waits for them, and re-layouts  3.25 us (3%)
    ppermute x18, starting transfers between devices, passed_along(): return lax.ppermute(value, axis, pairs)  29 us
    all_to_all x3, starting transfers between devices, exchanged(): return lax.all_to_all(value, axis, 0, 0, tiled=True)  27 us
    ppermute x18, waiting for transfers between devices, passed_along(): return lax.ppermute(value, axis, pairs)  23.4 us
    all_to_all x3, waiting for transfers between devices, exchanged(): return lax.all_to_all(value, axis, 0, 0, tiled=True)  13.8 us
    pallas_call x1, Pallas kernels, grads(): pl.pallas_call(grads_body, in_specs=[VMEM, VMEM, HBM, HBM, VMEM, VMEM, HB...  13.5 us
    pallas_call x1, Pallas kernels, prep(): pl.pallas_call(prep_body, out_shape=[pltpu.HBM((total, padded), bf16), pl...  3.54 us
    pallas_call x1, Pallas kernels, serve(): pl.pallas_call(serve_body, in_specs=[SMEM, SMEM, VMEM], out_specs=[HBM, V...  2.83 us
    pallas_call x1, Pallas kernels, owner(): pl.pallas_call(owner_body, in_specs=[VMEM, VMEM, HBM], out_specs=[VMEM, V...  2.79 us
  transfers between devices with their start and end apart: 21, of which 10 were waited for; matrix products, arithmetic and copies ran while one was open for 1% of the time, Pallas kernels for 5%

profile of v8, /device:TPU:1, one launch (start us, length us, event | category | flops | bytes accessed | tf_op | source)
XLA Modules:
  0.0 125.3 jit_solution(12875227539232953848)
XLA Ops:
  0.6 1.4 %copy.25 = s32[1,1,64,16]{3,2,1,0:T(8,128)} copy(s32[1,1,64,16]{2,3,1,0:T(8,128)} %param.8) | data formatting | bytes 8192 | tf_op args[2]
  2.0 13.1 %all-to-all-start = ((s32[64,1,16]{2,1,0:T(1,128)}), s32[64,1,16]{2,1,0:T(1,128)S(1)}, u32[]{:S(2)}, u32[]{:S(2)}) async-start(s32[64,1,16]{2,1,0:T(1,128)} %bitcast.1), calls=%async_computation | async-start | bytes 65536 | tf_op jit(solution)/shard_map/all_to_all | solution.py:28
  15.2 1.1 copy-done
  16.3 0.6 spread.1.rows
  17.0 7.4 %all-to-all-done.ids = s32[64,1,16]{2,1,0:T(1,128)S(1)} async-done(((s32[64,1,16]{2,1,0:T(1,128)}), s32[64,1,16]{2,1,0:T(1,128)S(1)}, u32[]{:S(2)}, u32[]{:S(2)}) %all-to-all-start) | async-done | bytes 4128 | tf_op jit(solution)/shard_map/all_to_all | solution.py:28
  24.4 2.8 %serve.1 = (f32[1600,128]{1,0:T(8,128)}, f32[32,512]{1,0:T(8,128)S(1)}) custom-call(s32[64,1,16]{2,1,0:T(1,128)S(1)} %all-to-all-done.ids, s32[1]{0:T(128)} %bitcast.2.here, f32[512,4,128]{2,1,0:T(4,128)S(1)} %spread.1.rows), custom_call_target="tpu_custom_call" | custom-call | tf_op jit(solution)/shard_map/serve/pallas_call | solution.py:119
  27.3 4.8 %all-to-all-start.1 = ((f32[64,25,1,128]{3,2,1,0:T(1,128)}), f32[64,25,1,128]{3,2,1,0:T(1,128)S(1)}, u32[]{:S(2)}, u32[]{:S(2)}) async-start(f32[64,25,1,128]{3,2,1,0:T(1,128)} %bitcast.49), calls=%async_computation.1 | async-start | bytes 1638400 | tf_op jit(solution)/shard_map/all_to_all | solution.py:28
  32.1 0.1 iota_compare_fusion
  32.2 0.1 slice.50
  32.3 0.1 copy.28
  32.3 0.2 select_reduce_fusion
  32.5 0.1 reshape.323
  32.6 0.1 reshape.322
  32.7 0.2 slice_reduce_fusion
  32.9 0.1 pad_add_fusion.1.refs_0_
  33.0 2.5 %collective-permute-start.3 = (s32[1,544]{1,0:T(1,128)S(1)}, s32[1,544]{1,0:T(1,128)S(1)}, u32[]{:S(2)}, u32[]{:S(2)}) collective-permute-start(s32[1,544]{1,0:T(1,128)S(1)} %pad_add_fusion.1.refs_0_), channel_id=1, source_target_pairs={{0,3},{1,0},{2,1},{3,2},{4,7},{5,4},{6,5},{7,6},{8,11},{9,8},{10,9... | collective-permute-start | bytes 6536 | tf_op jit(solution)/shard_map/ppermute | solution.py:24
  35.5 0.5 collective-permute-start.4
  36.0 0.6 collective-permute-start.5
  36.6 6.2 %collective-permute-start.2 = (f32[8,512]{1,0:T(8,128)S(1)}, f32[8,512]{1,0:T(8,128)S(1)}, u32[]{:S(2)}, u32[]{:S(2)}) collective-permute-start(f32[8,512]{1,0:T(8,128)S(1)} %get-tuple-element.35), channel_id=1, source_target_pairs={{0,244},{4,248},{8,252},{12,0},{16,4},{20,8},{24,12},{28,16},{32,2... | collective-permute-start | bytes 49160 | tf_op jit(solution)/shard_map/ppermute | solution.py:24
  42.8 1.2 collective-permute-start.1
  44.0 0.4 collective-permute-start
  44.4 0.1 compare_select_fusion.2.slots
  44.6 3.5 %prep.1 = (bf16[2048,640]{1,0:T(8,128)(2,1)}, bf16[544,2048]{1,0:T(8,128)(2,1)}, f32[2,8,512]{2,1,0:T(8,128)}, f32[2,512,128]{2,1,0:T(8,128)}) custom-call(s32[1,2048]{1,0:T(1,128)S(1)} %compare_select_fusion.2.slots, s32[1,2048]{1,0:T(1,128)S(1)} %reshape_squeeze.10.negs), custom_call_target="tpu_custom_call" | custom-call | tf_op jit(solution)/shard_map/prep/pallas_call | solution.py:165
  48.1 2.3 %hot.1.ahead = bf16[512,2176]{1,0:T(8,128)(2,1)} custom-call(s32[1]{0:T(128)} %bitcast.me, s32[1,544]{1,0:T(1,128)S(1)} %pad_add_fusion.1.refs_0_, s32[1,544]{1,0:T(1,128)S(1)} %collective-permute-done.3.refs_1_, s32[1,544]{1,0:T(1,128)S(1)} %collective-permute-done.4.refs_2_, s32[1,544]{1,0:T(1,128)S(1)} %collective-permute-done.5.refs_3_), custom_call_target="tpu_custom_call" | custom-call | tf_op jit(solution)/shard_map/hot/pallas_call | solution.py:326
  50.4 2.5 %collective-permute-done.2 = f32[8,512]{1,0:T(8,128)S(1)} collective-permute-done((f32[8,512]{1,0:T(8,128)S(1)}, f32[8,512]{1,0:T(8,128)S(1)}, u32[]{:S(2)}, u32[]{:S(2)}) %collective-permute-start.2) | collective-permute-done | bytes 16416 | tf_op jit(solution)/shard_map/ppermute | solution.py:24
  52.9 0.2 collective-permute-done
  53.1 2.6 %all-to-all-done.1 = f32[64,25,1,128]{3,2,1,0:T(1,128)S(1)} async-done(((f32[64,25,1,128]{3,2,1,0:T(1,128)}), f32[64,25,1,128]{3,2,1,0:T(1,128)S(1)}, u32[]{:S(2)}, u32[]{:S(2)}) %all-to-all-start.1) | async-done | bytes 819232 | tf_op jit(solution)/shard_map/all_to_all | solution.py:28
  55.7 13.5 %grads.1 = (f32[1792,128]{1,0:T(8,128)}, f32[32,512]{1,0:T(8,128)S(1)}) custom-call(f32[1600,128]{1,0:T(8,128)S(1)} %bitcast.40, f32[32,512]{1,0:T(8,128)S(1)} %pad_maximum_fusion.tails, bf16[2048,640]{1,0:T(8,128)(2,1)} %get-tuple-element.16.by_edge, bf16[544,2048]{1,0:T(8,128)(2,1)} %get-tuple-element.17.by_slot, f32[2,8,512]{2,1,0:T(8,128)S(1)} %copy-done.3, ...), custom_call_target="tpu_custom_call" | custom-call | tf_op jit(solution)/shard_map/grads/pallas_call | solution.py:285
  69.2 9.1 %all-to-all-start.2 = ((f32[256,7,1,128]{3,2,1,0:T(1,128)}), f32[256,7,1,128]{3,2,1,0:T(1,128)S(1)}, u32[]{:S(2)}, u32[]{:S(2)}) async-start(f32[256,7,1,128]{3,2,1,0:T(1,128)} %bitcast.48), calls=%async_computation.2 | async-start | bytes 1835008 | tf_op jit(solution)/shard_map/all_to_all | solution.py:28
  78.4 0.1 constant_dynamic-slice_fusion.3
  78.5 1.4 %collective-permute-start.8 = (f32[32,128]{1,0:T(8,128)S(1)}, f32[32,128]{1,0:T(8,128)S(1)}, u32[]{:S(2)}, u32[]{:S(2)}) collective-permute-start(f32[32,128]{1,0:T(8,128)S(1)} %bitcast.55), channel_id=1, source_target_pairs={{0,1},{1,2},{2,3},{3,0},{4,5},{5,6},{6,7},{7,4},{8,9},{9,10},{10,1... | collective-permute-start | bytes 49160 | tf_op jit(solution)/shard_map/ppermute | solution.py:24
  79.9 2.4 %collective-permute-start.7 = (f32[32,128]{1,0:T(8,128)S(1)}, f32[32,128]{1,0:T(8,128)S(1)}, u32[]{:S(2)}, u32[]{:S(2)}) collective-permute-start(f32[32,128]{1,0:T(8,128)S(1)} %bitcast.52), channel_id=1, source_target_pairs={{0,2},{1,3},{2,0},{3,1},{4,6},{5,7},{6,4},{7,5},{8,10},{9,11},{10,... | collective-permute-start | bytes 49160 | tf_op jit(solution)/shard_map/ppermute | solution.py:24
  82.3 1.2 collective-permute-start.6
  83.5 0.8 collective-permute-done.7
  84.3 1.1 collective-permute-done.6
  85.5 4.4 %collective-permute-start.11 = (f32[4,8,128]{2,1,0:T(8,128)S(1)}, f32[4,8,128]{2,1,0:T(8,128)S(1)}, u32[]{:S(2)}, u32[]{:S(2)}) collective-permute-start(f32[4,8,128]{2,1,0:T(8,128)S(1)} %get-tuple-element.27), channel_id=1, source_target_pairs={{0,12},{4,16},{8,20},{12,24},{16,28},{20,32},{24,36},{28,40},{32,4... | collective-permute-start | bytes 49160 | tf_op jit(solution)/shard_map/ppermute | solution.py:24
  89.9 1.2 collective-permute-start.10
  91.2 13.5 %collective-permute-done.11 = f32[4,8,128]{2,1,0:T(8,128)S(1)} collective-permute-done((f32[4,8,128]{2,1,0:T(8,128)S(1)}, f32[4,8,128]{2,1,0:T(8,128)S(1)}, u32[]{:S(2)}, u32[]{:S(2)}) %collective-permute-start.11) | collective-permute-done | bytes 16416 | tf_op jit(solution)/shard_map/ppermute | solution.py:24
  104.7 3.7 %all-to-all-done.2 = f32[256,7,1,128]{3,2,1,0:T(1,128)S(1)} async-done(((f32[256,7,1,128]{3,2,1,0:T(1,128)}), f32[256,7,1,128]{3,2,1,0:T(1,128)S(1)}, u32[]{:S(2)}, u32[]{:S(2)}) %all-to-all-start.2) | async-done | bytes 917536 | tf_op jit(solution)/shard_map/all_to_all | solution.py:28
  108.5 2.8 %owner.1 = (f32[56,512]{1,0:T(8,128)S(1)}, f32[48,512]{1,0:T(8,128)S(1)}) custom-call(f32[1792,128]{1,0:T(8,128)S(1)} %bitcast.39, f32[128,128]{1,0:T(8,128)S(1)} %bitcast.46, bf16[512,2176]{1,0:T(8,128)(2,1)} %hot.1.ahead), custom_call_target="tpu_custom_call" | custom-call | tf_op jit(solution)/shard_map/owner/pallas_call | solution.py:367
  111.3 0.9 collective-permute-start.15
  112.2 0.6 collective-permute-start.12
  112.8 0.7 collective-permute-start.14
  113.5 2.0 %collective-permute-start.17 = (f32[56,512]{1,0:T(8,128)S(1)}, f32[56,512]{1,0:T(8,128)S(1)}, u32[]{:S(2)}, u32[]{:S(2)}) collective-permute-start(f32[56,512]{1,0:T(8,128)S(1)} %get-tuple-element.22.refs_0_), channel_id=1, source_target_pairs={{0,3},{1,0},{2,1},{3,2},{4,7},{5,4},{6,5},{7,6},{8,11},{9,8},{10,9... | collective-permute-start | bytes 344072 | tf_op jit(solution)/shard_map/ppermute | solution.py:24
  115.5 2.7 %collective-permute-start.16 = (f32[48,512]{1,0:T(8,128)S(1)}, f32[48,512]{1,0:T(8,128)S(1)}, u32[]{:S(2)}, u32[]{:S(2)}) collective-permute-start(f32[48,512]{1,0:T(8,128)S(1)} %collective-permute-done.15.refs_7_), channel_id=1, source_target_pairs={{0,3},{1,0},{2,1},{3,2},{4,7},{5,4},{6,5},{7,6},{8,11},{9,8},{10,9... | collective-permute-start | bytes 294920 | tf_op jit(solution)/shard_map/ppermute | solution.py:24
  118.2 4.2 %collective-permute-done.13.refs_3_ = f32[48,512]{1,0:T(8,128)S(1)} collective-permute-done((f32[48,512]{1,0:T(8,128)S(1)}, f32[48,512]{1,0:T(8,128)S(1)}, u32[]{:S(2)}, u32[]{:S(2)}) %collective-permute-start.13) | collective-permute-done | bytes 98336 | tf_op jit(solution)/shard_map/ppermute | solution.py:24
  122.4 1.0 collective-permute-done.16.refs_5_
  123.4 1.7 %update.1 = (f32[400,512]{1,0:T(8,128)}, f32[1,512]{1,0:T(1,128)}) custom-call(s32[1]{0:T(128)} %bitcast.me, f32[56,512]{1,0:T(8,128)S(1)} %get-tuple-element.22.refs_0_, f32[48,512]{1,0:T(8,128)S(1)} %get-tuple-element.23.refs_1_, f32[56,512]{1,0:T(8,128)S(1)} %collective-permute-done.12.refs_2_, f32[48,512]{1,0:T(8,128)S(1)} %collective-permute-done.13.refs_3_, ...), custom_call_target="tpu_custom_call" | custom-call | tf_op jit(solution)/shard_map/update/pallas_call | solution.py:414
  (39 shorter events, 0.2 us)
Async XLA Ops:
  2.0 22.4 %all-to-all-start = ((s32[64,1,16]{2,1,0:T(1,128)}), s32[64,1,16]{2,1,0:T(1,128)S(1)}, u32[]{:S(2)}, u32[]{:S(2)}) async-start(s32[64,1,16]{2,1,0:T(1,128)} %bitcast.1), calls=%async_computation | async-start | bytes 65536 | tf_op jit(solution)/shard_map/all_to_all | solution.py:28
  15.2 1.1 copy-start
  16.3 15.7 %copy-start.6 = (s32[1,1,2,512]{3,2,1,0:T(2,128)S(1)}, s32[1,1,2,512]{3,2,1,0:T(2,128)}, u32[]{:S(2)}) copy-start(s32[1,1,2,512]{3,2,1,0:T(2,128)} %param.10) | copy-start | bytes 12292
  16.3 15.7 %copy-start.7 = (s32[1,1,2,512]{3,2,1,0:T(2,128)S(1)}, s32[1,1,2,512]{3,2,1,0:T(2,128)}, u32[]{:S(2)}) copy-start(s32[1,1,2,512]{3,2,1,0:T(2,128)} %param.9) | copy-start | bytes 12292
  16.3 28.2 %copy-start.5 = (s32[1,1,2,2,512]{4,3,2,1,0:T(2,128)S(1)}, s32[1,1,2,2,512]{4,3,2,1,0:T(2,128)}, u32[]{:S(2)}) copy-start(s32[1,1,2,2,512]{4,3,2,1,0:T(2,128)} %param.11) | copy-start | bytes 24580
  27.3 28.5 %all-to-all-start.1 = ((f32[64,25,1,128]{3,2,1,0:T(1,128)}), f32[64,25,1,128]{3,2,1,0:T(1,128)S(1)}, u32[]{:S(2)}, u32[]{:S(2)}) async-start(f32[64,25,1,128]{3,2,1,0:T(1,128)} %bitcast.49), calls=%async_computation.1 | async-start | bytes 1638400 | tf_op jit(solution)/shard_map/all_to_all | solution.py:28
  33.0 11.0 %collective-permute-start.3 = (s32[1,544]{1,0:T(1,128)S(1)}, s32[1,544]{1,0:T(1,128)S(1)}, u32[]{:S(2)}, u32[]{:S(2)}) collective-permute-start(s32[1,544]{1,0:T(1,128)S(1)} %pad_add_fusion.1.refs_0_), channel_id=1, source_target_pairs={{0,3},{1,0},{2,1},{3,2},{4,7},{5,4},{6,5},{7,6},{8,11},{9,8},{10,9... | collective-permute-start | bytes 6536 | tf_op jit(solution)/shard_map/ppermute | solution.py:24
  35.5 12.7 %collective-permute-start.4 = (s32[1,544]{1,0:T(1,128)S(1)}, s32[1,544]{1,0:T(1,128)S(1)}, u32[]{:S(2)}, u32[]{:S(2)}) collective-permute-start(s32[1,544]{1,0:T(1,128)S(1)} %pad_add_fusion.1.refs_0_), channel_id=1, source_target_pairs={{0,2},{1,3},{2,0},{3,1},{4,6},{5,7},{6,4},{7,5},{8,10},{9,11},{10,... | collective-permute-start | bytes 6536 | tf_op jit(solution)/shard_map/ppermute | solution.py:24
  36.0 12.1 %collective-permute-start.5 = (s32[1,544]{1,0:T(1,128)S(1)}, s32[1,544]{1,0:T(1,128)S(1)}, u32[]{:S(2)}, u32[]{:S(2)}) collective-permute-start(s32[1,544]{1,0:T(1,128)S(1)} %pad_add_fusion.1.refs_0_), channel_id=1, source_target_pairs={{0,1},{1,2},{2,3},{3,0},{4,5},{5,6},{6,7},{7,4},{8,9},{9,10},{10,1... | collective-permute-start | bytes 6536 | tf_op jit(solution)/shard_map/ppermute | solution.py:24
  36.6 16.3 %collective-permute-start.2 = (f32[8,512]{1,0:T(8,128)S(1)}, f32[8,512]{1,0:T(8,128)S(1)}, u32[]{:S(2)}, u32[]{:S(2)}) collective-permute-start(f32[8,512]{1,0:T(8,128)S(1)} %get-tuple-element.35), channel_id=1, source_target_pairs={{0,244},{4,248},{8,252},{12,0},{16,4},{20,8},{24,12},{28,16},{32,2... | collective-permute-start | bytes 49160 | tf_op jit(solution)/shard_map/ppermute | solution.py:24
  42.8 10.1 %collective-permute-start.1 = (f32[8,512]{1,0:T(8,128)S(1)}, f32[8,512]{1,0:T(8,128)S(1)}, u32[]{:S(2)}, u32[]{:S(2)}) collective-permute-start(f32[8,512]{1,0:T(8,128)S(1)} %get-tuple-element.36), channel_id=1, source_target_pairs={{0,248},{4,252},{8,0},{12,4},{16,8},{20,12},{24,16},{28,20},{32,24... | collective-permute-start | bytes 49160 | tf_op jit(solution)/shard_map/ppermute | solution.py:24
  44.0 9.1 %collective-permute-start = (f32[8,512]{1,0:T(8,128)S(1)}, f32[8,512]{1,0:T(8,128)S(1)}, u32[]{:S(2)}, u32[]{:S(2)}) collective-permute-start(f32[8,512]{1,0:T(8,128)S(1)} %get-tuple-element.37), channel_id=1, source_target_pairs={{0,252},{4,0},{8,4},{12,8},{16,12},{20,16},{24,20},{28,24},{32,28}... | collective-permute-start | bytes 49160 | tf_op jit(solution)/shard_map/ppermute | solution.py:24
  48.1 7.6 %copy-start.2 = (f32[2,512,128]{2,1,0:T(8,128)S(1)}, f32[2,512,128]{2,1,0:T(8,128)}, u32[]{:S(2)}) copy-start(f32[2,512,128]{2,1,0:T(8,128)} %get-tuple-element.19.count_col) | copy-start | bytes 1572868
  48.1 7.6 %copy-start.3 = (f32[2,8,512]{2,1,0:T(8,128)S(1)}, f32[2,8,512]{2,1,0:T(8,128)}, u32[]{:S(2)}) copy-start(f32[2,8,512]{2,1,0:T(8,128)} %get-tuple-element.18.count_row) | copy-start | bytes 98308
  69.2 39.2 %all-to-all-start.2 = ((f32[256,7,1,128]{3,2,1,0:T(1,128)}), f32[256,7,1,128]{3,2,1,0:T(1,128)S(1)}, u32[]{:S(2)}, u32[]{:S(2)}) async-start(f32[256,7,1,128]{3,2,1,0:T(1,128)} %bitcast.48), calls=%async_computation.2 | async-start | bytes 1835008 | tf_op jit(solution)/shard_map/all_to_all | solution.py:28
  78.3 45.1 %copy-start.1 = (f32[512,400]{0,1:T(8,128)S(1)}, f32[512,400]{0,1:T(8,128)}, u32[]{:S(2)}) copy-start(f32[512,400]{0,1:T(8,128)} %param.6) | copy-start | bytes 2457604
  78.3 45.1 %copy-start.4 = (f32[512]{0:T(512)S(1)}, f32[512]{0:T(512)}, u32[]{:S(2)}) copy-start(f32[512]{0:T(512)} %param.7) | copy-start | bytes 6148
  78.5 5.0 %collective-permute-start.8 = (f32[32,128]{1,0:T(8,128)S(1)}, f32[32,128]{1,0:T(8,128)S(1)}, u32[]{:S(2)}, u32[]{:S(2)}) collective-permute-start(f32[32,128]{1,0:T(8,128)S(1)} %bitcast.55), channel_id=1, source_target_pairs={{0,1},{1,2},{2,3},{3,0},{4,5},{5,6},{6,7},{7,4},{8,9},{9,10},{10,1... | collective-permute-start | bytes 49160 | tf_op jit(solution)/shard_map/ppermute | solution.py:24
  79.9 4.4 %collective-permute-start.7 = (f32[32,128]{1,0:T(8,128)S(1)}, f32[32,128]{1,0:T(8,128)S(1)}, u32[]{:S(2)}, u32[]{:S(2)}) collective-permute-start(f32[32,128]{1,0:T(8,128)S(1)} %bitcast.52), channel_id=1, source_target_pairs={{0,2},{1,3},{2,0},{3,1},{4,6},{5,7},{6,4},{7,5},{8,10},{9,11},{10,... | collective-permute-start | bytes 49160 | tf_op jit(solution)/shard_map/ppermute | solution.py:24
  82.3 3.1 %collective-permute-start.6 = (f32[32,128]{1,0:T(8,128)S(1)}, f32[32,128]{1,0:T(8,128)S(1)}, u32[]{:S(2)}, u32[]{:S(2)}) collective-permute-start(f32[32,128]{1,0:T(8,128)S(1)} %bitcast.51), channel_id=1, source_target_pairs={{0,3},{1,0},{2,1},{3,2},{4,7},{5,4},{6,5},{7,6},{8,11},{9,8},{10,9... | collective-permute-start | bytes 49160 | tf_op jit(solution)/shard_map/ppermute | solution.py:24
  85.5 19.2 %collective-permute-start.11 = (f32[4,8,128]{2,1,0:T(8,128)S(1)}, f32[4,8,128]{2,1,0:T(8,128)S(1)}, u32[]{:S(2)}, u32[]{:S(2)}) collective-permute-start(f32[4,8,128]{2,1,0:T(8,128)S(1)} %get-tuple-element.27), channel_id=1, source_target_pairs={{0,12},{4,16},{8,20},{12,24},{16,28},{20,32},{24,36},{28,40},{32,4... | collective-permute-start | bytes 49160 | tf_op jit(solution)/shard_map/ppermute | solution.py:24
  89.9 14.8 %collective-permute-start.10 = (f32[4,8,128]{2,1,0:T(8,128)S(1)}, f32[4,8,128]{2,1,0:T(8,128)S(1)}, u32[]{:S(2)}, u32[]{:S(2)}) collective-permute-start(f32[4,8,128]{2,1,0:T(8,128)S(1)} %get-tuple-element.28), channel_id=1, source_target_pairs={{0,8},{4,12},{8,16},{12,20},{16,24},{20,28},{24,32},{28,36},{32,40... | collective-permute-start | bytes 49160 | tf_op jit(solution)/shard_map/ppermute | solution.py:24
  91.2 13.5 %collective-permute-start.9 = (f32[4,8,128]{2,1,0:T(8,128)S(1)}, f32[4,8,128]{2,1,0:T(8,128)S(1)}, u32[]{:S(2)}, u32[]{:S(2)}) collective-permute-start(f32[4,8,128]{2,1,0:T(8,128)S(1)} %get-tuple-element.29), channel_id=1, source_target_pairs={{0,4},{4,8},{8,12},{12,16},{16,20},{20,24},{24,28},{28,32},{32,36}... | collective-permute-start | bytes 49160 | tf_op jit(solution)/shard_map/ppermute | solution.py:24
  111.3 4.2 %collective-permute-start.15 = (f32[48,512]{1,0:T(8,128)S(1)}, f32[48,512]{1,0:T(8,128)S(1)}, u32[]{:S(2)}, u32[]{:S(2)}) collective-permute-start(f32[48,512]{1,0:T(8,128)S(1)} %get-tuple-element.23.refs_1_), channel_id=1, source_target_pairs={{0,3},{1,0},{2,1},{3,2},{4,7},{5,4},{6,5},{7,6},{8,11},{9,8},{10,9... | collective-permute-start | bytes 294920 | tf_op jit(solution)/shard_map/ppermute | solution.py:24
  112.2 10.2 %collective-permute-start.12 = (f32[56,512]{1,0:T(8,128)S(1)}, f32[56,512]{1,0:T(8,128)S(1)}, u32[]{:S(2)}, u32[]{:S(2)}) collective-permute-start(f32[56,512]{1,0:T(8,128)S(1)} %get-tuple-element.22.refs_0_), channel_id=1, source_target_pairs={{0,1},{1,2},{2,3},{3,0},{4,5},{5,6},{6,7},{7,4},{8,9},{9,10},{10,1... | collective-permute-start | bytes 344072 | tf_op jit(solution)/shard_map/ppermute | solution.py:24
  112.8 9.6 %collective-permute-start.14 = (f32[56,512]{1,0:T(8,128)S(1)}, f32[56,512]{1,0:T(8,128)S(1)}, u32[]{:S(2)}, u32[]{:S(2)}) collective-permute-start(f32[56,512]{1,0:T(8,128)S(1)} %get-tuple-element.22.refs_0_), channel_id=1, source_target_pairs={{0,2},{1,3},{2,0},{3,1},{4,6},{5,7},{6,4},{7,5},{8,10},{9,11},{10,... | collective-permute-start | bytes 344072 | tf_op jit(solution)/shard_map/ppermute | solution.py:24
  113.5 8.9 %collective-permute-start.17 = (f32[56,512]{1,0:T(8,128)S(1)}, f32[56,512]{1,0:T(8,128)S(1)}, u32[]{:S(2)}, u32[]{:S(2)}) collective-permute-start(f32[56,512]{1,0:T(8,128)S(1)} %get-tuple-element.22.refs_0_), channel_id=1, source_target_pairs={{0,3},{1,0},{2,1},{3,2},{4,7},{5,4},{6,5},{7,6},{8,11},{9,8},{10,9... | collective-permute-start | bytes 344072 | tf_op jit(solution)/shard_map/ppermute | solution.py:24
  115.5 6.9 %collective-permute-start.13 = (f32[48,512]{1,0:T(8,128)S(1)}, f32[48,512]{1,0:T(8,128)S(1)}, u32[]{:S(2)}, u32[]{:S(2)}) collective-permute-start(f32[48,512]{1,0:T(8,128)S(1)} %get-tuple-element.23.refs_1_), channel_id=1, source_target_pairs={{0,1},{1,2},{2,3},{3,0},{4,5},{5,6},{6,7},{7,4},{8,9},{9,10},{10,1... | collective-permute-start | bytes 294920 | tf_op jit(solution)/shard_map/ppermute | solution.py:24
  115.5 7.9 %collective-permute-start.16 = (f32[48,512]{1,0:T(8,128)S(1)}, f32[48,512]{1,0:T(8,128)S(1)}, u32[]{:S(2)}, u32[]{:S(2)}) collective-permute-start(f32[48,512]{1,0:T(8,128)S(1)} %collective-permute-done.15.refs_7_), channel_id=1, source_target_pairs={{0,3},{1,0},{2,1},{3,2},{4,7},{5,4},{6,5},{7,6},{8,11},{9,8},{10,9... | collective-permute-start | bytes 294920 | tf_op jit(solution)/shard_map/ppermute | solution.py:24
